TPU v7x, 32 devices: a whole 2x2x4 slice. The times are simulated.
32 devices in a mesh: dp: 4 (over y, x), seq: 8 (over z, core).
Axes of the slice: x: 2, y: 2, z: 4, core: 2. Of those that a mesh axis runs over, the one named last changes fastest.
Arguments:
- tokens: bfloat16 [4, 2048, 2048], P('dp', 'seq'), may hold values from -6 to 6
- gain_attn: bfloat16 [2048], P(('dp', 'seq')), may hold values from 0.099609375 to 1.8984375
- w_query: bfloat16 [2048, 2048], P(('dp', 'seq')), may hold values from -0.1875 to 0.1875
- w_key: bfloat16 [2048, 512], P(('dp', 'seq')), may hold values from -0.125 to 0.125
- w_value: bfloat16 [2048, 512], P(('dp', 'seq')), may hold values from -0.125 to 0.125
- w_out: bfloat16 [2048, 2048], P(('dp', 'seq')), may hold values from -2 to 2
- gain_mlp: bfloat16 [2048], P(('dp', 'seq')), may hold values from 0.099609375 to 1.8984375
- w_gate: bfloat16 [2048, 8192], P('dp', 'seq'), may hold values from -0.125 to 0.125
- w_up: bfloat16 [2048, 8192], P('dp', 'seq'), may hold values from -0.125 to 0.125
- w_down: bfloat16 [2048, 8192], P('dp', 'seq'), may hold values from -0.0625 to 0.0625
- cotangent: bfloat16 [4, 2048, 2048], P('dp', 'seq'), may hold values from -6 to 6
Outputs:
- block_out: bfloat16 [4, 2048, 2048], P('dp', 'seq')
- grad_tokens: bfloat16 [4, 2048, 2048], P('dp', 'seq')
- grad_gain_attn: float32 [2048], P(('dp', 'seq'))
- grad_query: float32 [2048, 2048], P(('dp', 'seq'))
- grad_key: float32 [2048, 512], P(('dp', 'seq'))
- grad_value: float32 [2048, 512], P(('dp', 'seq'))
- grad_out: float32 [2048, 2048], P(('dp', 'seq'))
- grad_gain_mlp: float32 [2048], P(('dp', 'seq'))
- grad_gate: float32 [2048, 8192], P('dp', 'seq')
- grad_up: float32 [2048, 8192], P('dp', 'seq')
- grad_down: float32 [2048, 8192], P('dp', 'seq')
All inputs are finite; a program needn't handle non-finite values.
Results may differ from a plain program's by a relative error of at most 0.017.
Values may be sent and summed in bfloat16 or wider, within the bound.
No kernel may reach another device: no remote copies, remote signals or barrier semaphores. Data moves between devices by JAX's collectives and lax.ppermute only.
A program may use at most 256 MiB of HBM per device.

v0:
```python
import jax
import jax.numpy as jnp
from jax import lax
from jax.sharding import PartitionSpec as P

H = 32
KV = 8
HD = 64
BLOCK = 512


epsilon = 1e-05
rope_theta = 500000.0
rope_factor = 32.0
old_context = 8192.0


def for_sending(shard):

    def short(part):
        return part.astype(jnp.bfloat16) if part.dtype == jnp.float32 else part

    return jax.tree.map(short, shard)


def frequencies(head_size):
    halves = jnp.arange(head_size // 2).astype(jnp.float32)
    plain = rope_theta ** (-2.0 * halves / head_size)
    blend = jnp.clip((old_context * plain / (2.0 * jnp.pi) - 1.0) / 3.0, 0.0, 1.0)
    return (1.0 - blend) * plain / rope_factor + blend * plain


def rope_tables(positions, head_size):
    angles = positions.astype(jnp.float32)[:, None] * frequencies(head_size)[None, :]
    return (jnp.cos(angles), jnp.sin(angles))


def rotate(heads_in, cosine_part, sine_part):
    half_size = heads_in.shape[-1] // 2
    first_half = heads_in[..., :half_size]
    second_half = heads_in[..., half_size:]
    cosine_wide = cosine_part[:, None, :]
    sine_wide = sine_part[:, None, :]
    return jnp.concatenate(
        [
            first_half * cosine_wide - second_half * sine_wide,
            second_half * cosine_wide + first_half * sine_wide,
        ],
        axis=-1,
    )


def rotate_back(heads_in, cosine_part, sine_part):
    half_size = heads_in.shape[-1] // 2
    first_half = heads_in[..., :half_size]
    second_half = heads_in[..., half_size:]
    cosine_wide = cosine_part[:, None, :]
    sine_wide = sine_part[:, None, :]
    return jnp.concatenate(
        [
            first_half * cosine_wide + second_half * sine_wide,
            second_half * cosine_wide - first_half * sine_wide,
        ],
        axis=-1,
    )


def norm_rows(values_in, gain_row):
    inverse = lax.rsqrt(jnp.mean(values_in * values_in, axis=-1, keepdims=True) + epsilon)
    return values_in * inverse * gain_row


def rounded(values_in):
    return lax.optimization_barrier(values_in.astype(jnp.bfloat16)).astype(jnp.float32)


def head_scores(block_queries, key_rows, first_row, scale_factor):
    scores = (
        jnp.einsum("qhgd,khd->hgqk", block_queries, key_rows, preferred_element_type=jnp.float32)
        * scale_factor
    )
    query_places = first_row + jnp.arange(block_queries.shape[0])
    allowed = jnp.arange(key_rows.shape[0])[None, :] <= query_places[:, None]
    return jnp.where(allowed, scores, -jnp.inf)


def gate_grads(grad_hidden, gate, up_proj):
    sigmoid_gate = jax.nn.sigmoid(gate)
    grad_gate_act = (
        grad_hidden * up_proj * sigmoid_gate * (1.0 + gate * (1.0 - sigmoid_gate))
    ).astype(jnp.bfloat16)
    grad_up_act = (grad_hidden * gate * sigmoid_gate).astype(jnp.bfloat16)
    return (grad_gate_act, grad_up_act)


def shards(
    tokens, gain_attn, w_query, w_key, w_value, w_out, gain_mlp, w_gate, w_up, w_down, cotangent
):
    groups = lax.axis_size("seq")
    seq_count, piece_len, model_width = tokens.shape
    row_count = seq_count * piece_len
    heads_dev = H // groups
    repeat = max(1, groups // KV)
    kv_dev = max(KV, groups) // groups
    share = heads_dev // kv_dev
    scale_factor = HD ** (-0.5)
    positions = lax.axis_index("seq") * piece_len + jnp.arange(piece_len)
    cosine_part, sine_part = rope_tables(positions, HD)
    cosine_part = jnp.tile(cosine_part, (seq_count, 1))
    sine_part = jnp.tile(sine_part, (seq_count, 1))
    attn_parts = (
        lax.all_gather(gain_attn, ("dp", "seq"), axis=0, tiled=True),
        lax.all_gather(gain_mlp, ("dp", "seq"), axis=0, tiled=True),
        lax.all_gather(w_query, ("dp", "seq"), axis=0, tiled=True),
        lax.all_gather(w_key, ("dp", "seq"), axis=0, tiled=True),
        lax.all_gather(w_value, ("dp", "seq"), axis=0, tiled=True),
        lax.all_gather(w_out, ("dp", "seq"), axis=0, tiled=True),
    )
    gain_one, gain_two, query_full, key_full, value_full, out_full = attn_parts
    flat = tokens.reshape(row_count, model_width).astype(jnp.float32)
    normed = norm_rows(flat, gain_one.astype(jnp.float32)).astype(jnp.bfloat16)
    query_pre = jnp.dot(normed, query_full, preferred_element_type=jnp.float32).reshape(
        row_count, H, HD
    )
    key_pre = jnp.dot(normed, key_full, preferred_element_type=jnp.float32).reshape(
        row_count, KV, HD
    )
    value_low = jnp.dot(normed, value_full, preferred_element_type=jnp.float32).astype(jnp.bfloat16)
    value_low = value_low.reshape(row_count, KV, HD)
    query_low = rotate(query_pre, cosine_part, sine_part).astype(jnp.bfloat16)
    key_low = rotate(key_pre, cosine_part, sine_part).astype(jnp.bfloat16)

    def to_groups(heads_in):
        return jnp.repeat(heads_in, repeat, axis=1).reshape(
            seq_count, piece_len, groups, kv_dev * HD
        )

    query_send = query_low.reshape(seq_count, piece_len, groups, heads_dev * HD)
    query_heads, key_heads, value_heads = (
        lax.all_to_all(query_send, "seq", split_axis=2, concat_axis=1, tiled=True),
        lax.all_to_all(to_groups(key_low), "seq", split_axis=2, concat_axis=1, tiled=True),
        lax.all_to_all(to_groups(value_low), "seq", split_axis=2, concat_axis=1, tiled=True),
    )
    seq_len = query_heads.shape[1]
    query_heads = query_heads.reshape(seq_count, seq_len, kv_dev, share, HD)

    def forward_sequence(items):
        queries, key_rows, value_rows = items
        outputs = []
        totals = []
        for block_index in range(seq_len // BLOCK):
            first_row = block_index * BLOCK
            last_row = first_row + BLOCK
            scores = head_scores(
                queries[first_row:last_row], key_rows[:last_row], first_row, scale_factor
            )
            row_peak = jnp.max(scores, axis=-1, keepdims=True)
            exponent = jnp.exp(scores - row_peak)
            row_total = jnp.sum(exponent, axis=-1, keepdims=True)
            weights_low = (exponent / row_total).astype(jnp.bfloat16)
            block_result = jnp.einsum(
                "hgqk,khd->qhgd",
                weights_low,
                value_rows[:last_row],
                preferred_element_type=jnp.float32,
            )
            outputs.append(block_result.astype(jnp.bfloat16))
            totals.append(row_peak + jnp.log(row_total))
        return (
            jnp.concatenate(outputs, axis=0).reshape(seq_len, heads_dev * HD),
            jnp.concatenate(totals, axis=2),
        )

    head_out, log_totals = lax.map(forward_sequence, (query_heads, key_heads, value_heads))
    mixed = lax.all_to_all(
        for_sending(head_out.reshape(seq_count, seq_len, 1, heads_dev * HD)),
        "seq",
        split_axis=1,
        concat_axis=2,
        tiled=True,
    )
    mixed = mixed.reshape(row_count, H * HD)
    middle = flat + jnp.dot(mixed, out_full, preferred_element_type=jnp.float32)
    gain_two_wide = gain_two.astype(jnp.float32)
    normed_two = norm_rows(middle, gain_two_wide).astype(jnp.bfloat16)
    cot_rows = cotangent.reshape(row_count, model_width)
    gate_rows, up_rows, down_rows = (
        lax.all_gather(w_gate, "dp", axis=0, tiled=True),
        lax.all_gather(w_up, "dp", axis=0, tiled=True),
        lax.all_gather(w_down, "dp", axis=0, tiled=True),
    )
    unit_count = gate_rows.shape[1]
    normed_all, cot_all = (
        lax.all_gather(
            normed_two.reshape(seq_count, piece_len, model_width), "seq", axis=1, tiled=True
        ),
        lax.all_gather(cotangent, "seq", axis=1, tiled=True),
    )
    full_len = normed_all.shape[1]
    normed_flat = normed_all.reshape(seq_count * full_len, model_width)
    cot_flat = cot_all.reshape(seq_count * full_len, model_width)
    gate = jnp.dot(normed_flat, gate_rows, preferred_element_type=jnp.float32)
    up_proj = jnp.dot(normed_flat, up_rows, preferred_element_type=jnp.float32)
    hidden = (gate * jax.nn.sigmoid(gate) * up_proj).astype(jnp.bfloat16)
    grad_hidden = jnp.dot(cot_flat, down_rows, preferred_element_type=jnp.float32)
    grad_gate_act, grad_up_act = gate_grads(grad_hidden, gate, up_proj)
    hidden_three = hidden.reshape(seq_count, full_len, unit_count)
    gate_three = grad_gate_act.reshape(seq_count, full_len, unit_count)
    up_three = grad_up_act.reshape(seq_count, full_len, unit_count)
    out_part = jnp.einsum(
        "blf,df->lbd", hidden_three, down_rows, preferred_element_type=jnp.float32
    )
    back_part = jnp.einsum("blf,df->lbd", gate_three, gate_rows, preferred_element_type=jnp.float32)
    back_part = back_part + jnp.einsum(
        "blf,df->lbd", up_three, up_rows, preferred_element_type=jnp.float32
    )
    summed = lax.psum_scatter(
        jnp.stack([out_part, back_part], axis=2).astype(jnp.bfloat16),
        "seq",
        scatter_dimension=0,
        tiled=True,
    ).astype(jnp.float32)
    down_sum = jnp.transpose(summed[:, :, 0], (1, 0, 2)).reshape(row_count, model_width)
    grad_normed_two = jnp.transpose(summed[:, :, 1], (1, 0, 2)).reshape(row_count, model_width)
    grad_stack = jnp.stack(
        [
            jnp.einsum("nf,nd->fd", grad_gate_act, normed_flat, preferred_element_type=jnp.float32),
            jnp.einsum("nf,nd->fd", grad_up_act, normed_flat, preferred_element_type=jnp.float32),
            jnp.einsum("nf,nd->fd", hidden, cot_flat, preferred_element_type=jnp.float32),
        ],
        axis=1,
    )
    grad_own = lax.psum_scatter(
        grad_stack.astype(jnp.bfloat16), "dp", scatter_dimension=2, tiled=True
    ).astype(jnp.float32)
    result = middle + down_sum
    block_out = result.astype(jnp.bfloat16).reshape(seq_count, piece_len, model_width)
    _, norm_pull = jax.vjp(norm_rows, middle, gain_two_wide)
    grad_middle, grad_gain_two = norm_pull(grad_normed_two)
    grad_middle = grad_middle + cot_rows.astype(jnp.float32)
    gain_first, query_back, key_back, value_back, out_back = (
        lax.all_gather(gain_attn, ("dp", "seq"), axis=0, tiled=True),
        lax.all_gather(w_query, ("dp", "seq"), axis=0, tiled=True),
        lax.all_gather(w_key, ("dp", "seq"), axis=0, tiled=True),
        lax.all_gather(w_value, ("dp", "seq"), axis=0, tiled=True),
        lax.all_gather(w_out, ("dp", "seq"), axis=0, tiled=True),
    )
    grad_branch = grad_middle.astype(jnp.bfloat16)
    grad_out = jnp.einsum("nh,nd->hd", mixed, grad_branch, preferred_element_type=jnp.float32)
    grad_mixed = jnp.einsum("nd,hd->nh", grad_branch, out_back, preferred_element_type=jnp.float32)
    grad_mixed = grad_mixed.astype(jnp.bfloat16).reshape(
        seq_count, piece_len, groups, heads_dev * HD
    )
    grad_head_out = lax.all_to_all(grad_mixed, "seq", split_axis=2, concat_axis=1, tiled=True)
    grad_head_out = grad_head_out.reshape(seq_count, seq_len, kv_dev, share, HD)

    def backward_sequence(items):
        queries, key_rows, value_rows, grad_rows_all, log_total = items
        query_grads = []
        key_grad = jnp.zeros((seq_len, kv_dev, HD), jnp.float32)
        value_grad = jnp.zeros((seq_len, kv_dev, HD), jnp.float32)
        for block_index in range(seq_len // BLOCK):
            first_row = block_index * BLOCK
            last_row = first_row + BLOCK
            block_queries = queries[first_row:last_row]
            scores = head_scores(block_queries, key_rows[:last_row], first_row, scale_factor)
            probabilities = jnp.exp(scores - log_total[:, :, first_row:last_row])
            grad_rows = grad_rows_all[first_row:last_row]
            grad_probs = jnp.einsum(
                "qhgd,khd->hgqk",
                grad_rows,
                value_rows[:last_row],
                preferred_element_type=jnp.float32,
            )
            inner = jnp.sum(probabilities * grad_probs, axis=-1, keepdims=True)
            grad_scores = (probabilities * (grad_probs - inner)).astype(jnp.bfloat16)
            query_grads.append(
                jnp.einsum(
                    "hgqk,khd->qhgd",
                    grad_scores,
                    key_rows[:last_row],
                    preferred_element_type=jnp.float32,
                )
                * scale_factor
            )
            key_part = (
                jnp.einsum(
                    "hgqk,qhgd->khd", grad_scores, block_queries, preferred_element_type=jnp.float32
                )
                * scale_factor
            )
            value_part = jnp.einsum(
                "hgqk,qhgd->khd",
                probabilities.astype(jnp.bfloat16),
                grad_rows,
                preferred_element_type=jnp.float32,
            )
            key_grad = key_grad.at[:last_row].add(key_part)
            value_grad = value_grad.at[:last_row].add(value_part)
        query_grad = jnp.concatenate(query_grads, axis=0).reshape(seq_len, 1, heads_dev * HD)
        return (query_grad, key_grad, value_grad)

    query_grad, key_grad, value_grad = lax.map(
        backward_sequence, (query_heads, key_heads, value_heads, grad_head_out, log_totals)
    )
    query_tok, key_tok, value_tok = (
        lax.all_to_all(
            for_sending(query_grad), "seq", split_axis=1, concat_axis=2, tiled=True
        ).astype(query_grad.dtype),
        lax.all_to_all(
            key_grad.astype(jnp.bfloat16), "seq", split_axis=1, concat_axis=2, tiled=True
        ).astype(key_grad.dtype),
        lax.all_to_all(
            value_grad.astype(jnp.bfloat16), "seq", split_axis=1, concat_axis=2, tiled=True
        ).astype(value_grad.dtype),
    )

    def fold_heads(grad_in):
        return jnp.sum(grad_in.reshape(row_count, KV, repeat, HD), axis=2)

    grad_query_rot = rounded(query_tok.reshape(row_count, H, HD))
    grad_key_rot = rounded(fold_heads(key_tok))
    grad_query_pre = (
        rotate_back(grad_query_rot, cosine_part, sine_part)
        .astype(jnp.bfloat16)
        .reshape(row_count, H * HD)
    )
    grad_key_pre = (
        rotate_back(grad_key_rot, cosine_part, sine_part)
        .astype(jnp.bfloat16)
        .reshape(row_count, KV * HD)
    )
    grad_value_pre = fold_heads(value_tok).astype(jnp.bfloat16).reshape(row_count, KV * HD)
    grad_query = jnp.einsum("nd,nh->dh", normed, grad_query_pre, preferred_element_type=jnp.float32)
    grad_key = jnp.einsum("nd,nh->dh", normed, grad_key_pre, preferred_element_type=jnp.float32)
    grad_value = jnp.einsum("nd,nh->dh", normed, grad_value_pre, preferred_element_type=jnp.float32)
    grad_normed = jnp.einsum(
        "nh,dh->nd", grad_query_pre, query_back, preferred_element_type=jnp.float32
    )
    grad_normed = grad_normed + jnp.einsum(
        "nh,dh->nd", grad_key_pre, key_back, preferred_element_type=jnp.float32
    )
    grad_normed = grad_normed + jnp.einsum(
        "nh,dh->nd", grad_value_pre, value_back, preferred_element_type=jnp.float32
    )
    _, first_pull = jax.vjp(norm_rows, flat, gain_first.astype(jnp.float32))
    grad_flat, grad_gain_one = first_pull(grad_normed)
    grad_tokens = (
        (grad_middle + grad_flat).astype(jnp.bfloat16).reshape(seq_count, piece_len, model_width)
    )
    attn_sums = (
        lax.psum_scatter(grad_gain_one, ("dp", "seq"), scatter_dimension=0, tiled=True),
        lax.psum_scatter(grad_gain_two, ("dp", "seq"), scatter_dimension=0, tiled=True),
        lax.psum_scatter(grad_query, ("dp", "seq"), scatter_dimension=0, tiled=True),
        lax.psum_scatter(grad_key, ("dp", "seq"), scatter_dimension=0, tiled=True),
        lax.psum_scatter(grad_value, ("dp", "seq"), scatter_dimension=0, tiled=True),
        lax.psum_scatter(grad_out, ("dp", "seq"), scatter_dimension=0, tiled=True),
    )
    grad_gate_own = jnp.transpose(grad_own[:, 0, :])
    grad_up_own = jnp.transpose(grad_own[:, 1, :])
    grad_down_own = jnp.transpose(grad_own[:, 2, :])
    return (
        block_out,
        grad_tokens,
        attn_sums[0],
        attn_sums[2],
        attn_sums[3],
        attn_sums[4],
        attn_sums[5],
        attn_sums[1],
        grad_gate_own,
        grad_up_own,
        grad_down_own,
    )


def solution(mesh):
    in_specs = (
        P("dp", "seq", None),
        P(("dp", "seq")),
        P(("dp", "seq"), None),
        P(("dp", "seq"), None),
        P(("dp", "seq"), None),
        P(("dp", "seq"), None),
        P(("dp", "seq")),
        P("dp", "seq"),
        P("dp", "seq"),
        P("dp", "seq"),
        P("dp", "seq", None),
    )
    out_specs = (
        P("dp", "seq", None),
        P("dp", "seq", None),
        P(("dp", "seq")),
        P(("dp", "seq"), None),
        P(("dp", "seq"), None),
        P(("dp", "seq"), None),
        P(("dp", "seq"), None),
        P(("dp", "seq")),
        P("dp", "seq"),
        P("dp", "seq"),
        P("dp", "seq"),
    )
    return jax.shard_map(shards, mesh=mesh, in_specs=in_specs, out_specs=out_specs, check_vma=False)
```

profile of v0, /device:TPU:0, one launch (start us, length us, event | category | flops | bytes accessed | tf_op | source)
XLA Modules:
  0.0 1668.1 jit_solution(4856291589369216014)
XLA Ops:
  12.9 42.2 %all-reduce.7 = (bf16[2048]{0:T(1024)(128)(2,1)S(1)}, bf16[2048]{0:T(1024)(128)(2,1)S(1)}) all-reduce(bf16[2048]{0:T(1024)(128)(2,1)S(1)} %dynamic-update-slice.28, bf16[2048]{0:T(1024)(128)(2,1)S(1)} %dynamic-update-slice.29), channel_id=1, replica_groups=mesh['dp'=4,'seq'=8] {'dp','seq'}, use_global_device_ids=true, to_apply=%add.2 | all-reduce | flops 4096 | bytes 16384
  57.4 12.8 all-gather.11.cloned.1.call-done
  77.2 51.9 %all-gather.13.cloned.1.call-done = bf16[2048,512]{1,0:T(8,128)(2,1)} async-done(((bf16[64,512]{1,0:T(8,128)(2,1)}), bf16[2048,512]{1,0:T(8,128)(2,1)}) %all-gather.13.cloned.1.call-update) | async-done | bytes 2097168 | tf_op jit(solution)/shard_map/all_gather | solution.py:115
  136.2 71.8 %all-gather.15.cloned.1.call-done = bf16[2048,2048]{1,0:T(8,128)(2,1)} async-done(((bf16[64,2048]{1,0:T(8,128)(2,1)}), bf16[2048,2048]{1,0:T(8,128)(2,1)}) %all-gather.15.cloned.1.call-update) | async-done | bytes 8388624 | tf_op jit(solution)/shard_map/all_gather | solution.py:114
  208.1 12.3 copy.197
  255.7 21.9 %all-to-all-done.2 = bf16[1,256,8,256]{1,3,0,2:T(8,128)(2,1)S(1)} async-done(((bf16[1,256,8,256]{1,3,0,2:T(8,128)(2,1)}), bf16[1,256,8,256]{1,3,0,2:T(8,128)(2,1)S(1)}, u32[]{:S(2)}, u32[]{:S(2)}) %all-to-all-start.2) | async-done | bytes 1048608 | tf_op jit(solution)/shard_map/all_to_all | solution.py:140
  329.0 11.8 reduce.34
  345.5 39.1 %all-to-all-done.3 = bf16[8,2,32768]{2,1,0:T(2,128)(2,1)S(1)} async-done(((bf16[8,2,32768]{2,1,0:T(2,128)(2,1)}), bf16[8,2,32768]{2,1,0:T(2,128)(2,1)S(1)}, u32[]{:S(2)}, u32[]{:S(2)}) %all-to-all-start.3) | async-done | bytes 1048608 | tf_op jit(solution)/shard_map/all_to_all | solution.py:175
  402.1 39.4 %all-gather.25.cloned.1.call-done = bf16[1,2048,2048]{2,1,0:T(8,128)(2,1)} async-done(((bf16[1,256,2048]{2,1,0:T(8,128)(2,1)}), bf16[1,2048,2048]{2,1,0:T(8,128)(2,1)}) %all-gather.25.cloned.1.call-update) | async-done | bytes 8388624 | tf_op jit(solution)/shard_map/all_gather | solution.py:197
  441.5 14.4 fusion.20
  455.9 38.9 %all-gather.19.cloned.1.call-done = bf16[2048,1024]{1,0:T(8,128)(2,1)} async-done(((bf16[512,1024]{1,0:T(8,128)(2,1)}), bf16[2048,1024]{1,0:T(8,128)(2,1)}) %all-gather.19.cloned.1.call-update) | async-done | bytes 4194320 | tf_op jit(solution)/shard_map/all_gather | solution.py:188
  494.7 84.2 %all-gather.27.cloned.1.call-done = bf16[2048,2048]{1,0:T(8,128)(2,1)} async-done(((bf16[256,2048]{1,0:T(8,128)(2,1)}), bf16[2048,2048]{1,0:T(8,128)(2,1)}) %all-gather.27.cloned.1.call-update) | async-done | bytes 8388624 | tf_op jit(solution)/shard_map/all_gather | solution.py:194
  579.0 14.5 fusion.187
  593.5 38.5 %all-gather.21.cloned.1.call-done = bf16[2048,1024]{1,0:T(8,128)(2,1)} async-done(((bf16[512,1024]{1,0:T(8,128)(2,1)}), bf16[2048,1024]{1,0:T(8,128)(2,1)}) %all-gather.21.cloned.1.call-update) | async-done | bytes 4194320 | tf_op jit(solution)/shard_map/all_gather | solution.py:189
  631.9 21.7 %multiply_convert_fusion.2 = (bf16[2048,1024]{1,0:T(8,128)(2,1)}, bf16[2048,1024]{1,0:T(8,128)(2,1)}, bf16[2048,1024]{1,0:T(8,128)(2,1)}) fusion(f32[2048,1024]{1,0:T(8,128)} %fusion.187, f32[2048,1024]{1,0:T(8,128)} %fusion.20, bf16[2048,2048]{1,0:T(8,128)(2,1)} %all-gather.27.cloned.1.call-done, bf16[2048,1024]{1,0:T(8,128)(2,1)} %all-gather.21.cloned.1.call-done), kind=kOutput, calls=%fused_computation.46 | convolution fusion | flops 8623489024 | bytes 41943040 | tf_op jit(solution)/shard_map/dot_general | solution.py:203
  653.6 12.4 convert_bitcast_fusion
  666.0 11.8 fusion.188
  677.8 16.4 fusion.13
  704.8 13.3 convert_bitcast_fusion.1
  718.2 11.9 convert_bitcast_fusion.3
  745.4 127.6 %reduce-scatter.7.cloned.1.call-done = bf16[256,1,2,2048]{3,0,2,1:T(8,128)(2,1)} async-done(((bf16[2048,1,2,2048]{3,0,2,1:T(8,128)(2,1)}), bf16[256,1,2,2048]{3,0,2,1:T(8,128)(2,1)}) %reduce-scatter.7.cloned.1.call-update) | async-done | bytes 2097168 | tf_op jit(solution)/shard_map/reduce_scatter | solution.py:217
  886.4 26.3 %all-to-all-done.4 = bf16[1,256,8,256]{3,1,0,2:T(8,128)(2,1)S(1)} async-done(((bf16[1,256,8,256]{3,1,0,2:T(8,128)(2,1)}), bf16[1,256,8,256]{3,1,0,2:T(8,128)(2,1)S(1)}, u32[]{:S(2)}, u32[]{:S(2)}) %all-to-all-start.4) | async-done | bytes 1048608 | tf_op jit(solution)/shard_map/all_to_all | solution.py:254
  939.4 11.9 reduce.37
  1005.1 10.6 fusion.30
  1045.4 11.8 reduce.36
  1057.5 15.8 all_to_all.129
  1109.9 12.6 reduce.35
  1124.6 32.4 %all_to_all.130 = bf16[8,2,32768]{2,1,0:T(2,128)(2,1)} all-to-all(bf16[8,2,32768]{2,1,0:T(2,128)(2,1)} %reshape.1150), channel_id=1, replica_groups=mesh['dp'=4,'seq'=8] {'seq'}, dimensions={0} | all-to-all | bytes 2097152 | tf_op jit(solution)/shard_map/all_to_all | solution.py:307
  1203.8 41.5 %all-reduce.6 = (f32[2048]{0:T(1024)S(1)}, f32[2048]{0:T(1024)S(1)}) all-reduce(f32[2048]{0:T(1024)S(1)} %get-tuple-element.265, f32[2048]{0:T(1024)S(1)} %copy-done.78), channel_id=4, replica_groups=mesh['dp'=4,'seq'=8] {'dp','seq'}, use_global_device_ids=true, to_apply=%region_18.19.clone | all-reduce | flops 4096 | bytes 32768
  1249.7 38.4 %reduce-scatter.11.cloned.1.call-done = f32[64,512]{1,0:T(8,128)} async-done(((f32[2048,512]{1,0:T(8,128)}), f32[64,512]{1,0:T(8,128)}) %reduce-scatter.11.cloned.1.call-update) | async-done | bytes 131088 | tf_op jit(solution)/shard_map/reduce_scatter | solution.py:355
  1288.1 186.0 %reduce-scatter.15.cloned.1.call-done = f32[64,2048]{1,0:T(8,128)} async-done(((f32[2048,2048]{1,0:T(8,128)}), f32[64,2048]{1,0:T(8,128)}) %reduce-scatter.15.cloned.1.call-update) | async-done | bytes 524304 | tf_op jit(solution)/shard_map/reduce_scatter | solution.py:357
  1474.1 187.1 %reduce-scatter.9.cloned.1.call-done = f32[64,2048]{1,0:T(8,128)} async-done(((f32[2048,2048]{1,0:T(8,128)}), f32[64,2048]{1,0:T(8,128)}) %reduce-scatter.9.cloned.1.call-update) | async-done | bytes 524304 | tf_op jit(solution)/shard_map/reduce_scatter | solution.py:354
  (407 shorter events, 368.9 us)
Async XLA Ops:
  7.2 63.0 %all-gather.11.cloned.1.call-start = ((), (), s32[]{:S(2)}) async-start(), calls=%async_computation.14 | async-start | bytes 2162688 | tf_op jit(solution)/shard_map/all_gather | solution.py:116
  7.9 121.2 %all-gather.13.cloned.1.call-start = ((), (), s32[]{:S(2)}) async-start(), calls=%async_computation.15 | async-start | bytes 2162688 | tf_op jit(solution)/shard_map/all_gather | solution.py:115
  8.7 199.4 %all-gather.15.cloned.1.call-start = ((), (), s32[]{:S(2)}) async-start(), calls=%async_computation.16 | async-start | bytes 8650752 | tf_op jit(solution)/shard_map/all_gather | solution.py:114
  9.4 383.0 %all-gather.17.cloned.1.call-start = ((), (), s32[]{:S(2)}) async-start(), calls=%async_computation.17 | async-start | bytes 8650752 | tf_op jit(solution)/shard_map/all_gather | solution.py:117
  10.0 392.1 %all-gather.23.cloned.1.call-start = ((), (), s32[]{:S(2)}) async-start(), calls=%async_computation.20 | async-start | bytes 5242880 | tf_op jit(solution)/shard_map/all_gather | solution.py:190
  10.6 430.9 %all-gather.25.cloned.1.call-start = ((), (), s32[]{:S(2)}) async-start(), calls=%async_computation.21 | async-start | bytes 9437184 | tf_op jit(solution)/shard_map/all_gather | solution.py:197
  55.0 168.8 %copy-start.37 = (f32[2048]{0:T(1024)}, f32[2048]{0:T(1024)S(1)}, u32[]{:S(2)}) copy-start(f32[2048]{0:T(1024)S(1)} %convert_element_type.299) | copy-start | bytes 24580
  57.1 166.7 %copy-start.61 = (f32[256]{0:T(256)}, f32[256]{0:T(256)S(1)}, u32[]{:S(2)}) copy-start(f32[256]{0:T(256)S(1)} %fusion.174) | copy-start | bytes 3076
  57.3 172.4 %copy-start.39 = (f32[256,32]{0,1:T(8,128)}, f32[256,32]{0,1:T(8,128)S(1)}, u32[]{:S(2)}) copy-start(f32[256,32]{0,1:T(8,128)S(1)} %get-tuple-element.295) | copy-start | bytes 98308
  57.4 172.4 %copy-start.42 = (f32[256,32]{0,1:T(8,128)}, f32[256,32]{0,1:T(8,128)S(1)}, u32[]{:S(2)}) copy-start(f32[256,32]{0,1:T(8,128)S(1)} %get-tuple-element.296) | copy-start | bytes 98308
  57.4 75.6 %copy-start.4 = (bf16[1,256,2048]{2,1,0:T(8,128)(2,1)S(1)}, bf16[1,256,2048]{2,1,0:T(8,128)(2,1)}, u32[]{:S(2)}) copy-start(bf16[1,256,2048]{2,1,0:T(8,128)(2,1)} %param.31) | copy-start | bytes 3145732
  73.7 146.7 %all-to-all-start = ((bf16[1,256,8,64]{1,3,0,2:T(8,128)(2,1)}), bf16[1,256,8,64]{1,3,0,2:T(8,128)(2,1)S(1)}, u32[]{:S(2)}, u32[]{:S(2)}) async-start(bf16[1,256,8,64]{1,3,0,2:T(8,128)(2,1)} %bitcast.2), calls=%async_computation | async-start | bytes 524288 | tf_op jit(solution)/shard_map/all_to_all | solution.py:142
  220.4 15.0 all-to-all-start.1
  235.4 42.2 %all-to-all-start.2 = ((bf16[1,256,8,256]{1,3,0,2:T(8,128)(2,1)}), bf16[1,256,8,256]{1,3,0,2:T(8,128)(2,1)S(1)}, u32[]{:S(2)}, u32[]{:S(2)}) async-start(bf16[1,256,8,256]{1,3,0,2:T(8,128)(2,1)} %bitcast.585), calls=%async_computation.2 | async-start | bytes 2097152 | tf_op jit(solution)/shard_map/all_to_all | solution.py:140
  238.9 255.8 %all-gather.19.cloned.1.call-start = ((), (), s32[]{:S(2)}) async-start(), calls=%async_computation.18 | async-start | bytes 5242880 | tf_op jit(solution)/shard_map/all_gather | solution.py:188
  341.9 42.7 %all-to-all-start.3 = ((bf16[8,2,32768]{2,1,0:T(2,128)(2,1)}), bf16[8,2,32768]{2,1,0:T(2,128)(2,1)S(1)}, u32[]{:S(2)}, u32[]{:S(2)}) async-start(bf16[8,2,32768]{2,1,0:T(2,128)(2,1)} %reshape.1148), calls=%async_computation.3 | async-start | bytes 2097152 | tf_op jit(solution)/shard_map/all_to_all | solution.py:175
  345.5 233.5 %all-gather.27.cloned.1.call-start = ((), (), s32[]{:S(2)}) async-start(), calls=%async_computation.28 | async-start | bytes 9437184 | tf_op jit(solution)/shard_map/all_gather | solution.py:194
  401.3 230.7 %all-gather.21.cloned.1.call-start = ((), (), s32[]{:S(2)}) async-start(), calls=%async_computation.19 | async-start | bytes 5242880 | tf_op jit(solution)/shard_map/all_gather | solution.py:189
  402.0 471.1 %reduce-scatter.7.cloned.1.call-start = ((), (), s32[]{:S(2)}) async-start(), calls=%async_computation.22 | async-start | bytes 18874368 | tf_op jit(solution)/shard_map/reduce_scatter | solution.py:217
  704.7 474.3 %reduce-scatter.17.cloned.1.call-start = ((), (), s32[]{:S(2)}) async-start(), calls=%async_computation.27 | async-start | bytes 15728640 | tf_op jit(solution)/shard_map/reduce_scatter | solution.py:233
  745.4 130.0 %copy-start.9 = (f32[256,2048]{1,0:T(8,128)S(1)}, f32[256,2048]{1,0:T(8,128)}, u32[]{:S(2)}) copy-start(f32[256,2048]{1,0:T(8,128)} %copy-done.8) | copy-start | bytes 6291460
  745.4 130.0 %copy-start.60 = (f32[2048]{0:T(1024)S(1)}, f32[2048]{0:T(1024)}, u32[]{:S(2)}) copy-start(f32[2048]{0:T(1024)} %copy-done.59) | copy-start | bytes 24580
  745.4 130.0 %copy-start.82 = (f32[256]{0:T(256)S(1)}, f32[256]{0:T(256)}, u32[]{:S(2)}) copy-start(f32[256]{0:T(256)} %copy-done.81) | copy-start | bytes 3076
  745.4 131.3 %copy-start.86 = (f32[256]{0:T(256)S(1)}, f32[256]{0:T(256)}, u32[]{:S(2)}) copy-start(f32[256]{0:T(256)} %copy-done.85) | copy-start | bytes 3076
  745.4 131.3 %copy-start.15 = (bf16[1,256,2048]{2,1,0:T(8,128)(2,1)S(1)}, bf16[1,256,2048]{2,1,0:T(8,128)(2,1)}, u32[]{:S(2)}) copy-start(bf16[1,256,2048]{2,1,0:T(8,128)(2,1)} %param.41) | copy-start | bytes 3145732
  882.5 30.3 %all-to-all-start.4 = ((bf16[1,256,8,256]{3,1,0,2:T(8,128)(2,1)}), bf16[1,256,8,256]{3,1,0,2:T(8,128)(2,1)S(1)}, u32[]{:S(2)}, u32[]{:S(2)}) async-start(bf16[1,256,8,256]{3,1,0,2:T(8,128)(2,1)} %copy.215), calls=%async_computation.5 | async-start | bytes 2097152 | tf_op jit(solution)/shard_map/all_to_all | solution.py:254
  886.4 74.3 %copy-start.56 = (f32[4,512]{1,0:T(4,128)}, f32[4,512]{1,0:T(4,128)S(1)}, u32[]{:S(2)}) copy-start(f32[4,512]{1,0:T(4,128)S(1)} %log_add_fusion.2) | copy-start | bytes 24580
  952.4 18.4 %all-to-all-start.7 = ((bf16[8,2,8192]{2,1,0:T(2,128)(2,1)}), bf16[8,2,8192]{2,1,0:T(2,128)(2,1)}, u32[]{:S(2)}, u32[]{:S(2)}) async-start(bf16[8,2,8192]{2,1,0:T(2,128)(2,1)} %reshape.1154), calls=%async_computation.8 | async-start | bytes 524288 | tf_op jit(solution)/shard_map/all_to_all | solution.py:313
  956.5 293.2 %reduce-scatter.13.cloned.1.call-start = ((), (), s32[]{:S(2)}) async-start(), calls=%async_computation.25 | async-start | bytes 4325376 | tf_op jit(solution)/shard_map/reduce_scatter | solution.py:356
  982.6 305.5 %reduce-scatter.11.cloned.1.call-start = ((), (), s32[]{:S(2)}) async-start(), calls=%async_computation.24 | async-start | bytes 4325376 | tf_op jit(solution)/shard_map/reduce_scatter | solution.py:355
  1077.3 396.8 %reduce-scatter.15.cloned.1.call-start = ((), (), s32[]{:S(2)}) async-start(), calls=%async_computation.26 | async-start | bytes 17301504 | tf_op jit(solution)/shard_map/reduce_scatter | solution.py:357
  1088.3 572.9 %reduce-scatter.9.cloned.1.call-start = ((), (), s32[]{:S(2)}) async-start(), calls=%async_computation.23 | async-start | bytes 17301504 | tf_op jit(solution)/shard_map/reduce_scatter | solution.py:354
  (88 other events, 991.1 us)
Sparse Core Ops, SparseCore 0:
  11.0 59.1 all-gather.10
  73.2 55.8 all-gather.12
  132.1 75.9 all-gather.14
  210.9 90.5 all-gather.16
  303.2 51.1 all-gather.22
  355.9 85.5 all-gather.24
  443.3 51.3 all-gather.18
  496.9 82.0 all-gather.26
  580.8 51.0 all-gather.20
  704.9 168.1 reduce-scatter.6
  876.2 119.0 reduce-scatter.16
  998.0 145.6 reduce-scatter.12
  1146.6 141.4 reduce-scatter.10
  1290.8 183.1 reduce-scatter.14
  1476.8 184.3 reduce-scatter.8
where the time goes:
time: 1680 us; the launch traced here: 1670 us
  waiting for transfers between devices  973 us (58%)
  matrix products  286 us (17%)
  blocking collectives  132 us (8%)
  other arithmetic  131 us (8%)
  local copies, waits for them, and re-layouts  107 us (6%)
  starting transfers between devices  22.6 us (1%)
    reduce_scatter x1, waiting for transfers between devices, shards(): lax.psum_scatter(grad_query, ('dp', 'seq'), scatter_dimension=0, tiled=True)  187 us
    reduce_scatter x1, waiting for transfers between devices, shards(): lax.psum_scatter(grad_out, ('dp', 'seq'), scatter_dimension=0, tiled=True)  186 us
    reduce_scatter x1, waiting for transfers between devices, shards(): lax.psum_scatter(jnp.stack([out_part, back_part], axis=2).astype(jnp.bflo...  128 us
    all_gather x1, waiting for transfers between devices, shards(): lax.all_gather(normed_two.reshape(seq_count, piece_len, model_width), 'se...  84.2 us
    unnamed x2, blocking collectives  83.7 us
    all_gather x1, waiting for transfers between devices, shards(): lax.all_gather(w_query, ('dp', 'seq'), axis=0, tiled=True)  71.8 us
    unnamed x221, local copies, waits for them, and re-layouts  53.3 us
    all_gather x1, waiting for transfers between devices, shards(): lax.all_gather(w_key, ('dp', 'seq'), axis=0, tiled=True)  51.9 us
  transfers between devices with their start and end apart: 21, of which 15 were waited for; matrix products, arithmetic and copies ran while one was open for 26% of the time, Pallas kernels for 0%

commit v1 on v0

v1 whole, which is shorter than its diff:
```python
import functools

import jax
import jax.numpy as jnp
import numpy as np
from jax import lax
from jax.experimental import pallas as pl
from jax.experimental.pallas import tpu as pltpu
from jax.sharding import PartitionSpec as P

H = 32
KV = 8
HD = 64
LANES = 128
VMEM_BYTES = 50 * 2**20

epsilon = 1e-05
rope_theta = 500000.0
rope_factor = 32.0
old_context = 8192.0

f32 = jnp.float32
bf16 = jnp.bfloat16

NN = (((1,), (0,)), ((), ()))
NT = (((1,), (1,)), ((), ()))
TN = (((0,), (0,)), ((), ()))


def mm(a, b, dims):
    return lax.dot_general(a, b, dims, preferred_element_type=f32)


def cost(flops, moved, transcendentals=0):
    return pl.CostEstimate(flops=flops, bytes_accessed=moved, transcendentals=transcendentals)


def params():
    return pltpu.CompilerParams(vmem_limit_bytes=VMEM_BYTES)


def frequencies(head_size):
    halves = jnp.arange(head_size // 2).astype(f32)
    plain = rope_theta ** (-2.0 * halves / head_size)
    blend = jnp.clip((old_context * plain / (2.0 * jnp.pi) - 1.0) / 3.0, 0.0, 1.0)
    return (1.0 - blend) * plain / rope_factor + blend * plain


def rope_tables(length):
    freq = jnp.tile(frequencies(HD), LANES // (HD // 2))
    angles = jnp.arange(length).astype(f32)[:, None] * freq[None, :]
    sign = jnp.where((jnp.arange(LANES) % HD) < HD // 2, -1.0, 1.0).astype(f32)
    return jnp.cos(angles), jnp.sin(angles) * sign[None, :]


def turn(x, cos, sin):
    lane = lax.broadcasted_iota(jnp.int32, x.shape, 1)
    swapped = jnp.where(
        lane % HD < HD // 2, pltpu.roll(x, LANES - HD // 2, 1), pltpu.roll(x, HD // 2, 1)
    )
    return x * cos + swapped * sin


def qkv_kernel(width, mine, other, gain, w, cos, sin, normed, qkv):
    x = jnp.concatenate([mine[...], other[...]], axis=0).astype(f32)
    inverse = lax.rsqrt(jnp.mean(x * x, axis=-1, keepdims=True) + epsilon)
    low = (x * inverse * gain[...]).astype(bf16)
    normed[...] = low
    y = mm(low, w[...], NN)
    lane = lax.broadcasted_iota(jnp.int32, (x.shape[0], LANES), 1)
    for at in range(0, width + 2 * HD, LANES):
        part = y[:, at : at + LANES]
        turned = turn(part, cos[...], sin[...])
        if at >= width:
            turned = jnp.where(lane < HD, turned, part)
        qkv[:, at : at + LANES] = turned.astype(bf16)


def qkv_call(mine, other, gain, w, cos, sin, width):
    rows, depth = mine.shape
    cols = width + 2 * HD
    return pl.pallas_call(
        functools.partial(qkv_kernel, width),
        out_shape=[
            jax.ShapeDtypeStruct((2 * rows, depth), bf16),
            jax.ShapeDtypeStruct((2 * rows, cols), bf16),
        ],
        compiler_params=params(),
        cost_estimate=cost(4 * rows * depth * cols, 8 * rows * depth + 2 * depth * cols),
        name="qkv",
    )(mine, other, gain, w, cos, sin)


def fwd_kernel(bq, share, q_ref, kv_ref, out_ref, ot_ref, lse_ref, m_s, l_s, acc_s):
    i = pl.program_id(0)
    m_s[...] = jnp.full(m_s.shape, -1e30, f32)
    l_s[...] = jnp.zeros(l_s.shape, f32)
    acc_s[...] = jnp.zeros(acc_s.shape, f32)
    qs = q_ref[...] * jnp.asarray(HD**-0.5, bf16)

    def step(j, masked):
        start = pl.multiple_of(j * bq, bq)
        kk = kv_ref[pl.ds(start, bq), :HD]
        vv = kv_ref[pl.ds(start, bq), HD:]
        for h in range(share):
            at = slice(h * HD, (h + 1) * HD)
            s = mm(kk, qs[:, at], NT)
            if masked:
                ki = lax.broadcasted_iota(jnp.int32, s.shape, 0)
                qi = lax.broadcasted_iota(jnp.int32, s.shape, 1)
                s = jnp.where(ki <= qi, s, -1e30)
            m_old = m_s[h : h + 1, :]
            m_new = jnp.maximum(m_old, jnp.max(s, axis=0, keepdims=True))
            p = jnp.exp(s - m_new)
            alpha = jnp.exp(m_old - m_new)
            l_s[h : h + 1, :] = l_s[h : h + 1, :] * alpha + jnp.sum(p, axis=0, keepdims=True)
            m_s[h : h + 1, :] = m_new
            acc_s[at, :] = acc_s[at, :] * alpha + mm(vv, p.astype(bf16), TN)

    def plain(j, carry):
        step(j, False)
        return carry

    lax.fori_loop(0, i, plain, 0)
    step(i, True)
    for h in range(share):
        at = slice(h * HD, (h + 1) * HD)
        total = l_s[h : h + 1, :]
        ot_ref[at, :] = acc_s[at, :] / total
        lse_ref[h : h + 1, :] = m_s[h : h + 1, :] + jnp.log(total)
    out_ref[...] = ot_ref[...].T.astype(bf16)


def attn_fwd(q, kv, bq=1024):
    length, width = q.shape
    share = width // HD
    rows = max(8, share)
    return pl.pallas_call(
        functools.partial(fwd_kernel, bq, share),
        grid=(length // bq,),
        in_specs=[
            pl.BlockSpec((bq, width), lambda i: (i, 0)),
            pl.BlockSpec((length, 2 * HD), lambda i: (0, 0)),
        ],
        out_specs=[
            pl.BlockSpec((bq, width), lambda i: (i, 0)),
            pl.BlockSpec((width, bq), lambda i: (0, i)),
            pl.BlockSpec((rows, bq), lambda i: (0, i)),
        ],
        out_shape=[
            jax.ShapeDtypeStruct((length, width), bf16),
            jax.ShapeDtypeStruct((width, length), f32),
            jax.ShapeDtypeStruct((rows, length), f32),
        ],
        scratch_shapes=[
            pltpu.VMEM((rows, bq), f32),
            pltpu.VMEM((rows, bq), f32),
            pltpu.VMEM((width, bq), f32),
        ],
        compiler_params=params(),
        cost_estimate=cost(8 * length * length * width, 8 * length * width, share * length * length // 2),
        name="attn_fwd",
    )(q, kv)


def bwd_kernel(
    bq, share, q_ref, kv_ref, do_ref, ot_ref, lse_ref, cos_ref, sin_ref, dq_ref, dkv_ref, dqt_s, dk_s, dv_s
):
    i = pl.program_id(0)

    @pl.when(i == 0)
    def _():
        dk_s[...] = jnp.zeros(dk_s.shape, f32)
        dv_s[...] = jnp.zeros(dv_s.shape, f32)

    dqt_s[...] = jnp.zeros(dqt_s.shape, f32)
    qs = q_ref[...] * jnp.asarray(HD**-0.5, bf16)
    do = do_ref[...]
    product = do.astype(f32).T * ot_ref[...]
    inner = [jnp.sum(product[h * HD : (h + 1) * HD], axis=0, keepdims=True) for h in range(share)]

    def step(j, masked):
        start = pl.multiple_of(j * bq, bq)
        kk = kv_ref[pl.ds(start, bq), :HD]
        vv = kv_ref[pl.ds(start, bq), HD:]
        dk = jnp.zeros((bq, HD), f32)
        dv = jnp.zeros((bq, HD), f32)
        for h in range(share):
            at = slice(h * HD, (h + 1) * HD)
            s = mm(kk, qs[:, at], NT)
            p = jnp.exp(s - lse_ref[h : h + 1, :])
            if masked:
                ki = lax.broadcasted_iota(jnp.int32, s.shape, 0)
                qi = lax.broadcasted_iota(jnp.int32, s.shape, 1)
                p = jnp.where(ki <= qi, p, 0.0)
            dp = mm(vv, do[:, at], NT)
            ds = (p * (dp - inner[h])).astype(bf16)
            dv = dv + mm(p.astype(bf16), do[:, at], NN)
            dk = dk + mm(ds, qs[:, at], NN)
            dqt_s[at, :] += mm(kk, ds, TN)
        dk_s[pl.ds(start, bq), :] += dk
        dv_s[pl.ds(start, bq), :] += dv

    def plain(j, carry):
        step(j, False)
        return carry

    lax.fori_loop(0, i, plain, 0)
    step(i, True)
    dq = (dqt_s[...] * (HD**-0.5)).T.astype(bf16).astype(f32)
    rows = pl.ds(pl.multiple_of(i * bq, bq), bq)
    for at in range(0, share * HD, LANES):
        part = dq[:, at : at + LANES]
        dq_ref[:, at : at + LANES] = turn(part, cos_ref[rows, :], -sin_ref[rows, :]).astype(bf16)

    @pl.when(i == pl.num_programs(0) - 1)
    def _():
        both = jnp.concatenate([dk_s[...], dv_s[...]], axis=1).astype(bf16).astype(f32)
        lane = lax.broadcasted_iota(jnp.int32, both.shape, 1)
        turned = turn(both, cos_ref[...], -sin_ref[...])
        dkv_ref[...] = jnp.where(lane < HD, turned, both).astype(bf16)


def attn_bwd(q, kv, do, ot, lse, cos, sin, bq=512):
    length, width = q.shape
    share = width // HD
    rows = lse.shape[0]
    return pl.pallas_call(
        functools.partial(bwd_kernel, bq, share),
        grid=(length // bq,),
        in_specs=[
            pl.BlockSpec((bq, width), lambda i: (i, 0)),
            pl.BlockSpec((length, 2 * HD), lambda i: (0, 0)),
            pl.BlockSpec((bq, width), lambda i: (i, 0)),
            pl.BlockSpec((width, bq), lambda i: (0, i)),
            pl.BlockSpec((rows, bq), lambda i: (0, i)),
            pl.BlockSpec((length, LANES), lambda i: (0, 0)),
            pl.BlockSpec((length, LANES), lambda i: (0, 0)),
        ],
        out_specs=[
            pl.BlockSpec((bq, width), lambda i: (i, 0)),
            pl.BlockSpec((length, 2 * HD), lambda i: (0, 0)),
        ],
        out_shape=[
            jax.ShapeDtypeStruct((length, width), bf16),
            jax.ShapeDtypeStruct((length, 2 * HD), bf16),
        ],
        scratch_shapes=[
            pltpu.VMEM((width, bq), f32),
            pltpu.VMEM((length, HD), f32),
            pltpu.VMEM((length, HD), f32),
        ],
        compiler_params=params(),
        cost_estimate=cost(20 * length * length * width, 16 * length * width, share * length * length // 2),
        name="attn_bwd",
    )(q, kv, do, ot, lse, cos, sin)


def out_kernel(mixed, w, x, gain, middle, normed, acc):
    g = pl.program_id(0)

    @pl.when(g == 0)
    def _():
        acc[...] = x[...].astype(f32)

    acc[...] += mm(mixed[0], w[...], NN)

    @pl.when(g == pl.num_programs(0) - 1)
    def _():
        total = acc[...]
        middle[...] = total
        inverse = lax.rsqrt(jnp.mean(total * total, axis=-1, keepdims=True) + epsilon)
        normed[...] = (total * inverse * gain[...]).astype(bf16)


def out_call(mixed, w, x, gain):
    groups, rows, part = mixed.shape
    depth = w.shape[1]
    return pl.pallas_call(
        out_kernel,
        grid=(groups,),
        in_specs=[
            pl.BlockSpec((1, rows, part), lambda g: (g, 0, 0)),
            pl.BlockSpec((part, depth), lambda g: (g, 0)),
            pl.BlockSpec((rows, depth), lambda g: (0, 0)),
            pl.BlockSpec((1, depth), lambda g: (0, 0)),
        ],
        out_specs=[
            pl.BlockSpec((rows, depth), lambda g: (0, 0)),
            pl.BlockSpec((rows, depth), lambda g: (0, 0)),
        ],
        out_shape=[
            jax.ShapeDtypeStruct((rows, depth), f32),
            jax.ShapeDtypeStruct((rows, depth), bf16),
        ],
        scratch_shapes=[pltpu.VMEM((rows, depth), f32)],
        compiler_params=params(),
        cost_estimate=cost(2 * groups * part * rows * depth, 2 * groups * part * depth + 8 * rows * depth),
        name="out_norm",
    )(mixed, w, x, gain)


def ffn_kernel(
    x_mine, x_other, c_mine, c_other, w_gate, w_up, w_down,
    hidden, d_gate, d_up, back_mine, back_other, down_mine, down_other, back, down,
):
    u = pl.program_id(0)
    x = jnp.concatenate([x_mine[...], x_other[...]], axis=0)
    c = jnp.concatenate([c_mine[...], c_other[...]], axis=0)
    gate = mm(x, w_gate[...], NN)
    up = mm(x, w_up[...], NN)
    grad = mm(c, w_down[...], NN)
    sig = jax.nn.sigmoid(gate)
    silu = gate * sig
    act = (silu * up).astype(bf16)
    dg = (grad * up * sig * (1.0 + gate * (1.0 - sig))).astype(bf16)
    du = (grad * silu).astype(bf16)
    hidden[...] = act
    d_gate[...] = dg
    d_up[...] = du

    @pl.when(u == 0)
    def _():
        back[...] = mm(dg, w_gate[...], NT) + mm(du, w_up[...], NT)
        down[...] = mm(act, w_down[...], NT)

    @pl.when(u > 0)
    def _():
        back[...] += mm(dg, w_gate[...], NT) + mm(du, w_up[...], NT)
        down[...] += mm(act, w_down[...], NT)

    @pl.when(u == pl.num_programs(0) - 1)
    def _():
        rows = back_mine.shape[0]
        back_mine[...] = back[:rows].astype(bf16)
        back_other[...] = back[rows:].astype(bf16)
        down_mine[...] = down[:rows].astype(bf16)
        down_other[...] = down[rows:].astype(bf16)


def ffn_call(x_mine, x_other, c_mine, c_other, w_gate, w_up, w_down, tile=256):
    rows, depth = x_mine.shape
    units = w_gate.shape[1]
    block = pl.BlockSpec((rows, depth), lambda u: (0, 0))
    weight = pl.BlockSpec((depth, tile), lambda u: (0, u))
    act = pl.BlockSpec((2 * rows, tile), lambda u: (0, u))
    act_shape = jax.ShapeDtypeStruct((2 * rows, units), bf16)
    row_shape = jax.ShapeDtypeStruct((rows, depth), bf16)
    return pl.pallas_call(
        ffn_kernel,
        grid=(units // tile,),
        in_specs=[block] * 4 + [weight] * 3,
        out_specs=[act] * 3 + [block] * 4,
        out_shape=[act_shape] * 3 + [row_shape] * 4,
        scratch_shapes=[pltpu.VMEM((2 * rows, depth), f32)] * 2,
        compiler_params=params(),
        cost_estimate=cost(24 * rows * depth * units, 6 * depth * units + 20 * rows * depth + 12 * rows * units),
        name="ffn",
    )(x_mine, x_other, c_mine, c_other, w_gate, w_up, w_down)


def mid_kernel(got, own, middle, cot, gain, w, d_middle, branch, d_gain, d_mixed, low):
    @pl.when(pl.program_id(0) == 0)
    def _():
        grad = got[...].astype(f32) + own[...].astype(f32)
        m = middle[...]
        inverse = lax.rsqrt(jnp.mean(m * m, axis=-1, keepdims=True) + epsilon)
        scaled = grad * gain[...]
        slope = jnp.mean(m * scaled, axis=-1, keepdims=True) * (inverse * inverse * inverse)
        total = cot[...].astype(f32) + inverse * scaled - m * slope
        d_middle[...] = total
        branch[...] = total.astype(bf16)
        low[...] = total.astype(bf16)
        d_gain[...] = jnp.sum(grad * m * inverse, axis=0, keepdims=True)

    d_mixed[0] = mm(low[...], w[...], NT).astype(bf16)


def mid_call(got, own, middle, cot, gain, w, part):
    rows, depth = middle.shape
    groups = w.shape[0] // part
    block = pl.BlockSpec((rows, depth), lambda g: (0, 0))
    line = pl.BlockSpec((1, depth), lambda g: (0, 0))
    return pl.pallas_call(
        mid_kernel,
        grid=(groups,),
        in_specs=[block, block, block, block, line, pl.BlockSpec((part, depth), lambda g: (g, 0))],
        out_specs=[block, block, line, pl.BlockSpec((1, rows, part), lambda g: (g, 0, 0))],
        out_shape=[
            jax.ShapeDtypeStruct((rows, depth), f32),
            jax.ShapeDtypeStruct((rows, depth), bf16),
            jax.ShapeDtypeStruct((1, depth), f32),
            jax.ShapeDtypeStruct((groups, rows, part), bf16),
        ],
        scratch_shapes=[pltpu.VMEM((rows, depth), bf16)],
        compiler_params=params(),
        cost_estimate=cost(2 * groups * part * rows * depth, 2 * groups * part * depth + 16 * rows * depth),
        name="mid",
    )(got, own, middle, cot, gain, w)


def first_kernel(got, own, x_ref, d_middle, gain, out):
    grad = got[...].astype(f32) + own[...].astype(f32)
    x = x_ref[...].astype(f32)
    inverse = lax.rsqrt(jnp.mean(x * x, axis=-1, keepdims=True) + epsilon)
    scaled = grad * gain[...]
    slope = jnp.mean(x * scaled, axis=-1, keepdims=True) * (inverse * inverse * inverse)
    out[...] = (d_middle[...] + inverse * scaled - x * slope).astype(bf16)


def first_call(got, own, x, d_middle, gain):
    rows, depth = x.shape
    return pl.pallas_call(
        first_kernel,
        out_shape=jax.ShapeDtypeStruct((rows, depth), bf16),
        compiler_params=params(),
        cost_estimate=cost(20 * rows * depth, 12 * rows * depth),
        name="first_norm_back",
    )(got, own, x, d_middle, gain)


def after(value, *others):
    return lax.optimization_barrier((value,) + others)[0]


def shards(
    tokens, gain_attn, w_query, w_key, w_value, w_out, gain_mlp, w_gate, w_up, w_down, cotangent
):
    groups = lax.axis_size("seq")
    dp_count = lax.axis_size("dp")
    seq_count, piece, depth = tokens.shape
    assert seq_count == 1 and groups >= KV and groups % 2 == 0
    length = piece * groups
    width = H // groups * HD
    repeat = groups // KV
    own_rows = w_query.shape[0]

    chips = groups // 2
    half = chips // 2
    order = list(range(half)) + list(range(chips - 1, half - 1, -1))
    place = np.argsort(order)
    follow = [order[(place[c] + 1) % chips] for c in range(chips)]
    ring = [(2 * c + k, 2 * follow[c] + k) for c in range(chips) for k in range(2)]
    swap = [(i, i ^ 1) for i in range(groups)]

    seq_at = lax.axis_index("seq")
    core_at = seq_at % 2
    ring_at = jnp.asarray(place, jnp.int32)[seq_at // 2]
    chunk = [jnp.asarray(order, jnp.int32)[(ring_at + (chips - s)) % chips] for s in range(chips)]
    mine_at = [(2 * c + core_at) * piece for c in chunk]
    other_at = [(2 * c + 1 - core_at) * piece for c in chunk]
    dp_at = lax.axis_index("dp")

    def step_ring(x):
        return lax.ppermute(x, "seq", ring)

    def step_swap(x):
        return lax.ppermute(x, "seq", swap)

    def ring_gather(x):
        mine, other = [x], [step_swap(x)]
        for _ in range(chips - 1):
            mine.append(step_ring(mine[-1]))
            other.append(step_swap(mine[-1]))
        return mine, other

    def rows_at(x, start, count):
        return lax.dynamic_slice_in_dim(x, start, count, 0)

    x_own = tokens.reshape(piece, depth)
    cot_own = cotangent.reshape(piece, depth)

    def per_group(w):
        return jnp.repeat(w.reshape(own_rows, KV, HD), repeat, axis=1)

    gains_own = jnp.stack([gain_attn, gain_mlp], axis=-1)
    gains_own = jnp.pad(gains_own, ((0, 0), (0, LANES - 2)))
    gains_own = jnp.broadcast_to(gains_own[:, None, :], (own_rows, groups, LANES))
    own_cols = jnp.concatenate(
        [w_query.reshape(own_rows, groups, width), per_group(w_key), per_group(w_value), gains_own], axis=-1
    )
    cols = own_cols.shape[-1]
    cols_dp = lax.all_to_all(jnp.transpose(own_cols, (1, 0, 2)), "seq", 0, 0, tiled=True)
    dp_rows = groups * own_rows
    cols_dp = cols_dp.reshape(dp_rows, cols)
    cols_all = jnp.zeros((depth, cols), bf16)
    for k in range(dp_count):
        block = cols_dp if k == 0 else lax.ppermute(cols_dp, "dp", [(i, i ^ k) for i in range(dp_count)])
        cols_all = lax.dynamic_update_slice_in_dim(cols_all, block, (dp_at ^ k) * dp_rows, 0)
    w_qkv = cols_all[:, : width + 2 * HD]
    gains = jnp.transpose(cols_all[:, width + 2 * HD : width + 2 * HD + 2].astype(f32))
    gain_one, gain_two = gains[:1], gains[1:]

    out_full = lax.all_gather(w_out, ("dp", "seq"), axis=0, tiled=True)
    gate_full = lax.all_gather(w_gate, "dp", axis=0, tiled=True)
    up_full = lax.all_gather(w_up, "dp", axis=0, tiled=True)
    down_full = lax.all_gather(w_down, "dp", axis=0, tiled=True)

    cos, sin = rope_tables(length)

    x_mine, x_other = ring_gather(x_own)
    queries = jnp.zeros((length, width), bf16)
    keys_values = jnp.zeros((length, 2 * HD), bf16)
    normed_parts = []
    for s in range(chips):
        cos_s = jnp.concatenate([rows_at(cos, mine_at[s], piece), rows_at(cos, other_at[s], piece)], axis=0)
        sin_s = jnp.concatenate([rows_at(sin, mine_at[s], piece), rows_at(sin, other_at[s], piece)], axis=0)
        normed, qkv = qkv_call(x_mine[s], x_other[s], gain_one, w_qkv, cos_s, sin_s, width)
        normed_parts.append(normed)
        for start, part in ((mine_at[s], qkv[:piece]), (other_at[s], qkv[piece:])):
            queries = lax.dynamic_update_slice_in_dim(queries, part[:, :width], start, 0)
            keys_values = lax.dynamic_update_slice_in_dim(keys_values, part[:, width:], start, 0)

    c_mine, c_other = ring_gather(after(cot_own, x_mine[-1]))

    head_out, out_t, lse = attn_fwd(queries, keys_values)
    mixed = lax.all_to_all(head_out.reshape(groups, piece, width), "seq", 0, 0, tiled=True)
    middle, normed_two = out_call(mixed, out_full, x_own, gain_two)

    n_mine, n_other = ring_gather(normed_two)
    ffn = [
        ffn_call(n_mine[s], n_other[s], c_mine[s], c_other[s], gate_full, up_full, down_full)
        for s in range(chips)
    ]

    def ring_scatter(mine, other):
        got = [step_swap(o) for o in other]

        def own(s):
            return mine[s].astype(f32) + got[s].astype(f32)

        acc = own(1).astype(bf16)
        for s in range(2, chips):
            acc = (step_ring(acc).astype(f32) + own(s)).astype(bf16)
        return step_ring(acc), own(0)

    back_got, back_own = ring_scatter([f[3] for f in ffn], [f[4] for f in ffn])
    d_middle, branch, d_gain_two, d_mixed = mid_call(
        back_got, back_own, middle, cot_own, gain_two, out_full, width
    )
    down_got, down_own = ring_scatter(
        [after(f[5], back_got) for f in ffn], [after(f[6], back_got) for f in ffn]
    )
    block_out = (middle + (down_got.astype(f32) + down_own)).astype(bf16)

    n_all = jnp.concatenate([b for pair in zip(n_mine, n_other) for b in pair], axis=0)
    c_all = jnp.concatenate([b for pair in zip(c_mine, c_other) for b in pair], axis=0)

    def weight_grad(rows, grads):
        return mm(rows, jnp.concatenate(grads, axis=0), TN).astype(bf16)

    def scatter_dp(x):
        return lax.psum_scatter(x, "dp", scatter_dimension=0, tiled=True)

    grad_gate = scatter_dp(weight_grad(n_all, [f[1] for f in ffn])).astype(f32)
    grad_up = scatter_dp(weight_grad(n_all, [f[2] for f in ffn])).astype(f32)
    grad_down = scatter_dp(weight_grad(c_all, [f[0] for f in ffn])).astype(f32)

    grad_out = jnp.einsum("gnh,nd->ghd", mixed, branch, preferred_element_type=f32)
    grad_out = scatter_dp(grad_out.reshape(groups * width, depth).astype(bf16))
    grad_out = lax.psum_scatter(grad_out, "seq", scatter_dimension=0, tiled=True).astype(f32)

    d_heads = lax.all_to_all(d_mixed, "seq", 0, 0, tiled=True).reshape(length, width)
    d_queries, d_kv = attn_bwd(queries, keys_values, d_heads, out_t, lse, cos, sin)
    d_qkv = jnp.concatenate([d_queries, d_kv], axis=1)
    d_parts = [
        jnp.concatenate([rows_at(d_qkv, mine_at[s], piece), rows_at(d_qkv, other_at[s], piece)], axis=0)
        for s in range(chips)
    ]
    d_normed = [mm(part, w_qkv, NT).astype(bf16) for part in d_parts]
    first_got, first_own = ring_scatter([d[:piece] for d in d_normed], [d[piece:] for d in d_normed])
    grad_tokens = first_call(first_got, first_own, x_own, d_middle, gain_one)

    grad_cols = mm(jnp.concatenate(normed_parts, axis=0), jnp.concatenate(d_parts, axis=0), TN)
    high = d_gain_two.astype(bf16)
    rest = (d_gain_two - high.astype(f32)).astype(bf16)
    extra = jnp.pad(jnp.transpose(jnp.concatenate([high, rest], axis=0)), ((0, 0), (0, LANES - 2)))
    grad_cols = jnp.concatenate([grad_cols.astype(bf16), extra], axis=1)
    total = rows_at(grad_cols, dp_at * dp_rows, dp_rows).astype(f32)
    for k in range(1, dp_count):
        send = rows_at(grad_cols, (dp_at ^ k) * dp_rows, dp_rows)
        total = total + lax.ppermute(send, "dp", [(i, i ^ k) for i in range(dp_count)]).astype(f32)
    dealt = lax.all_to_all(
        total.astype(bf16).reshape(groups, own_rows, cols), "seq", 0, 0, tiled=True
    ).astype(f32)

    def join(x):
        return jnp.transpose(x, (1, 0, 2)).reshape(own_rows, -1)

    def fold(x):
        return join(jnp.sum(x.reshape(KV, repeat, own_rows, HD), axis=1))

    grad_query = join(dealt[:, :, :width])
    grad_key = fold(dealt[:, :, width : width + HD])
    grad_value = fold(dealt[:, :, width + HD : width + 2 * HD])
    grad_gain_two = jnp.sum(dealt[:, :, width + 2 * HD : width + 2 * HD + 2], axis=(0, 2))

    def against(w, grad):
        return jnp.sum(w.astype(f32) * grad, axis=1)

    grad_gain_one = against(w_query, grad_query) + against(w_key, grad_key) + against(w_value, grad_value)
    grad_gain_one = grad_gain_one / gain_attn.astype(f32)

    return (
        block_out.reshape(1, piece, depth),
        grad_tokens.reshape(1, piece, depth),
        grad_gain_one,
        grad_query,
        grad_key,
        grad_value,
        grad_out,
        grad_gain_two,
        grad_gate,
        grad_up,
        grad_down,
    )


def solution(mesh):
    rows = P("dp", "seq", None)
    both = P(("dp", "seq"))
    flat = P(("dp", "seq"), None)
    tiles = P("dp", "seq")
    in_specs = (rows, both, flat, flat, flat, flat, both, tiles, tiles, tiles, rows)
    out_specs = (rows, rows, both, flat, flat, flat, flat, both, tiles, tiles, tiles)
    return jax.shard_map(shards, mesh=mesh, in_specs=in_specs, out_specs=out_specs, check_vma=False)
```

time: 1680 us -> 828 us (0.49)
  waiting for transfers between devices: 973 us -> 388 us
  matrix products: 286 us -> 53 us
  Pallas kernels: 0 us -> 191 us
  blocking collectives: 132 us -> 0 us
  other arithmetic: 131 us -> 49.8 us
  local copies, waits for them, and re-layouts: 107 us -> 63.3 us
  starting transfers between devices: 22.6 us -> 53.4 us
    reduce_scatter x6 -> x5, waiting for transfers between devices: 539 us -> 8.88 us  [the longest x1 8.88 us: shards(): lax.psum_scatter(grad_out, 'seq', scatter_dimension=0, tiled=True)]
    all_gather x9 -> x4, waiting for transfers between devices: 338 us -> 60.5 us  [the longest x1 54.3 us: shards(): down_full = lax.all_gather(w_down, 'dp', axis=0, tiled=True)]
    ppermute x0 -> x48, waiting for transfers between devices: none -> 260 us  [the longest x18 216 us: step_ring(): return lax.ppermute(x, 'seq', ring)]
    dot_general x45 -> x9, matrix products: 286 us -> 53 us  [the longest x8 47.3 us: mm(): return lax.dot_general(a, b, dims, preferred_element_type=f32)]
    pallas_call x0 -> x13, Pallas kernels: none -> 191 us  [the longest x4 85.1 us: ffn_call(): pl.pallas_call(ffn_kernel, grid=(units // tile,), in_specs=[block] * 4 +...]
    unnamed x2 -> x0, blocking collectives: 83.7 us -> none
    all_to_all x2 -> x0, blocking collectives: 48.1 us -> none  [the longest x1 32.4 us: shards(): lax.all_to_all(for_sending(query_grad), 'seq', split_axis=1, concat_axis=...]
    unnamed x7 -> x0, other arithmetic: 48.1 us -> none
  transfers between devices with their start and end apart: 21 -> 61, of which waited for: 15 -> 21; matrix products, arithmetic and copies ran while one was open for 26% -> 16% of each run, Pallas kernels for 0% -> 22%
where the time goes in v1:
time: 828 us; the launch traced here: 819 us
  waiting for transfers between devices  388 us (47%)
  Pallas kernels  191 us (23%)
  local copies, waits for them, and re-layouts  63.3 us (8%)
  starting transfers between devices  53.4 us (6%)
  matrix products  53 us (6%)
  other arithmetic  49.8 us (6%)
  between operations  21 us (3%)
    ppermute x18, waiting for transfers between devices, step_ring(): return lax.ppermute(x, 'seq', ring)  216 us
    pallas_call x4, Pallas kernels, ffn_call(): pl.pallas_call(ffn_kernel, grid=(units // tile,), in_specs=[block] * 4 +...  85.1 us
    all_gather x1, waiting for transfers between devices, shards(): down_full = lax.all_gather(w_down, 'dp', axis=0, tiled=True)  54.3 us
    dot_general x8, matrix products, mm(): return lax.dot_general(a, b, dims, preferred_element_type=f32)  47.3 us
    unnamed x175, local copies, waits for them, and re-layouts  41.8 us
    pallas_call x1, Pallas kernels, attn_bwd(): pl.pallas_call(functools.partial(bwd_kernel, bq, share), grid=(length //...  33.3 us
    all_to_all x1, waiting for transfers between devices, shards(): lax.all_to_all(head_out.reshape(groups, piece, width), 'seq', 0, 0, tiled...  25.1 us
    ppermute x18, starting transfers between devices, step_ring(): return lax.ppermute(x, 'seq', ring)  24.8 us
  transfers between devices with their start and end apart: 61, of which 21 were waited for; matrix products, arithmetic and copies ran while one was open for 16% of the time, Pallas kernels for 22%

profile of v1, /device:TPU:0, one launch (start us, length us, event | category | flops | bytes accessed | tf_op | source)
XLA Modules:
  0.0 819.1 jit_solution(1828247453371059158)
XLA Ops:
  30.7 22.9 %all-to-all-done = bf16[8,64,512]{2,1,0:T(8,128)(2,1)S(1)} async-done(((bf16[8,64,512]{2,1,0:T(8,128)(2,1)}), bf16[8,64,512]{2,1,0:T(8,128)(2,1)S(1)}, u32[]{:S(2)}, u32[]{:S(2)}) %all-to-all-start) | async-done | bytes 524320 | tf_op jit(solution)/shard_map/all_to_all | solution.py:483
  62.7 14.6 %collective-permute-done.1 = bf16[512,512]{0,1:T(8,128)(2,1)} collective-permute-done((bf16[512,512]{0,1:T(8,128)(2,1)}, bf16[512,512]{0,1:T(8,128)(2,1)}, u32[]{:S(2)}, u32[]{:S(2)}) %collective-permute-start.1) | collective-permute-done | bytes 524320 | tf_op jit(solution)/shard_map/ppermute | solution.py:488
  79.4 8.2 collective-permute-done.3
  99.2 4.9 qkv.5
  104.1 41.2 %collective-permute-done.8.mine = bf16[256,2048]{1,0:T(8,128)(2,1)S(1)} collective-permute-done((bf16[256,2048]{1,0:T(8,128)(2,1)}, bf16[256,2048]{1,0:T(8,128)(2,1)S(1)}, u32[]{:S(2)}, u32[]{:S(2)}) %collective-permute-start.8) | collective-permute-done | bytes 1048608 | tf_op jit(solution)/shard_map/ppermute | solution.py:455
  153.4 19.8 %attn_fwd.1 = (bf16[2048,256]{1,0:T(8,128)(2,1)}, f32[256,2048]{1,0:T(8,128)}, f32[8,2048]{1,0:T(8,128)S(1)}) custom-call(bf16[2048,256]{1,0:T(8,128)(2,1)S(1)} %slice_dynamic-update-slice_fusion.q_ref, bf16[2048,128]{1,0:T(8,128)(2,1)S(1)} %slice_dynamic-update-slice_fusion.8.kv_ref), custom_call_target="tpu_custom_call" | custom-call | flops 8589934592 | bytes 4194304 | tf_op jit(solution)/shard_map/attn_fwd/pallas_call | solution.py:138
  180.0 25.1 %all-to-all-done.1.mixed = bf16[8,256,256]{2,1,0:T(8,128)(2,1)S(1)} async-done(((bf16[8,256,256]{2,1,0:T(8,128)(2,1)}), bf16[8,256,256]{2,1,0:T(8,128)(2,1)S(1)}, u32[]{:S(2)}, u32[]{:S(2)}) %all-to-all-start.1) | async-done | bytes 1048608 | tf_op jit(solution)/shard_map/all_to_all | solution.py:517
  205.1 18.9 %out_norm.1 = (f32[256,2048]{1,0:T(8,128)}, bf16[256,2048]{1,0:T(8,128)(2,1)S(1)}) custom-call(bf16[8,256,256]{2,1,0:T(8,128)(2,1)S(1)} %all-to-all-done.1.mixed, bf16[2048,2048]{1,0:T(8,128)(2,1)} %all-gather.5.cloned.1.call-done.w, bf16[256,2048]{1,0:T(8,128)(2,1)S(1)} %bitcast.47, f32[1,2048]{1,0:T(1,128)S(1)} %get-tuple-element.160.gain), custom_call_target="tpu_custom_call" | custom-call | flops 2147483648 | bytes 12582912 | tf_op jit(solution)/shard_map/out_norm/pallas_call | solution.py:279
  227.5 22.0 %collective-permute-done.10.x_mine = bf16[256,2048]{1,0:T(8,128)(2,1)} collective-permute-done((bf16[256,2048]{1,0:T(8,128)(2,1)S(1)}, bf16[256,2048]{1,0:T(8,128)(2,1)}, u32[]{:S(2)}, u32[]{:S(2)}) %collective-permute-start.10) | collective-permute-done | bytes 1048608 | tf_op jit(solution)/shard_map/ppermute | solution.py:455
  251.8 6.2 all-gather.9.cloned.1.call-done.w_up
  257.9 54.3 %all-gather.11.cloned.1.call-done.w_down = bf16[2048,1024]{1,0:T(8,128)(2,1)} async-done(((bf16[512,1024]{1,0:T(8,128)(2,1)}), bf16[2048,1024]{1,0:T(8,128)(2,1)}) %all-gather.11.cloned.1.call-update) | async-done | bytes 4194320 | tf_op jit(solution)/shard_map/all_gather | solution.py:497
  312.3 21.2 %ffn.4 = (bf16[512,1024]{1,0:T(8,128)(2,1)S(1)}, bf16[512,1024]{1,0:T(8,128)(2,1)S(1)}, bf16[512,1024]{1,0:T(8,128)(2,1)S(1)}, bf16[256,2048]{1,0:T(8,128)(2,1)}...) custom-call(bf16[256,2048]{1,0:T(8,128)(2,1)} %collective-permute-done.10.x_mine, ...), custom_call_target="tpu_custom_call" | custom-call | flops 12884901888 | bytes 26214400 | tf_op jit(solution)/shard_map/ffn/pallas_call | solution.py:349
  344.1 21.2 %ffn.5 = (bf16[512,1024]{1,0:T(8,128)(2,1)S(1)}, bf16[512,1024]{1,0:T(8,128)(2,1)S(1)}, bf16[512,1024]{1,0:T(8,128)(2,1)S(1)}, bf16[256,2048]{1,0:T(8,128)(2,1)}...) custom-call(bf16[256,2048]{1,0:T(8,128)(2,1)} %collective-permute-done.16.x_mine, ...), custom_call_target="tpu_custom_call" | custom-call | flops 12884901888 | bytes 26214400 | tf_op jit(solution)/shard_map/ffn/pallas_call | solution.py:349
  366.0 19.7 %collective-permute-done.22.x_mine = bf16[256,2048]{1,0:T(8,128)(2,1)S(1)} collective-permute-done((bf16[256,2048]{1,0:T(8,128)(2,1)}, bf16[256,2048]{1,0:T(8,128)(2,1)S(1)}, u32[]{:S(2)}, u32[]{:S(2)}) %collective-permute-start.22) | collective-permute-done | bytes 1048608 | tf_op jit(solution)/shard_map/ppermute | solution.py:455
  386.2 21.4 %collective-permute-done.15 = bf16[256,2048]{1,0:T(8,128)(2,1)S(1)} collective-permute-done((bf16[256,2048]{1,0:T(8,128)(2,1)S(1)}, bf16[256,2048]{1,0:T(8,128)(2,1)S(1)}, u32[]{:S(2)}, u32[]{:S(2)}) %collective-permute-start.15) | collective-permute-done | bytes 1048608 | tf_op jit(solution)/shard_map/ppermute | solution.py:455
  413.1 21.4 %ffn.6 = (bf16[512,1024]{1,0:T(8,128)(2,1)S(1)}, bf16[512,1024]{1,0:T(8,128)(2,1)S(1)}, bf16[512,1024]{1,0:T(8,128)(2,1)S(1)}, bf16[256,2048]{1,0:T(8,128)(2,1)}...) custom-call(bf16[256,2048]{1,0:T(8,128)(2,1)} %copy-done.43, ...), custom_call_target="tpu_custom_call" | custom-call | flops 12884901888 | bytes 26214400 | tf_op jit(solution)/shard_map/ffn/pallas_call | solution.py:349
  439.6 21.2 %ffn.7 = (bf16[512,1024]{1,0:T(8,128)(2,1)S(1)}, bf16[512,1024]{1,0:T(8,128)(2,1)S(1)}, bf16[512,1024]{1,0:T(8,128)(2,1)S(1)}, bf16[256,2048]{1,0:T(8,128)(2,1)}...) custom-call(bf16[256,2048]{1,0:T(8,128)(2,1)} %copy-done.1, ...), custom_call_target="tpu_custom_call" | custom-call | flops 12884901888 | bytes 26214400 | tf_op jit(solution)/shard_map/ffn/pallas_call | solution.py:349
  467.8 21.2 %collective-permute-done.27.got = bf16[256,2048]{1,0:T(8,128)(2,1)S(1)} collective-permute-done((bf16[256,2048]{1,0:T(8,128)(2,1)S(1)}, bf16[256,2048]{1,0:T(8,128)(2,1)S(1)}, u32[]{:S(2)}, u32[]{:S(2)}) %collective-permute-start.27) | collective-permute-done | bytes 1048608 | tf_op jit(solution)/shard_map/ppermute | solution.py:455
  489.0 12.8 %mid.1 = (f32[256,2048]{1,0:T(8,128)}, bf16[256,2048]{1,0:T(8,128)(2,1)S(1)}, f32[1,2048]{1,0:T(1,128)S(1)}, bf16[8,256,256]{2,1,0:T(8,128)(2,1)}) custom-call(bf16[256,2048]{1,0:T(8,128)(2,1)S(1)} %collective-permute-done.27.got, f32[256,2048]{1,0:T(8,128)} %convert_add_fusion.1.own, f32[256,2048]{1,0:T(8,128)} %get-tuple-element.72.middle, ...), custom_call_target="tpu_custom_call" | custom-call | flops 2147483648 | bytes 16777216 | tf_op jit(solution)/shard_map/mid/pallas_call | solution.py:384
  501.8 5.8 convolution_convert_fusion
  519.1 10.6 %fusion.36 = bf16[2048,1024]{1,0:T(8,128)(2,1)} fusion(bf16[2048,2048]{1,0:T(8,128)(2,1)S(1)} %constant_dynamic-update-slice_fusion.10, bf16[512,1024]{1,0:T(8,128)(2,1)S(1)} %copy-done.23, bf16[512,1024]{1,0:T(8,128)(2,1)S(1)} %copy-done.19, bf16[512,1024]{1,0:T(8,128)(2,1)S(1)} %copy-done.14, bf16[512,1024]{1,0:T(8,128)(2,1)S(1)} %get-tuple-element.115), kind=kOutput, calls=%fused_computation.36 | convolution fusion | flops 8608808960 | bytes 16777216 | tf_op jit(solution)/shard_map/dot_general | solution.py:31
  531.3 13.7 %fusion.39 = bf16[2048,1024]{1,0:T(8,128)(2,1)} fusion(bf16[2048,2048]{1,0:T(8,128)(2,1)} %copy-done.65, bf16[512,1024]{1,0:T(8,128)(2,1)} %copy-done.21, bf16[512,1024]{1,0:T(8,128)(2,1)S(1)} %copy-done.16, bf16[512,1024]{1,0:T(8,128)(2,1)S(1)} %copy-done.10, bf16[512,1024]{1,0:T(8,128)(2,1)} %copy-done.24), kind=kOutput, calls=%fused_computation.37 | convolution fusion | flops 8608808960 | bytes 16777216 | tf_op jit(solution)/shard_map/dot_general | solution.py:31
  560.7 13.5 %fusion.33 = bf16[2048,1024]{1,0:T(8,128)(2,1)} fusion(bf16[2048,2048]{1,0:T(8,128)(2,1)} %copy-done.66, bf16[512,1024]{1,0:T(8,128)(2,1)} %copy-done.17, bf16[512,1024]{1,0:T(8,128)(2,1)S(1)} %copy-done.12, bf16[512,1024]{1,0:T(8,128)(2,1)S(1)} %copy-done.8, bf16[512,1024]{1,0:T(8,128)(2,1)} %copy-done.20), kind=kOutput, calls=%fused_computation.35 | convolution fusion | flops 8608808960 | bytes 16777216 | tf_op jit(solution)/shard_map/dot_general | solution.py:31
  580.1 7.7 all-to-all-done.2
  587.8 33.3 %attn_bwd.1 = (bf16[2048,256]{1,0:T(8,128)(2,1)S(1)}, bf16[2048,128]{1,0:T(8,128)(2,1)S(1)}) custom-call(bf16[2048,256]{1,0:T(8,128)(2,1)S(1)} %copy-done.4, bf16[2048,128]{1,0:T(8,128)(2,1)S(1)} %copy-done.6, bf16[2048,256]{1,0:T(8,128)(2,1)} %bitcast.17.do_ref, f32[256,2048]{1,0:T(8,128)} %get-tuple-element.100.ot_ref, ...), custom_call_target="tpu_custom_call" | custom-call | flops 21474836480 | bytes 8388608 | tf_op jit(solution)/shard_map/attn_bwd/pallas_call | solution.py:228
  645.0 12.9 %collective-permute-done.45 = bf16[512,512]{0,1:T(8,128)(2,1)S(1)} collective-permute-done((bf16[512,512]{0,1:T(8,128)(2,1)S(1)}, bf16[512,512]{0,1:T(8,128)(2,1)S(1)}, u32[]{:S(2)}, u32[]{:S(2)}) %collective-permute-start.45) | collective-permute-done | bytes 524320 | tf_op jit(solution)/shard_map/ppermute | solution.py:582
  661.8 6.9 collective-permute-done.47
  690.4 27.5 %collective-permute-done.31 = bf16[256,2048]{1,0:T(8,128)(2,1)S(1)} collective-permute-done((bf16[256,2048]{1,0:T(8,128)(2,1)}, bf16[256,2048]{1,0:T(8,128)(2,1)S(1)}, u32[]{:S(2)}, u32[]{:S(2)}) %collective-permute-start.31) | collective-permute-done | bytes 1048608 | tf_op jit(solution)/shard_map/ppermute | solution.py:455
  722.4 18.0 %collective-permute-done.41 = bf16[256,2048]{1,0:T(8,128)(2,1)} collective-permute-done((bf16[256,2048]{1,0:T(8,128)(2,1)}, bf16[256,2048]{1,0:T(8,128)(2,1)}, u32[]{:S(2)}, u32[]{:S(2)}) %collective-permute-start.41) | collective-permute-done | bytes 1048608 | tf_op jit(solution)/shard_map/ppermute | solution.py:455
  744.2 18.7 %collective-permute-done.33 = bf16[256,2048]{1,0:T(8,128)(2,1)} collective-permute-done((bf16[256,2048]{1,0:T(8,128)(2,1)}, bf16[256,2048]{1,0:T(8,128)(2,1)}, u32[]{:S(2)}, u32[]{:S(2)}) %collective-permute-start.33) | collective-permute-done | bytes 1048608 | tf_op jit(solution)/shard_map/ppermute | solution.py:455
  766.2 22.4 %collective-permute-done.43.got = bf16[256,2048]{1,0:T(8,128)(2,1)S(1)} collective-permute-done((bf16[256,2048]{1,0:T(8,128)(2,1)S(1)}, bf16[256,2048]{1,0:T(8,128)(2,1)S(1)}, u32[]{:S(2)}, u32[]{:S(2)}) %collective-permute-start.43) | collective-permute-done | bytes 1048608 | tf_op jit(solution)/shard_map/ppermute | solution.py:455
  801.4 8.9 %reduce-scatter.8.cloned.1.call-done = bf16[64,2048]{1,0:T(8,128)(2,1)} async-done(((bf16[512,2048]{1,0:T(8,128)(2,1)}), bf16[64,2048]{1,0:T(8,128)(2,1)}) %reduce-scatter.8.cloned.1.call-update) | async-done | bytes 262160 | tf_op jit(solution)/shard_map/reduce_scatter | solution.py:561
  (390 shorter events, 199.9 us)
Async XLA Ops:
  7.2 197.8 %all-gather.5.cloned.1.call-start = ((), (), s32[]{:S(2)}) async-start(), calls=%async_computation.9 | async-start | bytes 8650752 | tf_op jit(solution)/shard_map/all_gather | solution.py:494
  8.0 243.8 %all-gather.7.cloned.1.call-start = ((), (), s32[]{:S(2)}) async-start(), calls=%async_computation.10 | async-start | bytes 5242880 | tf_op jit(solution)/shard_map/all_gather | solution.py:495
  8.7 249.2 %all-gather.9.cloned.1.call-start = ((), (), s32[]{:S(2)}) async-start(), calls=%async_computation.11 | async-start | bytes 5242880 | tf_op jit(solution)/shard_map/all_gather | solution.py:496
  9.5 52.1 %collective-permute-start.4 = (bf16[256,2048]{1,0:T(8,128)(2,1)S(1)}, bf16[256,2048]{1,0:T(8,128)(2,1)}, u32[]{:S(2)}, u32[]{:S(2)}) collective-permute-start(bf16[256,2048]{1,0:T(8,128)(2,1)S(1)} %bitcast.44), channel_id=1, source_target_pairs={{0,2},{1,3},{2,6},{3,7},{4,0},{5,1},{6,4},{7,5},{8,10},{9,11},{10,... | collective-permute-start | bytes 3145736 | tf_op jit(solution)/shard_map/ppermute | solution.py:455
  12.6 81.2 %collective-permute-start = (bf16[256,2048]{1,0:T(8,128)(2,1)S(1)}, bf16[256,2048]{1,0:T(8,128)(2,1)}, u32[]{:S(2)}, u32[]{:S(2)}) collective-permute-start(bf16[256,2048]{1,0:T(8,128)(2,1)S(1)} %bitcast.45), channel_id=1, source_target_pairs={{0,1},{1,0},{2,3},{3,2},{4,5},{5,4},{6,7},{7,6},{8,9},{9,8},{10,11... | collective-permute-start | bytes 3145736 | tf_op jit(solution)/shard_map/ppermute | solution.py:458
  14.2 39.4 %all-to-all-start = ((bf16[8,64,512]{2,1,0:T(8,128)(2,1)}), bf16[8,64,512]{2,1,0:T(8,128)(2,1)S(1)}, u32[]{:S(2)}, u32[]{:S(2)}) async-start(bf16[8,64,512]{2,1,0:T(8,128)(2,1)} %copy.65), calls=%async_computation | async-start | bytes 1048576 | tf_op jit(solution)/shard_map/all_to_all | solution.py:483
  18.2 294.1 %all-gather.11.cloned.1.call-start = ((), (), s32[]{:S(2)}) async-start(), calls=%async_computation.12 | async-start | bytes 5242880 | tf_op jit(solution)/shard_map/all_gather | solution.py:497
  97.9 47.4 %collective-permute-start.8 = (bf16[256,2048]{1,0:T(8,128)(2,1)}, bf16[256,2048]{1,0:T(8,128)(2,1)S(1)}, u32[]{:S(2)}, u32[]{:S(2)}) collective-permute-start(bf16[256,2048]{1,0:T(8,128)(2,1)} %collective-permute-done.6.mine), channel_id=1, source_target_pairs={{0,2},{1,3},{2,6},{3,7},{4,0},{5,1},{6,4},{7,5},{8,10},{9,11},{10,... | collective-permute-start | bytes 3145736 | tf_op jit(solution)/shard_map/ppermute | solution.py:455
  99.1 46.3 %collective-permute-start.7 = (bf16[256,2048]{1,0:T(8,128)(2,1)}, bf16[256,2048]{1,0:T(8,128)(2,1)S(1)}, u32[]{:S(2)}, u32[]{:S(2)}) collective-permute-start(bf16[256,2048]{1,0:T(8,128)(2,1)} %collective-permute-done.6.mine), channel_id=1, source_target_pairs={{0,1},{1,0},{2,3},{3,2},{4,5},{5,4},{6,7},{7,6},{8,9},{9,8},{10,11... | collective-permute-start | bytes 3145736 | tf_op jit(solution)/shard_map/ppermute | solution.py:458
  177.9 483.8 %reduce-scatter.6.cloned.1.call-start = ((), (), s32[]{:S(2)}) async-start(), calls=%async_computation.13 | async-start | bytes 10485760 | tf_op jit(solution)/shard_map/reduce_scatter | solution.py:553
  178.0 49.6 %collective-permute-start.12 = (bf16[256,2048]{1,0:T(8,128)(2,1)}, bf16[256,2048]{1,0:T(8,128)(2,1)}, u32[]{:S(2)}, u32[]{:S(2)}) collective-permute-start(bf16[256,2048]{1,0:T(8,128)(2,1)} %bitcast.15.c_mine.cot), channel_id=1, source_target_pairs={{0,2},{1,3},{2,6},{3,7},{4,0},{5,1},{6,4},{7,5},{8,10},{9,11},{10,... | collective-permute-start | bytes 3145736 | tf_op jit(solution)/shard_map/ppermute | solution.py:455
  249.5 62.7 %collective-permute-start.11 = (bf16[256,2048]{1,0:T(8,128)(2,1)}, bf16[256,2048]{1,0:T(8,128)(2,1)}, u32[]{:S(2)}, u32[]{:S(2)}) collective-permute-start(bf16[256,2048]{1,0:T(8,128)(2,1)} %collective-permute-done.10.x_mine), channel_id=1, source_target_pairs={{0,1},{1,0},{2,3},{3,2},{4,5},{5,4},{6,7},{7,6},{8,9},{9,8},{10,11... | collective-permute-start | bytes 3145736 | tf_op jit(solution)/shard_map/ppermute | solution.py:458
  249.5 85.9 %collective-permute-start.18 = (bf16[256,2048]{1,0:T(8,128)(2,1)}, bf16[256,2048]{1,0:T(8,128)(2,1)}, u32[]{:S(2)}, u32[]{:S(2)}) collective-permute-start(bf16[256,2048]{1,0:T(8,128)(2,1)} %collective-permute-done.12.c_mine), channel_id=1, source_target_pairs={{0,2},{1,3},{2,6},{3,7},{4,0},{5,1},{6,4},{7,5},{8,10},{9,11},{10,... | collective-permute-start | bytes 3145736 | tf_op jit(solution)/shard_map/ppermute | solution.py:455
  249.5 86.4 %collective-permute-start.16 = (bf16[256,2048]{1,0:T(8,128)(2,1)}, bf16[256,2048]{1,0:T(8,128)(2,1)}, u32[]{:S(2)}, u32[]{:S(2)}) collective-permute-start(bf16[256,2048]{1,0:T(8,128)(2,1)} %collective-permute-done.10.x_mine), channel_id=1, source_target_pairs={{0,2},{1,3},{2,6},{3,7},{4,0},{5,1},{6,4},{7,5},{8,10},{9,11},{10,... | collective-permute-start | bytes 3145736 | tf_op jit(solution)/shard_map/ppermute | solution.py:455
  337.6 48.1 %collective-permute-start.22 = (bf16[256,2048]{1,0:T(8,128)(2,1)}, bf16[256,2048]{1,0:T(8,128)(2,1)S(1)}, u32[]{:S(2)}, u32[]{:S(2)}) collective-permute-start(bf16[256,2048]{1,0:T(8,128)(2,1)} %collective-permute-done.16.x_mine), channel_id=1, source_target_pairs={{0,2},{1,3},{2,6},{3,7},{4,0},{5,1},{6,4},{7,5},{8,10},{9,11},{10,... | collective-permute-start | bytes 3145736 | tf_op jit(solution)/shard_map/ppermute | solution.py:455
  341.6 66.0 %collective-permute-start.15 = (bf16[256,2048]{1,0:T(8,128)(2,1)S(1)}, bf16[256,2048]{1,0:T(8,128)(2,1)S(1)}, u32[]{:S(2)}, u32[]{:S(2)}) collective-permute-start(bf16[256,2048]{1,0:T(8,128)(2,1)S(1)} %add_convert_fusion.9), channel_id=1, source_target_pairs={{0,2},{1,3},{2,6},{3,7},{4,0},{5,1},{6,4},{7,5},{8,10},{9,11},{10,... | collective-permute-start | bytes 3145736 | tf_op jit(solution)/shard_map/ppermute | solution.py:455
  365.4 42.3 %collective-permute-start.20 = (bf16[256,2048]{1,0:T(8,128)(2,1)}, bf16[256,2048]{1,0:T(8,128)(2,1)S(1)}, u32[]{:S(2)}, u32[]{:S(2)}) collective-permute-start(bf16[256,2048]{1,0:T(8,128)(2,1)} %get-tuple-element.79), channel_id=1, source_target_pairs={{0,1},{1,0},{2,3},{3,2},{4,5},{5,4},{6,7},{7,6},{8,9},{9,8},{10,11... | collective-permute-start | bytes 3145736 | tf_op jit(solution)/shard_map/ppermute | solution.py:458
  365.5 45.6 %collective-permute-start.25 = (bf16[256,2048]{1,0:T(8,128)(2,1)S(1)}, bf16[256,2048]{1,0:T(8,128)(2,1)S(1)}, u32[]{:S(2)}, u32[]{:S(2)}) collective-permute-start(bf16[256,2048]{1,0:T(8,128)(2,1)S(1)} %collective-permute-done.24.c_mine), channel_id=1, source_target_pairs={{0,1},{1,0},{2,3},{3,2},{4,5},{5,4},{6,7},{7,6},{8,9},{9,8},{10,11... | collective-permute-start | bytes 3145736 | tf_op jit(solution)/shard_map/ppermute | solution.py:458
  385.7 51.9 %collective-permute-start.35 = (bf16[256,2048]{1,0:T(8,128)(2,1)}, bf16[256,2048]{1,0:T(8,128)(2,1)S(1)}, u32[]{:S(2)}, u32[]{:S(2)}) collective-permute-start(bf16[256,2048]{1,0:T(8,128)(2,1)} %bitcast.15.c_mine.cot), channel_id=1, source_target_pairs={{0,1},{1,0},{2,3},{3,2},{4,5},{5,4},{6,7},{7,6},{8,9},{9,8},{10,11... | collective-permute-start | bytes 3145736 | tf_op jit(solution)/shard_map/ppermute | solution.py:458
  410.4 51.6 %collective-permute-start.21 = (bf16[256,2048]{1,0:T(8,128)(2,1)}, bf16[256,2048]{1,0:T(8,128)(2,1)S(1)}, u32[]{:S(2)}, u32[]{:S(2)}) collective-permute-start(bf16[256,2048]{1,0:T(8,128)(2,1)} %add_convert_fusion.8), channel_id=1, source_target_pairs={{0,2},{1,3},{2,6},{3,7},{4,0},{5,1},{6,4},{7,5},{8,10},{9,11},{10,... | collective-permute-start | bytes 3145736 | tf_op jit(solution)/shard_map/ppermute | solution.py:455
  507.6 285.4 %reduce-scatter.12.cloned.1.call-start = ((), (), s32[]{:S(2)}) async-start(), calls=%async_computation.16 | async-start | bytes 5242880 | tf_op jit(solution)/shard_map/reduce_scatter | solution.py:553
  529.8 266.0 %reduce-scatter.10.cloned.1.call-start = ((), (), s32[]{:S(2)}) async-start(), calls=%async_computation.15 | async-start | bytes 5242880 | tf_op jit(solution)/shard_map/reduce_scatter | solution.py:553
  560.6 238.0 %reduce-scatter.14.cloned.1.call-start = ((), (), s32[]{:S(2)}) async-start(), calls=%async_computation.17 | async-start | bytes 5242880 | tf_op jit(solution)/shard_map/reduce_scatter | solution.py:553
  574.2 236.1 %reduce-scatter.8.cloned.1.call-start = ((), (), s32[]{:S(2)}) async-start(), calls=%async_computation.14 | async-start | bytes 2359296 | tf_op jit(solution)/shard_map/reduce_scatter | solution.py:561
  574.3 69.9 %collective-permute-start.30 = (bf16[256,2048]{1,0:T(8,128)(2,1)}, bf16[256,2048]{1,0:T(8,128)(2,1)}, u32[]{:S(2)}, u32[]{:S(2)}) collective-permute-start(bf16[256,2048]{1,0:T(8,128)(2,1)} %get-tuple-element.88), channel_id=1, source_target_pairs={{0,1},{1,0},{2,3},{3,2},{4,5},{5,4},{6,7},{7,6},{8,9},{9,8},{10,11... | collective-permute-start | bytes 3145736 | tf_op jit(solution)/shard_map/ppermute | solution.py:458
  577.7 67.0 %collective-permute-start.29 = (bf16[256,2048]{1,0:T(8,128)(2,1)}, bf16[256,2048]{1,0:T(8,128)(2,1)}, u32[]{:S(2)}, u32[]{:S(2)}) collective-permute-start(bf16[256,2048]{1,0:T(8,128)(2,1)} %add_convert_fusion.6), channel_id=1, source_target_pairs={{0,2},{1,3},{2,6},{3,7},{4,0},{5,1},{6,4},{7,5},{8,10},{9,11},{10,... | collective-permute-start | bytes 3145736 | tf_op jit(solution)/shard_map/ppermute | solution.py:455
  644.8 40.3 %collective-permute-start.40 = (bf16[256,2048]{1,0:T(8,128)(2,1)}, bf16[256,2048]{1,0:T(8,128)(2,1)}, u32[]{:S(2)}, u32[]{:S(2)}) collective-permute-start(bf16[256,2048]{1,0:T(8,128)(2,1)} %slice.159), channel_id=1, source_target_pairs={{0,1},{1,0},{2,3},{3,2},{4,5},{5,4},{6,7},{7,6},{8,9},{9,8},{10,11... | collective-permute-start | bytes 3145736 | tf_op jit(solution)/shard_map/ppermute | solution.py:458
  670.2 74.0 %collective-permute-start.36 = (bf16[256,2048]{1,0:T(8,128)(2,1)}, bf16[256,2048]{1,0:T(8,128)(2,1)}, u32[]{:S(2)}, u32[]{:S(2)}) collective-permute-start(bf16[256,2048]{1,0:T(8,128)(2,1)} %get-tuple-element.96), channel_id=1, source_target_pairs={{0,1},{1,0},{2,3},{3,2},{4,5},{5,4},{6,7},{7,6},{8,9},{9,8},{10,11... | collective-permute-start | bytes 3145736 | tf_op jit(solution)/shard_map/ppermute | solution.py:458
  674.8 45.8 %all-to-all-start.3 = ((bf16[8,64,512]{2,1,0:T(8,128)(2,1)}), bf16[8,64,512]{2,1,0:T(8,128)(2,1)S(1)}, u32[]{:S(2)}, u32[]{:S(2)}) async-start(bf16[8,64,512]{2,1,0:T(8,128)(2,1)} %bitcast.20), calls=%async_computation.3 | async-start | bytes 1048576 | tf_op jit(solution)/shard_map/all_to_all | solution.py:583
  688.2 52.3 %collective-permute-start.41 = (bf16[256,2048]{1,0:T(8,128)(2,1)}, bf16[256,2048]{1,0:T(8,128)(2,1)}, u32[]{:S(2)}, u32[]{:S(2)}) collective-permute-start(bf16[256,2048]{1,0:T(8,128)(2,1)} %add_convert_fusion.1), channel_id=1, source_target_pairs={{0,2},{1,3},{2,6},{3,7},{4,0},{5,1},{6,4},{7,5},{8,10},{9,11},{10,... | collective-permute-start | bytes 3145736 | tf_op jit(solution)/shard_map/ppermute | solution.py:455
  720.6 42.3 %collective-permute-start.33 = (bf16[256,2048]{1,0:T(8,128)(2,1)}, bf16[256,2048]{1,0:T(8,128)(2,1)}, u32[]{:S(2)}, u32[]{:S(2)}) collective-permute-start(bf16[256,2048]{1,0:T(8,128)(2,1)} %add_convert_fusion.4), channel_id=1, source_target_pairs={{0,2},{1,3},{2,6},{3,7},{4,0},{5,1},{6,4},{7,5},{8,10},{9,11},{10,... | collective-permute-start | bytes 3145736 | tf_op jit(solution)/shard_map/ppermute | solution.py:455
  743.0 45.5 %collective-permute-start.43 = (bf16[256,2048]{1,0:T(8,128)(2,1)S(1)}, bf16[256,2048]{1,0:T(8,128)(2,1)S(1)}, u32[]{:S(2)}, u32[]{:S(2)}) collective-permute-start(bf16[256,2048]{1,0:T(8,128)(2,1)S(1)} %add_convert_fusion), channel_id=1, source_target_pairs={{0,2},{1,3},{2,6},{3,7},{4,0},{5,1},{6,4},{7,5},{8,10},{9,11},{10,... | collective-permute-start | bytes 3145736 | tf_op jit(solution)/shard_map/ppermute | solution.py:455
  (104 other events, 1570.9 us)
Sparse Core Ops, SparseCore 0:
  11.0 136.7 all-gather.4
  149.7 53.7 all-gather.6
  205.3 52.5 all-gather.8
  259.6 52.5 all-gather.10
  507.7 85.9 reduce-scatter.5
  596.5 63.9 reduce-scatter.11
  663.5 52.5 reduce-scatter.9
  719.1 52.5 reduce-scatter.13
  774.0 36.1 reduce-scatter.7

commit v2 on v1

v2 whole, which is shorter than its diff:
```python
import functools

import jax
import jax.numpy as jnp
import numpy as np
from jax import lax
from jax.experimental import pallas as pl
from jax.experimental.pallas import tpu as pltpu
from jax.sharding import PartitionSpec as P

H = 32
KV = 8
HD = 64
LANES = 128
VMEM_BYTES = 50 * 2**20

epsilon = 1e-05
rope_theta = 500000.0
rope_factor = 32.0
old_context = 8192.0

f32 = jnp.float32
bf16 = jnp.bfloat16

NN = (((1,), (0,)), ((), ()))
NT = (((1,), (1,)), ((), ()))
TN = (((0,), (0,)), ((), ()))


def mm(a, b, dims):
    return lax.dot_general(a, b, dims, preferred_element_type=f32)


def cost(flops, moved, transcendentals=0):
    return pl.CostEstimate(flops=flops, bytes_accessed=moved, transcendentals=transcendentals)


def params():
    return pltpu.CompilerParams(vmem_limit_bytes=VMEM_BYTES)


def frequencies(head_size):
    halves = jnp.arange(head_size // 2).astype(f32)
    plain = rope_theta ** (-2.0 * halves / head_size)
    blend = jnp.clip((old_context * plain / (2.0 * jnp.pi) - 1.0) / 3.0, 0.0, 1.0)
    return (1.0 - blend) * plain / rope_factor + blend * plain


def rope_tables(length):
    freq = jnp.tile(frequencies(HD), LANES // (HD // 2))
    angles = jnp.arange(length).astype(f32)[:, None] * freq[None, :]
    sign = jnp.where((jnp.arange(LANES) % HD) < HD // 2, -1.0, 1.0).astype(f32)
    return jnp.cos(angles), jnp.sin(angles) * sign[None, :]


def turn(x, cos, sin):
    lane = lax.broadcasted_iota(jnp.int32, x.shape, 1)
    swapped = jnp.where(
        lane % HD < HD // 2, pltpu.roll(x, LANES - HD // 2, 1), pltpu.roll(x, HD // 2, 1)
    )
    return x * cos + swapped * sin


def qkv_kernel(width, at, mine, other, gain, w, cos, sin, *refs):
    normed, queries, keys_values = refs[-3:]
    x = jnp.where(pl.program_id(0) == 0, mine[...], other[...]).astype(f32)
    inverse = lax.rsqrt(jnp.mean(x * x, axis=-1, keepdims=True) + epsilon)
    low = (x * inverse * gain[...]).astype(bf16)
    normed[...] = low
    y = mm(low, w[...], NN)
    for first in range(0, width, LANES):
        part = y[:, first : first + LANES]
        queries[:, first : first + LANES] = turn(part, cos[...], sin[...]).astype(bf16)
    part = y[:, width : width + LANES]
    lane = lax.broadcasted_iota(jnp.int32, part.shape, 1)
    keys_values[...] = jnp.where(lane < HD, turn(part, cos[...], sin[...]), part).astype(bf16)


def qkv_call(at, mine, other, gain, w, cos, sin, width, length, held):
    rows, depth = mine.shape
    cols = w.shape[1]

    def whole(shape):
        return pl.BlockSpec(shape, lambda i, at: (0, 0))

    def placed(n):
        return pl.BlockSpec((rows, n), lambda i, at: (at[i], 0))

    return pl.pallas_call(
        functools.partial(qkv_kernel, width),
        grid_spec=pltpu.PrefetchScalarGridSpec(
            num_scalar_prefetch=1,
            grid=(2,),
            in_specs=[
                whole((rows, depth)),
                whole((rows, depth)),
                whole((1, depth)),
                whole((depth, cols)),
                placed(LANES),
                placed(LANES),
            ]
            + [pl.BlockSpec(memory_space=pl.ANY)] * len(held),
            out_specs=[placed(depth), placed(width), placed(2 * HD)],
        ),
        out_shape=[
            jax.ShapeDtypeStruct((length, depth), bf16),
            jax.ShapeDtypeStruct((length, width), bf16),
            jax.ShapeDtypeStruct((length, 2 * HD), bf16),
        ],
        input_output_aliases={7 + i: i for i in range(len(held))},
        compiler_params=params(),
        cost_estimate=cost(4 * rows * depth * cols, 8 * rows * depth + 2 * depth * cols),
        name="qkv",
    )(at, mine, other, gain, w, cos, sin, *held)


def fwd_kernel(bq, share, q_ref, kv_ref, out_ref, ot_ref, lse_ref, m_s, l_s, acc_s):
    i = pl.program_id(0)
    m_s[...] = jnp.full(m_s.shape, -1e30, f32)
    l_s[...] = jnp.zeros(l_s.shape, f32)
    acc_s[...] = jnp.zeros(acc_s.shape, f32)
    qs = q_ref[...] * jnp.asarray(HD**-0.5, bf16)

    def step(j, masked):
        start = pl.multiple_of(j * bq, bq)
        kk = kv_ref[pl.ds(start, bq), :HD]
        vv = kv_ref[pl.ds(start, bq), HD:]
        for h in range(share):
            at = slice(h * HD, (h + 1) * HD)
            s = mm(kk, qs[:, at], NT)
            if masked:
                ki = lax.broadcasted_iota(jnp.int32, s.shape, 0)
                qi = lax.broadcasted_iota(jnp.int32, s.shape, 1)
                s = jnp.where(ki <= qi, s, -1e30)
            m_old = m_s[h : h + 1, :]
            m_new = jnp.maximum(m_old, jnp.max(s, axis=0, keepdims=True))
            p = jnp.exp(s - m_new)
            alpha = jnp.exp(m_old - m_new)
            l_s[h : h + 1, :] = l_s[h : h + 1, :] * alpha + jnp.sum(p, axis=0, keepdims=True)
            m_s[h : h + 1, :] = m_new
            acc_s[at, :] = acc_s[at, :] * alpha + mm(vv, p.astype(bf16), TN)

    def plain(j, carry):
        step(j, False)
        return carry

    lax.fori_loop(0, i, plain, 0)
    step(i, True)
    for h in range(share):
        at = slice(h * HD, (h + 1) * HD)
        total = l_s[h : h + 1, :]
        ot_ref[at, :] = acc_s[at, :] / total
        lse_ref[h : h + 1, :] = m_s[h : h + 1, :] + jnp.log(total)
    out_ref[...] = ot_ref[...].T.astype(bf16)


def attn_fwd(q, kv, bq=1024):
    length, width = q.shape
    share = width // HD
    rows = max(8, share)
    return pl.pallas_call(
        functools.partial(fwd_kernel, bq, share),
        grid=(length // bq,),
        in_specs=[
            pl.BlockSpec((bq, width), lambda i: (i, 0)),
            pl.BlockSpec((length, 2 * HD), lambda i: (0, 0)),
        ],
        out_specs=[
            pl.BlockSpec((bq, width), lambda i: (i, 0)),
            pl.BlockSpec((width, bq), lambda i: (0, i)),
            pl.BlockSpec((rows, bq), lambda i: (0, i)),
        ],
        out_shape=[
            jax.ShapeDtypeStruct((length, width), bf16),
            jax.ShapeDtypeStruct((width, length), f32),
            jax.ShapeDtypeStruct((rows, length), f32),
        ],
        scratch_shapes=[
            pltpu.VMEM((rows, bq), f32),
            pltpu.VMEM((rows, bq), f32),
            pltpu.VMEM((width, bq), f32),
        ],
        compiler_params=params(),
        cost_estimate=cost(8 * length * length * width, 8 * length * width, share * length * length // 2),
        name="attn_fwd",
    )(q, kv)


def bwd_kernel(
    bq, share, q_ref, kv_ref, do_ref, ot_ref, lse_ref, cos_ref, sin_ref, dq_ref, dkv_ref, dqt_s, dk_s, dv_s
):
    i = pl.program_id(0)

    @pl.when(i == 0)
    def _():
        dk_s[...] = jnp.zeros(dk_s.shape, f32)
        dv_s[...] = jnp.zeros(dv_s.shape, f32)

    dqt_s[...] = jnp.zeros(dqt_s.shape, f32)
    qs = q_ref[...] * jnp.asarray(HD**-0.5, bf16)
    do = do_ref[...]
    product = do.astype(f32).T * ot_ref[...]
    inner = [jnp.sum(product[h * HD : (h + 1) * HD], axis=0, keepdims=True) for h in range(share)]

    def step(j, masked):
        start = pl.multiple_of(j * bq, bq)
        kk = kv_ref[pl.ds(start, bq), :HD]
        vv = kv_ref[pl.ds(start, bq), HD:]
        dk = jnp.zeros((bq, HD), f32)
        dv = jnp.zeros((bq, HD), f32)
        for h in range(share):
            at = slice(h * HD, (h + 1) * HD)
            s = mm(kk, qs[:, at], NT)
            p = jnp.exp(s - lse_ref[h : h + 1, :])
            if masked:
                ki = lax.broadcasted_iota(jnp.int32, s.shape, 0)
                qi = lax.broadcasted_iota(jnp.int32, s.shape, 1)
                p = jnp.where(ki <= qi, p, 0.0)
            dp = mm(vv, do[:, at], NT)
            ds = (p * (dp - inner[h])).astype(bf16)
            dv = dv + mm(p.astype(bf16), do[:, at], NN)
            dk = dk + mm(ds, qs[:, at], NN)
            dqt_s[at, :] += mm(kk, ds, TN)
        dk_s[pl.ds(start, bq), :] += dk
        dv_s[pl.ds(start, bq), :] += dv

    def plain(j, carry):
        step(j, False)
        return carry

    lax.fori_loop(0, i, plain, 0)
    step(i, True)
    dq = (dqt_s[...] * (HD**-0.5)).T.astype(bf16).astype(f32)
    rows = pl.ds(pl.multiple_of(i * bq, bq), bq)
    for at in range(0, share * HD, LANES):
        part = dq[:, at : at + LANES]
        dq_ref[:, at : at + LANES] = turn(part, cos_ref[rows, :], -sin_ref[rows, :]).astype(bf16)

    @pl.when(i == pl.num_programs(0) - 1)
    def _():
        both = jnp.concatenate([dk_s[...], dv_s[...]], axis=1).astype(bf16).astype(f32)
        lane = lax.broadcasted_iota(jnp.int32, both.shape, 1)
        turned = turn(both, cos_ref[...], -sin_ref[...])
        dkv_ref[...] = jnp.where(lane < HD, turned, both).astype(bf16)


def attn_bwd(q, kv, do, ot, lse, cos, sin, bq=512):
    length, width = q.shape
    share = width // HD
    rows = lse.shape[0]
    return pl.pallas_call(
        functools.partial(bwd_kernel, bq, share),
        grid=(length // bq,),
        in_specs=[
            pl.BlockSpec((bq, width), lambda i: (i, 0)),
            pl.BlockSpec((length, 2 * HD), lambda i: (0, 0)),
            pl.BlockSpec((bq, width), lambda i: (i, 0)),
            pl.BlockSpec((width, bq), lambda i: (0, i)),
            pl.BlockSpec((rows, bq), lambda i: (0, i)),
            pl.BlockSpec((length, LANES), lambda i: (0, 0)),
            pl.BlockSpec((length, LANES), lambda i: (0, 0)),
        ],
        out_specs=[
            pl.BlockSpec((bq, width), lambda i: (i, 0)),
            pl.BlockSpec((length, 2 * HD), lambda i: (0, 0)),
        ],
        out_shape=[
            jax.ShapeDtypeStruct((length, width), bf16),
            jax.ShapeDtypeStruct((length, 2 * HD), bf16),
        ],
        scratch_shapes=[
            pltpu.VMEM((width, bq), f32),
            pltpu.VMEM((length, HD), f32),
            pltpu.VMEM((length, HD), f32),
        ],
        compiler_params=params(),
        cost_estimate=cost(20 * length * length * width, 16 * length * width, share * length * length // 2),
        name="attn_bwd",
    )(q, kv, do, ot, lse, cos, sin)


def out_kernel(pieces, blocks, at, *refs):
    w_mine, w_other = refs[:pieces], refs[pieces : 2 * pieces]
    mixed, x, gain, middle, normed, acc = refs[2 * pieces :]
    groups = mixed.shape[0]
    depth = x.shape[1]
    half, block, tile = depth // 2, depth // blocks, w_mine[0].shape[1]
    steps = half // tile
    u = pl.program_id(0)
    heads = jnp.concatenate([mixed[at[1 + blocks + g]] for g in range(groups)], axis=1)

    def put(ws, first):
        w = jnp.concatenate([r[...] for r in ws], axis=0)
        acc[:, pl.ds(pl.multiple_of(first, LANES), tile)] = mm(heads, w, NN)

    @pl.when(u < steps)
    def _():
        put(w_mine, at[0] * half + u * tile)

    @pl.when(u >= steps)
    def _():
        put(w_other, (1 - at[0]) * half + (u - steps) * tile)

    @pl.when(u == pl.num_programs(0) - 1)
    def _():
        squares = jnp.zeros((x.shape[0], 1), f32)
        for k in range(blocks):
            here = slice(k * block, (k + 1) * block)
            total = acc[:, pl.ds(pl.multiple_of(at[1 + k] * block, LANES), block)] + x[:, here].astype(f32)
            middle[:, here] = total
            squares = squares + jnp.sum(total * total, axis=-1, keepdims=True)
        inverse = lax.rsqrt(squares / depth + epsilon)
        normed[...] = (middle[...] * inverse * gain[...]).astype(bf16)


def halves_specs(w, tile, steps):
    mine = [pl.BlockSpec((p.shape[0], tile), lambda u, at: (0, jnp.minimum(u, steps - 1))) for p in w]
    other = [pl.BlockSpec((p.shape[0], tile), lambda u, at: (0, jnp.maximum(u - steps, 0))) for p in w]
    return mine + other


def out_call(at, w_mine, w_other, mixed, x, gain, blocks, tile=512):
    groups, rows, part = mixed.shape
    depth = x.shape[1]
    steps = depth // 2 // tile

    def whole(shape):
        return pl.BlockSpec(shape, lambda u, at: (0,) * len(shape))

    return pl.pallas_call(
        functools.partial(out_kernel, len(w_mine), blocks),
        grid_spec=pltpu.PrefetchScalarGridSpec(
            num_scalar_prefetch=1,
            grid=(2 * steps,),
            in_specs=halves_specs(w_mine, tile, steps)
            + [whole(mixed.shape), whole(x.shape), whole((1, depth))],
            out_specs=[whole((rows, depth)), whole((rows, depth))],
            scratch_shapes=[pltpu.VMEM((rows, depth), f32)],
        ),
        out_shape=[
            jax.ShapeDtypeStruct((rows, depth), f32),
            jax.ShapeDtypeStruct((rows, depth), bf16),
        ],
        compiler_params=params(),
        cost_estimate=cost(2 * groups * part * rows * depth, 2 * groups * part * depth + 8 * rows * depth),
        name="out_norm",
    )(at, *w_mine, *w_other, mixed, x, gain)


def ffn_kernel(pieces, *refs):
    x_mine, x_other, c_mine, c_other = refs[:4]
    weights = [refs[4 + i * pieces : 4 + (i + 1) * pieces] for i in range(3)]
    xs, cs, hidden, d_gate, d_up, back_mine, down_mine, others, back, down = refs[-10:]
    u = pl.program_id(0)
    w_gate, w_up, w_down = (jnp.concatenate([r[...] for r in w], axis=0) for w in weights)
    x = jnp.concatenate([x_mine[...], x_other[...]], axis=0)
    c = jnp.concatenate([c_mine[...], c_other[...]], axis=0)
    gate = mm(x, w_gate, NN)
    up = mm(x, w_up, NN)
    grad = mm(c, w_down, NN)
    sig = jax.nn.sigmoid(gate)
    silu = gate * sig
    act = (silu * up).astype(bf16)
    dg = (grad * up * sig * (1.0 + gate * (1.0 - sig))).astype(bf16)
    du = (grad * silu).astype(bf16)
    hidden[...] = act
    d_gate[...] = dg
    d_up[...] = du

    @pl.when(u == 0)
    def _():
        xs[...] = x
        cs[...] = c
        back[...] = mm(dg, w_gate, NT) + mm(du, w_up, NT)
        down[...] = mm(act, w_down, NT)

    @pl.when(u > 0)
    def _():
        back[...] += mm(dg, w_gate, NT) + mm(du, w_up, NT)
        down[...] += mm(act, w_down, NT)

    @pl.when(u == pl.num_programs(0) - 1)
    def _():
        rows = back_mine.shape[0]
        back_mine[...] = back[:rows].astype(bf16)
        down_mine[...] = down[:rows].astype(bf16)
        others[0] = back[rows:].astype(bf16)
        others[1] = down[rows:].astype(bf16)


def ffn_call(s, count, x_mine, x_other, c_mine, c_other, w_gate, w_up, w_down, held, tile=256):
    rows, depth = x_mine.shape
    units = w_gate[0].shape[1]
    block = pl.BlockSpec((rows, depth), lambda u: (0, 0))
    weights = [pl.BlockSpec((p.shape[0], tile), lambda u: (0, u)) for p in w_gate]
    full = pl.BlockSpec((2 * rows, depth), lambda u: (s, 0))
    act = pl.BlockSpec((2 * rows, tile), lambda u: (s, u))
    full_shape = jax.ShapeDtypeStruct((2 * rows * count, depth), bf16)
    act_shape = jax.ShapeDtypeStruct((2 * rows * count, units), bf16)
    row_shape = jax.ShapeDtypeStruct((rows, depth), bf16)
    first = 4 + 3 * len(w_gate)
    return pl.pallas_call(
        functools.partial(ffn_kernel, len(w_gate)),
        grid=(units // tile,),
        in_specs=[block] * 4 + weights * 3 + [pl.BlockSpec(memory_space=pl.ANY)] * len(held),
        out_specs=[full] * 2 + [act] * 3 + [block] * 2 + [pl.BlockSpec((2, rows, depth), lambda u: (0, 0, 0))],
        out_shape=[full_shape] * 2
        + [act_shape] * 3
        + [row_shape] * 2
        + [jax.ShapeDtypeStruct((2, rows, depth), bf16)],
        scratch_shapes=[pltpu.VMEM((2 * rows, depth), f32)] * 2,
        input_output_aliases={first + i: i for i in range(len(held))},
        compiler_params=params(),
        cost_estimate=cost(24 * rows * depth * units, 6 * depth * units + 20 * rows * depth + 12 * rows * units),
        name="ffn",
    )(x_mine, x_other, c_mine, c_other, *w_gate, *w_up, *w_down, *held)


def mid_kernel(pieces, blocks, at, *refs):
    w_mine, w_other = refs[:pieces], refs[pieces : 2 * pieces]
    ring, own, swapped, middle, cot, gain, d_middle, branch, d_gain, d_mixed, acc = refs[2 * pieces :]
    rows, depth = middle.shape
    groups, _, part = d_mixed.shape
    half, block, tile = depth // 2, depth // blocks, w_mine[0].shape[1]
    steps = half // tile
    u = pl.program_id(0)

    @pl.when(u == 0)
    def _():
        grad = ring[...].astype(f32) + (own[...].astype(f32) + swapped[...].astype(f32))
        m = middle[...]
        inverse = lax.rsqrt(jnp.mean(m * m, axis=-1, keepdims=True) + epsilon)
        scaled = grad * gain[...]
        slope = jnp.mean(m * scaled, axis=-1, keepdims=True) * (inverse * inverse * inverse)
        total = cot[...].astype(f32) + inverse * scaled - m * slope
        d_middle[...] = total
        for k in range(blocks):
            place = pl.ds(pl.multiple_of(at[1 + k] * block, LANES), block)
            branch[:, place] = total[:, k * block : (k + 1) * block].astype(bf16)
        d_gain[...] = jnp.sum(grad * m * inverse, axis=0, keepdims=True)
        acc[...] = jnp.zeros(acc.shape, f32)

    def add(ws, first):
        w = jnp.concatenate([r[...] for r in ws], axis=0)
        acc[...] += mm(branch[:, pl.ds(pl.multiple_of(first, LANES), tile)], w, NT)

    @pl.when(u < steps)
    def _():
        add(w_mine, at[0] * half + u * tile)

    @pl.when(u >= steps)
    def _():
        add(w_other, (1 - at[0]) * half + (u - steps) * tile)

    @pl.when(u == pl.num_programs(0) - 1)
    def _():
        for g in range(groups):
            d_mixed[at[1 + blocks + g]] = acc[:, g * part : (g + 1) * part].astype(bf16)


def mid_call(at, w_mine, w_other, ring, own, swapped, middle, cot, gain, part, blocks, tile=512):
    rows, depth = middle.shape
    heads = sum(p.shape[0] for p in w_mine)
    groups = heads // part
    steps = depth // 2 // tile

    def whole(shape):
        return pl.BlockSpec(shape, lambda u, at: (0,) * len(shape))

    block, line = whole((rows, depth)), whole((1, depth))
    return pl.pallas_call(
        functools.partial(mid_kernel, len(w_mine), blocks),
        grid_spec=pltpu.PrefetchScalarGridSpec(
            num_scalar_prefetch=1,
            grid=(2 * steps,),
            in_specs=halves_specs(w_mine, tile, steps) + [block] * 5 + [line],
            out_specs=[block, block, line, whole((groups, rows, part))],
            scratch_shapes=[pltpu.VMEM((rows, heads), f32)],
        ),
        out_shape=[
            jax.ShapeDtypeStruct((rows, depth), f32),
            jax.ShapeDtypeStruct((rows, depth), bf16),
            jax.ShapeDtypeStruct((1, depth), f32),
            jax.ShapeDtypeStruct((groups, rows, part), bf16),
        ],
        compiler_params=params(),
        cost_estimate=cost(2 * heads * rows * depth, 2 * heads * depth + 16 * rows * depth),
        name="mid",
    )(at, *w_mine, *w_other, ring, own, swapped, middle, cot, gain)


def first_kernel(blocks, at, ring, own, swapped, x_ref, d_middle, gain, out):
    depth = x_ref.shape[1]
    block = depth // blocks
    grad = ring[...].astype(f32) + (own[...].astype(f32) + swapped[...].astype(f32))
    x = x_ref[...].astype(f32)
    inverse = lax.rsqrt(jnp.mean(x * x, axis=-1, keepdims=True) + epsilon)
    scaled = grad * gain[...]
    slope = jnp.mean(x * scaled, axis=-1, keepdims=True) * (inverse * inverse * inverse)
    total = d_middle[...] + inverse * scaled - x * slope
    for k in range(blocks):
        place = pl.ds(pl.multiple_of(at[1 + k] * block, LANES), block)
        out[:, place] = total[:, k * block : (k + 1) * block].astype(bf16)


def first_call(at, ring, own, swapped, x, d_middle, gain, blocks, tile=64):
    rows, depth = x.shape
    block = pl.BlockSpec((tile, depth), lambda i, at: (i, 0))
    return pl.pallas_call(
        functools.partial(first_kernel, blocks),
        grid_spec=pltpu.PrefetchScalarGridSpec(
            num_scalar_prefetch=1,
            grid=(rows // tile,),
            in_specs=[block] * 5 + [pl.BlockSpec((1, depth), lambda i, at: (0, 0))],
            out_specs=block,
        ),
        out_shape=jax.ShapeDtypeStruct((rows, depth), bf16),
        compiler_params=params(),
        cost_estimate=cost(20 * rows * depth, 14 * rows * depth),
        name="first_norm_back",
    )(at, ring, own, swapped, x, d_middle, gain)


def after(value, *others):
    return lax.optimization_barrier((value,) + others)[0]


def shards(
    tokens, gain_attn, w_query, w_key, w_value, w_out, gain_mlp, w_gate, w_up, w_down, cotangent
):
    groups = lax.axis_size("seq")
    dp_count = lax.axis_size("dp")
    seq_count, piece, depth = tokens.shape
    assert seq_count == 1 and groups >= KV and groups % 2 == 0 and groups % dp_count == 0
    assert dp_count & (dp_count - 1) == 0
    length = piece * groups
    width = H // groups * HD
    repeat = groups // KV
    own_rows = w_query.shape[0]
    half = depth // 2
    block = depth // dp_count

    chips = groups // 2
    middle_chip = chips // 2
    order = list(range(middle_chip)) + list(range(chips - 1, middle_chip - 1, -1))
    place = np.argsort(order)
    follow = [order[(place[c] + 1) % chips] for c in range(chips)]
    ring = [(2 * c + k, 2 * follow[c] + k) for c in range(chips) for k in range(2)]
    swap = [(i, i ^ 1) for i in range(groups)]

    seq_at = lax.axis_index("seq")
    dp_at = lax.axis_index("dp")
    core_at = seq_at % 2
    ring_at = jnp.asarray(place, jnp.int32)[seq_at // 2]
    chunk = jnp.asarray(order, jnp.int32)[(ring_at + chips - jnp.arange(chips)) % chips]
    pair_at = 2 * chunk[:, None] + jnp.stack([core_at, 1 - core_at])[None, :]
    dp_order = dp_at ^ jnp.arange(dp_count)
    group_order = (dp_order[:, None] * (groups // dp_count) + jnp.arange(groups // dp_count)).reshape(-1)
    at = jnp.concatenate([core_at[None], dp_order, group_order]).astype(jnp.int32)

    def step_ring(x):
        return lax.ppermute(x, "seq", ring)

    def step_swap(x):
        return lax.ppermute(x, "seq", swap)

    def step_dp(x, k):
        return lax.ppermute(x, "dp", [(i, i ^ k) for i in range(dp_count)])

    def rows_at(x, start, count):
        return lax.dynamic_slice_in_dim(x, start, count, 0)

    def cols_at(x, start, count):
        return lax.dynamic_slice_in_dim(x, start, count, 1)

    def reorder(x):
        return jnp.concatenate([cols_at(x, dp_order[k] * block, block) for k in range(dp_count)], axis=1)

    def gather_dp(x):
        if dp_count != 4:
            return [x] + [step_dp(x, k) for k in range(1, dp_count)]
        cut = x.shape[0] // 2
        one, two = step_dp(x, 1), step_dp(x, 2)
        return [x, one, two, step_dp(one[:cut], 2), step_dp(two[cut:], 1)]

    def scatter_dp(parts):
        return [step_dp(parts[k], k) for k in range(1, dp_count)]

    def pair_sides(own, got):
        return jnp.where(core_at == 0, jnp.concatenate([own, got]), jnp.concatenate([got, own]))

    x_own = reorder(tokens.reshape(piece, depth))
    cot_own = reorder(cotangent.reshape(piece, depth))

    with jax.named_scope("tokens_ring"):
        x_mine, x_other = [x_own], [step_swap(x_own)]
        for _ in range(chips - 1):
            x_mine.append(step_ring(x_mine[-1]))
            x_other.append(step_swap(x_mine[-1]))

    def per_group(w):
        return jnp.repeat(w.reshape(own_rows, KV, HD), repeat, axis=1)

    with jax.named_scope("projection_columns"):
        gains_own = jnp.stack([gain_attn, gain_mlp], axis=-1)
        gains_own = jnp.pad(gains_own, ((0, 0), (0, LANES - 2)))
        gains_own = jnp.broadcast_to(gains_own[:, None, :], (own_rows, groups, LANES))
        own_cols = jnp.concatenate(
            [w_query.reshape(own_rows, groups, width), per_group(w_key), per_group(w_value), gains_own],
            axis=-1,
        )
        cols = own_cols.shape[-1]
        dp_rows = groups * own_rows
        cols_dp = lax.all_to_all(jnp.transpose(own_cols, (1, 0, 2)), "seq", 0, 0, tiled=True)
        cols_dp = cols_dp.reshape(dp_rows, cols)
        cols_all = jnp.concatenate([cols_dp] + [step_dp(cols_dp, k) for k in range(1, dp_count)], axis=0)
        w_qkv = cols_all[:, : width + 2 * HD]
        gains = jnp.transpose(cols_all[:, width + 2 * HD : width + 2 * HD + 2].astype(f32))
        gain_one, gain_two = gains[:1], gains[1:]

    with jax.named_scope("out_weight"):
        keep = cols_at(w_out, core_at * half, half)
        give = cols_at(w_out, (1 - core_at) * half, half)
        chip_rows = [pair_sides(keep, step_swap(give))]
        for _ in range(chips - 1):
            chip_rows.append(step_ring(chip_rows[-1]))
        out_rows = jnp.zeros((dp_rows, half), bf16)
        for s in range(chips):
            out_rows = lax.dynamic_update_slice_in_dim(out_rows, chip_rows[s], chunk[s] * 2 * own_rows, 0)

    with jax.named_scope("gate_weight"):
        gate_full = gather_dp(w_gate)
    with jax.named_scope("out_weight"):
        out_mine = gather_dp(after(out_rows, gate_full[-1]))
        out_other = [step_swap(p) for p in out_mine]
    with jax.named_scope("up_weight"):
        up_full = gather_dp(after(w_up, out_mine[-1]))
    with jax.named_scope("down_weight"):
        down_full = gather_dp(after(w_down, up_full[-1]))

    cos, sin = rope_tables(length)

    held = ()
    for s in range(chips):
        held = qkv_call(
            pair_at[s], x_mine[s], x_other[s], gain_one, w_qkv, cos, sin, width, length, held
        )
    normed, queries, keys_values = held

    with jax.named_scope("cotangent_ring"):
        c_mine = [cot_own, step_ring(after(cot_own, x_mine[-1]))]
        c_other = [step_swap(c) for c in c_mine]

    head_out, out_t, lse = attn_fwd(queries, keys_values)
    with jax.named_scope("mixed"):
        mixed = lax.all_to_all(head_out.reshape(groups, piece, width), "seq", 0, 0, tiled=True)
    middle, normed_two = out_call(at, out_mine, out_other, mixed, x_own, gain_two, dp_count)

    n_mine, n_other, ffn, held = [], [], [], ()
    for s in range(chips):
        with jax.named_scope("normed_ring"):
            n_mine.append(step_ring(n_mine[-1]) if s else normed_two)
            n_other.append(step_swap(n_mine[-1]))
        if s >= 2:
            with jax.named_scope("cotangent_ring"):
                c_mine.append(step_ring(after(c_mine[-1], mixed if s == 2 else n_mine[s - 2])))
                c_other.append(step_swap(c_mine[-1]))
        out = ffn_call(
            s, chips, n_mine[s], n_other[s], c_mine[s], c_other[s], gate_full, up_full, down_full, held
        )
        held, rest = out[:5], out[5:]
        with jax.named_scope("feed_forward_pair"):
            swapped = step_swap(rest[2])
        ffn.append((rest[0], rest[1], swapped[0], swapped[1]))
    n_all, c_all, hidden, d_gate, d_up = held

    def add(*parts):
        total = parts[0].astype(f32)
        for p in parts[1:]:
            total = total + p.astype(f32)
        return total

    def weight_grad(rows, grads):
        return [
            mm(rows[:, k * block : (k + 1) * block], grads, TN).astype(bf16) for k in range(dp_count)
        ]

    with jax.named_scope("back_ring"):
        acc = add(ffn[1][0], ffn[1][2]).astype(bf16)
        for s in range(2, chips):
            acc = add(step_ring(acc), ffn[s][0], ffn[s][2]).astype(bf16)
        back_got = step_ring(acc)

    with jax.named_scope("gate_grad"):
        gate_parts = weight_grad(n_all, d_gate)
        gate_sent = scatter_dp(gate_parts)
    with jax.named_scope("up_grad"):
        up_parts = weight_grad(n_all, d_up)
        up_sent = scatter_dp([after(p, gate_sent[-1]) for p in up_parts])
    back_got = after(back_got, gate_parts[-1], up_parts[-1])

    d_middle, branch, d_gain_two, d_mixed = mid_call(
        at, out_mine, out_other, back_got, ffn[0][0], ffn[0][2], middle, cot_own, gain_two, width, dp_count
    )
    with jax.named_scope("d_mixed"):
        d_heads = lax.all_to_all(d_mixed, "seq", 0, 0, tiled=True).reshape(length, width)

    with jax.named_scope("out_grad"):

        def out_part(start):
            g = jnp.einsum("gnh,nd->ghd", mixed, cols_at(branch, start, half), preferred_element_type=f32)
            return g.reshape(groups * width, half).astype(bf16)

        out_theirs = out_part((1 - core_at) * half)
        out_theirs_sent = step_swap(out_theirs)
        out_own = out_part(core_at * half)
    with jax.named_scope("down_grad"):
        down_rows, _ = lax.optimization_barrier((c_all, branch))
        down_parts = weight_grad(down_rows, hidden)
        down_sent = scatter_dp([after(p, up_sent[-1]) for p in down_parts])

    with jax.named_scope("down_ring"):
        acc = add(after(ffn[1][1], back_got), ffn[1][3]).astype(bf16)
        down_two = step_ring(acc)

    d_heads = after(d_heads, down_parts[-1], out_own)

    d_queries, d_kv = attn_bwd(queries, keys_values, d_heads, out_t, lse, cos, sin)

    with jax.named_scope("down_ring"):
        for s in range(2, chips):
            acc = add(after(down_two, d_heads if s == 2 else d_kv), ffn[s][1], ffn[s][3]).astype(bf16)
            down_two = step_ring(acc)

    with jax.named_scope("out_grad"):
        out_sum = add(out_own, after(out_theirs_sent, d_kv)).astype(bf16)
        out_parts = [rows_at(out_sum, dp_order[k] * dp_rows, dp_rows) for k in range(dp_count)]
        out_sent = scatter_dp([after(p, down_sent[-1]) for p in out_parts])

    with jax.named_scope("first_ring"):
        def d_normed(s, side):
            d_q = rows_at(d_queries, pair_at[s, side] * piece, piece)
            d_k = rows_at(d_kv, pair_at[s, side] * piece, piece)
            return mm(jnp.concatenate([d_q, d_k], axis=1), w_qkv, NT).astype(bf16)

        steps = list(range(1, chips)) + [0]
        theirs = {s: step_swap(d_normed(s, 1)) for s in steps}
        own = {s: d_normed(s, 0) for s in steps}
        acc = add(own[1], theirs[1]).astype(bf16)
        for s in range(2, chips):
            acc = add(step_ring(acc), own[s], theirs[s]).astype(bf16)
        first_last = acc
        first_got = step_ring(acc)

    with jax.named_scope("projection_grads"):
        d_qkv = jnp.concatenate([d_queries, d_kv], axis=1)
        grad_cols = mm(normed, d_qkv, TN).astype(bf16)
        high = d_gain_two.astype(bf16)
        rest = (d_gain_two - high.astype(f32)).astype(bf16)
        extra = jnp.pad(jnp.transpose(jnp.concatenate([high, rest], axis=0)), ((0, 0), (0, LANES - 2)))
        grad_cols = jnp.concatenate([grad_cols, extra], axis=1)
        col_parts = [grad_cols[k * block : (k + 1) * block] for k in range(dp_count)]
        total = add(col_parts[0], *scatter_dp(col_parts)).astype(bf16)
        dealt = lax.all_to_all(total.reshape(groups, own_rows, cols), "seq", 0, 0, tiled=True)

    with jax.named_scope("feed_forward_grads"):
        gate_sent, up_sent, down_sent = lax.optimization_barrier((gate_sent, up_sent, down_sent, first_last))[:3]
        grad_gate = add(gate_parts[0], *gate_sent)
        grad_up = add(up_parts[0], *up_sent)
        grad_down = add(down_parts[0], *down_sent)

    with jax.named_scope("out_grad"):
        out_dp = add(out_parts[0], *out_sent).astype(bf16)

        def chip_part(s):
            return rows_at(out_dp, chunk[s] * 2 * own_rows, 2 * own_rows)

        acc = chip_part(1)
        for s in range(2, chips):
            acc = add(step_ring(acc), chip_part(s)).astype(bf16)
        acc = add(step_ring(acc), chip_part(0))
        out_keep = rows_at(acc, core_at * own_rows, own_rows)
        out_give = rows_at(acc, (1 - core_at) * own_rows, own_rows).astype(bf16)
        out_take = step_swap(out_give).astype(f32)
        grad_out = jnp.where(
            core_at == 0,
            jnp.concatenate([out_keep, out_take], axis=1),
            jnp.concatenate([out_take, out_keep], axis=1),
        )

    grad_tokens = first_call(at, first_got, own[0], theirs[0], x_own, d_middle, gain_one, dp_count)
    block_out = reorder((middle + add(down_two, ffn[0][1], ffn[0][3])).astype(bf16))

    def join(x):
        return jnp.transpose(x, (1, 0, 2)).reshape(own_rows, -1)

    def fold(x):
        return join(jnp.sum(x.reshape(KV, repeat, own_rows, HD), axis=1))

    dealt = dealt.astype(f32)
    grad_query = join(dealt[:, :, :width])
    grad_key = fold(dealt[:, :, width : width + HD])
    grad_value = fold(dealt[:, :, width + HD : width + 2 * HD])
    grad_gain_two = jnp.sum(dealt[:, :, width + 2 * HD : width + 2 * HD + 2], axis=(0, 2))

    def against(w, grad):
        return jnp.sum(w.astype(f32) * grad, axis=1)

    grad_gain_one = against(w_query, grad_query) + against(w_key, grad_key) + against(w_value, grad_value)
    grad_gain_one = grad_gain_one / gain_attn.astype(f32)

    return (
        block_out.reshape(1, piece, depth),
        grad_tokens.reshape(1, piece, depth),
        grad_gain_one,
        grad_query,
        grad_key,
        grad_value,
        grad_out,
        grad_gain_two,
        grad_gate,
        grad_up,
        grad_down,
    )


def solution(mesh):
    rows = P("dp", "seq", None)
    both = P(("dp", "seq"))
    flat = P(("dp", "seq"), None)
    tiles = P("dp", "seq")
    in_specs = (rows, both, flat, flat, flat, flat, both, tiles, tiles, tiles, rows)
    out_specs = (rows, rows, both, flat, flat, flat, flat, both, tiles, tiles, tiles)
    return jax.shard_map(shards, mesh=mesh, in_specs=in_specs, out_specs=out_specs, check_vma=False)
```

time: 828 us -> 876 us (1.058)
  starting transfers between devices: 53.4 us -> 102 us
  matrix products: 53 us -> 87.2 us
  local copies, waits for them, and re-layouts: 63.3 us -> 45.4 us
  other arithmetic: 49.8 us -> 35.7 us
    ppermute x6 -> x34, waiting for transfers between devices: 44.1 us -> 231 us  [step_dp(): return lax.ppermute(x, 'dp', [(i, i ^ k) for i in range(dp_count)])]
    ppermute x18 -> x24, waiting for transfers between devices: 216 us -> 127 us  [step_ring(): return lax.ppermute(x, 'seq', ring)]
    all_gather x4 -> x0, waiting for transfers between devices: 60.5 us -> none  [the longest x1 54.3 us: shards(): down_full = lax.all_gather(w_down, 'dp', axis=0, tiled=True)]
    ppermute x6 -> x34, starting transfers between devices: 7.07 us -> 42.1 us  [step_dp(): return lax.ppermute(x, 'dp', [(i, i ^ k) for i in range(dp_count)])]
    dot_general x8 -> x21, matrix products: 47.3 us -> 78.2 us  [mm(): return lax.dot_general(a, b, dims, preferred_element_type=f32)]
    unnamed x175 -> x147, local copies, waits for them, and re-layouts: 41.8 us -> 13.1 us
    all_to_all x1, waiting for transfers between devices: 25.1 us -> 0.01 us  [shards(): lax.all_to_all(head_out.reshape(groups, piece, width), 'seq', 0, 0, tiled...]
    all_to_all x1, waiting for transfers between devices: 22.9 us -> 0.01 us  [shards(): lax.all_to_all(jnp.transpose(own_cols, (1, 0, 2)), 'seq', 0, 0, tiled=True)]
  transfers between devices with their start and end apart: 61 -> 90, of which waited for: 21 -> 34; matrix products, arithmetic and copies ran while one was open for 16% -> 17% of each run, Pallas kernels for 22% -> 22%
where the time goes in v2:
time: 876 us; the launch traced here: 866 us
  waiting for transfers between devices  389 us (44%)
  Pallas kernels  195 us (22%)
  starting transfers between devices  102 us (12%)
  matrix products  87.2 us (10%)
  local copies, waits for them, and re-layouts  45.4 us (5%)
  other arithmetic  35.7 us (4%)
  between operations  13 us (1%)
    ppermute x34, waiting for transfers between devices, step_dp(): return lax.ppermute(x, 'dp', [(i, i ^ k) for i in range(dp_count)])  231 us
    ppermute x24, waiting for transfers between devices, step_ring(): return lax.ppermute(x, 'seq', ring)  127 us
    pallas_call x4, Pallas kernels, ffn_call(): pl.pallas_call(functools.partial(ffn_kernel, len(w_gate)), grid=(units //...  90.7 us
    dot_general x21, matrix products, mm(): return lax.dot_general(a, b, dims, preferred_element_type=f32)  78.2 us
    ppermute x34, starting transfers between devices, step_dp(): return lax.ppermute(x, 'dp', [(i, i ^ k) for i in range(dp_count)])  42.1 us
    ppermute x24, starting transfers between devices, step_ring(): return lax.ppermute(x, 'seq', ring)  37.1 us
    pallas_call x1, Pallas kernels, attn_bwd(): pl.pallas_call(functools.partial(bwd_kernel, bq, share), grid=(length //...  33.5 us
    all_to_all x1, waiting for transfers between devices, shards(): lax.all_to_all(d_mixed, 'seq', 0, 0, tiled=True).reshape(length, width)  25.1 us
  transfers between devices with their start and end apart: 90, of which 34 were waited for; matrix products, arithmetic and copies ran while one was open for 17% of the time, Pallas kernels for 22%

profile of v2, /device:TPU:0, one launch (start us, length us, event | category | flops | bytes accessed | tf_op | source)
XLA Modules:
  0.0 866.4 jit_solution(14429617786882006305)
XLA Ops:
  20.2 15.4 %collective-permute-done.15.mine = bf16[256,2048]{1,0:T(8,128)(2,1)} collective-permute-done((bf16[256,2048]{1,0:T(8,128)(2,1)S(1)}, bf16[256,2048]{1,0:T(8,128)(2,1)}, u32[]{:S(2)}, u32[]{:S(2)}) %collective-permute-start.15) | collective-permute-done | bytes 1048608 | tf_op jit(solution)/shard_map/tokens_ring/ppermute | solution.py:562
  44.8 28.5 %collective-permute-done.1 = bf16[128,1024]{1,0:T(8,128)(2,1)S(1)} collective-permute-done((bf16[128,1024]{1,0:T(8,128)(2,1)S(1)}, bf16[128,1024]{1,0:T(8,128)(2,1)S(1)}, u32[]{:S(2)}, u32[]{:S(2)}) %collective-permute-start.1) | collective-permute-done | bytes 262176 | tf_op jit(solution)/shard_map/out_weight/ppermute | solution.py:562
  105.6 31.1 %collective-permute-done.20 = bf16[512,512]{0,1:T(8,128)(2,1)S(1)} collective-permute-done((bf16[512,512]{0,1:T(8,128)(2,1)S(1)}, bf16[512,512]{0,1:T(8,128)(2,1)S(1)}, u32[]{:S(2)}, u32[]{:S(2)}) %collective-permute-start.20) | collective-permute-done | bytes 524320 | tf_op jit(solution)/shard_map/projection_columns/ppermute | solution.py:568
  153.1 6.3 qkv.5
  181.6 20.0 %attn_fwd.1 = (bf16[2048,256]{1,0:T(8,128)(2,1)}, f32[256,2048]{1,0:T(8,128)}, f32[8,2048]{1,0:T(8,128)S(1)}) custom-call(bf16[2048,256]{1,0:T(8,128)(2,1)S(1)} %get-tuple-element.107.q_ref, bf16[2048,128]{1,0:T(8,128)(2,1)S(1)} %get-tuple-element.108.kv_ref), custom_call_target="tpu_custom_call" | custom-call | flops 8589934592 | bytes 4194304 | tf_op jit(solution)/shard_map/attn_fwd/pallas_call | solution.py:161
  208.1 13.7 %collective-permute-done.8.refs_3_ = bf16[256,1024]{1,0:T(8,128)(2,1)S(1)} collective-permute-done((bf16[256,1024]{1,0:T(8,128)(2,1)S(1)}, bf16[256,1024]{1,0:T(8,128)(2,1)S(1)}, u32[]{:S(2)}, u32[]{:S(2)}) %collective-permute-start.8) | collective-permute-done | bytes 524320 | tf_op jit(solution)/shard_map/out_weight/ppermute | solution.py:568
  229.1 8.6 collective-permute-done.34.refs_13_
  240.7 9.2 %out_norm.1 = (f32[256,2048]{1,0:T(8,128)}, bf16[256,2048]{1,0:T(8,128)(2,1)}) custom-call(s32[13]{0:T(128)S(1)} %pad_add_fusion.at, bf16[512,1024]{1,0:T(8,128)(2,1)} %constant_dynamic-update-slice_fusion.refs_0_, bf16[512,1024]{1,0:T(8,128)(2,1)} %collective-permute-done.6.refs_1_, bf16[512,1024]{1,0:T(8,128)(2,1)} %collective-permute-done.7.refs_2_, ...), custom_call_target="tpu_custom_call" | custom-call | flops 2147483648 | bytes 12582912 | tf_op jit(solution)/shard_map/out_norm/pallas_call | solution.py:330
  261.9 20.8 %collective-permute-done.31.refs_10_ = bf16[512,1024]{1,0:T(8,128)(2,1)} collective-permute-done((bf16[512,1024]{1,0:T(8,128)(2,1)}, bf16[512,1024]{1,0:T(8,128)(2,1)}, u32[]{:S(2)}, u32[]{:S(2)}) %collective-permute-start.31) | collective-permute-done | bytes 1048608 | tf_op jit(solution)/shard_map/up_weight/ppermute | solution.py:568
  284.4 20.4 %collective-permute-done.35.refs_15_ = bf16[512,1024]{1,0:T(8,128)(2,1)} collective-permute-done((bf16[512,1024]{1,0:T(8,128)(2,1)}, bf16[512,1024]{1,0:T(8,128)(2,1)}, u32[]{:S(2)}, u32[]{:S(2)}) %collective-permute-start.35) | collective-permute-done | bytes 1048608 | tf_op jit(solution)/shard_map/down_weight/ppermute | solution.py:568
  325.5 11.2 %collective-permute-done.33.refs_12_ = bf16[256,1024]{1,0:T(8,128)(2,1)} collective-permute-done((bf16[256,1024]{1,0:T(8,128)(2,1)}, bf16[256,1024]{1,0:T(8,128)(2,1)}, u32[]{:S(2)}, u32[]{:S(2)}) %collective-permute-start.33) | collective-permute-done | bytes 524320 | tf_op jit(solution)/shard_map/up_weight/ppermute | solution.py:568
  338.4 9.1 %collective-permute-done.37.refs_17_ = bf16[256,1024]{1,0:T(8,128)(2,1)} collective-permute-done((bf16[256,1024]{1,0:T(8,128)(2,1)}, bf16[256,1024]{1,0:T(8,128)(2,1)}, u32[]{:S(2)}, u32[]{:S(2)}) %collective-permute-start.37) | collective-permute-done | bytes 524320 | tf_op jit(solution)/shard_map/down_weight/ppermute | solution.py:568
  351.2 22.6 %ffn.4 = (bf16[2048,2048]{1,0:T(8,128)(2,1)}, bf16[2048,2048]{1,0:T(8,128)(2,1)}, bf16[2048,1024]{1,0:T(8,128)(2,1)}, bf16[2048,1024]{1,0:T(8,128)(2,1)}, bf16[2...) custom-call(bf16[256,2048]{1,0:T(8,128)(2,1)} %get-tuple-element.111, ...), custom_call_target="tpu_custom_call" | custom-call | flops 12884901888 | bytes 26214400 | tf_op jit(solution)/shard_map/ffn/pallas_call | solution.py:402
  374.5 10.1 %collective-permute-done.43.refs_0_ = bf16[256,2048]{1,0:T(8,128)(2,1)S(1)} collective-permute-done((bf16[256,2048]{1,0:T(8,128)(2,1)}, bf16[256,2048]{1,0:T(8,128)(2,1)S(1)}, u32[]{:S(2)}, u32[]{:S(2)}) %collective-permute-start.43) | collective-permute-done | bytes 1048608 | tf_op jit(solution)/shard_map/normed_ring/ppermute | solution.py:562
  385.3 22.8 %ffn.5 = (bf16[2048,2048]{1,0:T(8,128)(2,1)}, bf16[2048,2048]{1,0:T(8,128)(2,1)}, bf16[2048,1024]{1,0:T(8,128)(2,1)}, bf16[2048,1024]{1,0:T(8,128)(2,1)}, bf16[2...) custom-call(bf16[256,2048]{1,0:T(8,128)(2,1)} %copy-done.58, ...), custom_call_target="tpu_custom_call", output_to_operand_aliasing={{0}: (19, {}), {1}: (20, {}), {2}: (21, {}), {3}: (22, {}),... | custom-call | flops 12884901888 | bytes 26214400 | tf_op jit(solution)/shard_map/ffn/pallas_call | solution.py:402
  409.7 22.4 %ffn.6 = (bf16[2048,2048]{1,0:T(8,128)(2,1)}, bf16[2048,2048]{1,0:T(8,128)(2,1)}, bf16[2048,1024]{1,0:T(8,128)(2,1)}, bf16[2048,1024]{1,0:T(8,128)(2,1)}, bf16[2...) custom-call(bf16[256,2048]{1,0:T(8,128)(2,1)} %copy-done.60, ...), custom_call_target="tpu_custom_call", output_to_operand_aliasing={{0}: (19, {}), {1}: (20, {}), {2}: (21, {}), {3}: (22, {}),... | custom-call | flops 12884901888 | bytes 26214400 | tf_op jit(solution)/shard_map/ffn/pallas_call | solution.py:402
  433.6 22.9 %ffn.7 = (bf16[2048,2048]{1,0:T(8,128)(2,1)}, bf16[2048,2048]{1,0:T(8,128)(2,1)}, bf16[2048,1024]{1,0:T(8,128)(2,1)}, bf16[2048,1024]{1,0:T(8,128)(2,1)}, bf16[2...) custom-call(bf16[256,2048]{1,0:T(8,128)(2,1)} %collective-permute-do, ...), custom_call_target="tpu_custom_call", output_to_operand_aliasing={{0}: (19, {}), {1}: (20, {}), {2}: (21, {}), {3}: (22, {}),... | custom-call | flops 12884901888 | bytes 26214400 | tf_op jit(solution)/shard_map/ffn/pallas_call | solution.py:402
  471.0 12.6 %collective-permute-done.42 = bf16[256,2048]{1,0:T(8,128)(2,1)S(1)} collective-permute-done((bf16[256,2048]{1,0:T(8,128)(2,1)S(1)}, bf16[256,2048]{1,0:T(8,128)(2,1)S(1)}, u32[]{:S(2)}, u32[]{:S(2)}) %collective-permute-start.42) | collective-permute-done | bytes 1048608 | tf_op jit(solution)/shard_map/back_ring/ppermute | solution.py:562
  494.1 16.2 %collective-permute-done.48 = bf16[256,2048]{1,0:T(8,128)(2,1)S(1)} collective-permute-done((bf16[256,2048]{1,0:T(8,128)(2,1)S(1)}, bf16[256,2048]{1,0:T(8,128)(2,1)S(1)}, u32[]{:S(2)}, u32[]{:S(2)}) %collective-permute-start.48) | collective-permute-done | bytes 1048608 | tf_op jit(solution)/shard_map/back_ring/ppermute | solution.py:562
  521.5 14.8 %collective-permute-done.54.refs_10_ = bf16[256,2048]{1,0:T(8,128)(2,1)S(1)} collective-permute-done((bf16[256,2048]{1,0:T(8,128)(2,1)S(1)}, bf16[256,2048]{1,0:T(8,128)(2,1)S(1)}, u32[]{:S(2)}, u32[]{:S(2)}) %collective-permute-start.54) | collective-permute-done | bytes 1048608 | tf_op jit(solution)/shard_map/back_ring/ppermute | solution.py:562
  537.2 12.3 %mid.1 = (f32[256,2048]{1,0:T(8,128)}, bf16[256,2048]{1,0:T(8,128)(2,1)S(1)}, f32[1,2048]{1,0:T(1,128)S(1)}, bf16[8,256,256]{2,1,0:T(8,128)(2,1)}) custom-call(s32[13]{0:T(128)S(1)} %pad_add_fusion.at, bf16[512,1024]{1,0:T(8,128)(2,1)} %constant_dynamic-update-slice_fusion.refs_0_, bf16[512,1024]{1,0:T(8,128)(2,1)} %collective-permute-done.6.refs_1_, ...), custom_call_target="tpu_custom_call" | custom-call | flops 2147483648 | bytes 16777216 | tf_op jit(solution)/shard_map/mid/pallas_call | solution.py:471
  567.0 6.3 fusion.72
  582.8 25.1 %all-to-all-done.2 = bf16[8,256,256]{2,1,0:T(8,128)(2,1)} async-done(((bf16[8,256,256]{2,1,0:T(8,128)(2,1)}), bf16[8,256,256]{2,1,0:T(8,128)(2,1)}, u32[]{:S(2)}, u32[]{:S(2)}) %all-to-all-start.2) | async-done | bytes 1048608 | tf_op jit(solution)/shard_map/d_mixed/all_to_all | solution.py:706
  612.2 33.5 %attn_bwd.1 = (bf16[2048,256]{1,0:T(8,128)(2,1)S(1)}, bf16[2048,128]{1,0:T(8,128)(2,1)S(1)}) custom-call(bf16[2048,256]{1,0:T(8,128)(2,1)S(1)} %get-tuple-element.107.q_ref, bf16[2048,128]{1,0:T(8,128)(2,1)S(1)} %get-tuple-element.108.kv_ref, bf16[2048,256]{1,0:T(8,128)(2,1)} %bitcast.35.do_ref, f32[256,2048]{1,0:T(8,128)} %get-tuple-element.154.ot_ref, ...), custom_call_target="tpu_custom_call" | custom-call | flops 21474836480 | bytes 8388608 | tf_op jit(solution)/shard_map/attn_bwd/pallas_call | solution.py:251
  648.9 7.0 convolution_convert_fusion
  664.6 7.1 collective-permute-done.68
  675.8 7.0 collective-permute-done.67
  711.4 19.5 %collective-permute-done.72 = bf16[512,1024]{1,0:T(8,128)(2,1)} collective-permute-done((bf16[512,1024]{1,0:T(8,128)(2,1)}, bf16[512,1024]{1,0:T(8,128)(2,1)}, u32[]{:S(2)}, u32[]{:S(2)}) %collective-permute-start.72) | collective-permute-done | bytes 1048608 | tf_op jit(solution)/shard_map/down_grad/ppermute | solution.py:568
  746.4 12.7 %collective-permute-done.58 = bf16[256,2048]{1,0:T(8,128)(2,1)} collective-permute-done((bf16[256,2048]{1,0:T(8,128)(2,1)}, bf16[256,2048]{1,0:T(8,128)(2,1)}, u32[]{:S(2)}, u32[]{:S(2)}) %collective-permute-start.58) | collective-permute-done | bytes 1048608 | tf_op jit(solution)/shard_map/down_ring/ppermute | solution.py:562
  769.7 20.7 %collective-permute-done.74 = bf16[512,1024]{1,0:T(8,128)(2,1)S(1)} collective-permute-done((bf16[512,1024]{1,0:T(8,128)(2,1)S(1)}, bf16[512,1024]{1,0:T(8,128)(2,1)S(1)}, u32[]{:S(2)}, u32[]{:S(2)}) %collective-permute-start.74) | collective-permute-done | bytes 1048608 | tf_op jit(solution)/shard_map/out_grad/ppermute | solution.py:568
  795.6 17.5 %collective-permute-done.82 = bf16[512,1024]{1,0:T(8,128)(2,1)S(1)} collective-permute-done((bf16[512,1024]{1,0:T(8,128)(2,1)S(1)}, bf16[512,1024]{1,0:T(8,128)(2,1)S(1)}, u32[]{:S(2)}, u32[]{:S(2)}) %collective-permute-start.82) | collective-permute-done | bytes 1048608 | tf_op jit(solution)/shard_map/up_grad/ppermute | solution.py:568
  813.2 21.9 %collective-permute-done.84 = bf16[512,1024]{1,0:T(8,128)(2,1)S(1)} collective-permute-done((bf16[512,1024]{1,0:T(8,128)(2,1)S(1)}, bf16[512,1024]{1,0:T(8,128)(2,1)S(1)}, u32[]{:S(2)}, u32[]{:S(2)}) %collective-permute-start.84) | collective-permute-done | bytes 1048608 | tf_op jit(solution)/shard_map/down_grad/ppermute | solution.py:568
  (426 shorter events, 324.2 us)
Async XLA Ops:
  9.8 64.3 %collective-permute-start.4 = (bf16[512,1024]{1,0:T(8,128)(2,1)}, bf16[512,1024]{1,0:T(8,128)(2,1)}, u32[]{:S(2)}, u32[]{:S(2)}) collective-permute-start(bf16[512,1024]{1,0:T(8,128)(2,1)} %refs_4_.7), channel_id=1, source_target_pairs={{0,16},{8,24},{16,0},{24,8},{1,17},{9,25},{17,1},{25,9},{2,18},{10... | collective-permute-start | bytes 3145736 | tf_op jit(solution)/shard_map/gate_weight/ppermute | solution.py:568
  13.0 74.6 %all-to-all-start = ((bf16[8,64,512]{2,1,0:T(8,128)(2,1)}), bf16[8,64,512]{2,1,0:T(8,128)(2,1)S(1)}, u32[]{:S(2)}, u32[]{:S(2)}) async-start(bf16[8,64,512]{2,1,0:T(8,128)(2,1)} %copy.89), calls=%async_computation | async-start | bytes 1048576 | tf_op jit(solution)/shard_map/projection_columns/all_to_all | solution.py:614
  35.6 58.8 %collective-permute-start.16 = (bf16[256,2048]{1,0:T(8,128)(2,1)}, bf16[256,2048]{1,0:T(8,128)(2,1)}, u32[]{:S(2)}, u32[]{:S(2)}) collective-permute-start(bf16[256,2048]{1,0:T(8,128)(2,1)} %collective-permute-done.15.mine), channel_id=1, source_target_pairs={{0,2},{1,3},{2,6},{3,7},{4,0},{5,1},{6,4},{7,5},{8,10},{9,11},{10,... | collective-permute-start | bytes 3145736 | tf_op jit(solution)/shard_map/tokens_ring/ppermute | solution.py:562
  74.1 70.3 %collective-permute-start.24 = (bf16[256,2048]{1,0:T(8,128)(2,1)S(1)}, bf16[256,2048]{1,0:T(8,128)(2,1)S(1)}, u32[]{:S(2)}, u32[]{:S(2)}) collective-permute-start(bf16[256,2048]{1,0:T(8,128)(2,1)S(1)} %pad_maximum_fusion.3.mine.refs_11_.x_ref), channel_id=1, source_target_pairs={{0,1},{1,0},{2,3},{3,2},{4,5},{5,4},{6,7},{7,6},{8,9},{9,8},{10,11... | collective-permute-start | bytes 3145736 | tf_op jit(solution)/shard_map/tokens_ring/ppermute | solution.py:565
  153.1 72.3 %collective-permute-start.10 = (bf16[512,1024]{1,0:T(8,128)(2,1)}, bf16[512,1024]{1,0:T(8,128)(2,1)}, u32[]{:S(2)}, u32[]{:S(2)}) collective-permute-start(bf16[512,1024]{1,0:T(8,128)(2,1)} %constant_dynamic-update-slice_fusion.refs_0_), channel_id=1, source_target_pairs={{0,1},{1,0},{2,3},{3,2},{4,5},{5,4},{6,7},{7,6},{8,9},{9,8},{10,11... | collective-permute-start | bytes 3145736 | tf_op jit(solution)/shard_map/out_weight/ppermute | solution.py:565
  163.2 64.5 %collective-permute-start.12 = (bf16[512,1024]{1,0:T(8,128)(2,1)}, bf16[512,1024]{1,0:T(8,128)(2,1)}, u32[]{:S(2)}, u32[]{:S(2)}) collective-permute-start(bf16[512,1024]{1,0:T(8,128)(2,1)} %collective-permute-done.7.refs_2_), channel_id=1, source_target_pairs={{0,1},{1,0},{2,3},{3,2},{4,5},{5,4},{6,7},{7,6},{8,9},{9,8},{10,11... | collective-permute-start | bytes 3145736 | tf_op jit(solution)/shard_map/out_weight/ppermute | solution.py:565
  163.2 63.8 %collective-permute-start.11 = (bf16[512,1024]{1,0:T(8,128)(2,1)}, bf16[512,1024]{1,0:T(8,128)(2,1)}, u32[]{:S(2)}, u32[]{:S(2)}) collective-permute-start(bf16[512,1024]{1,0:T(8,128)(2,1)} %collective-permute-done.6.refs_1_), channel_id=1, source_target_pairs={{0,1},{1,0},{2,3},{3,2},{4,5},{5,4},{6,7},{7,6},{8,9},{9,8},{10,11... | collective-permute-start | bytes 3145736 | tf_op jit(solution)/shard_map/out_weight/ppermute | solution.py:565
  173.9 47.9 %collective-permute-start.32 = (bf16[512,1024]{1,0:T(8,128)(2,1)}, bf16[512,1024]{1,0:T(8,128)(2,1)}, u32[]{:S(2)}, u32[]{:S(2)}) collective-permute-start(bf16[512,1024]{1,0:T(8,128)(2,1)} %refs_9_.3), channel_id=1, source_target_pairs={{0,16},{8,24},{16,0},{24,8},{1,17},{9,25},{17,1},{25,9},{2,18},{10... | collective-permute-start | bytes 3145736 | tf_op jit(solution)/shard_map/up_weight/ppermute | solution.py:568
  227.7 55.1 %collective-permute-start.31 = (bf16[512,1024]{1,0:T(8,128)(2,1)}, bf16[512,1024]{1,0:T(8,128)(2,1)}, u32[]{:S(2)}, u32[]{:S(2)}) collective-permute-start(bf16[512,1024]{1,0:T(8,128)(2,1)} %refs_9_.3), channel_id=1, source_target_pairs={{0,8},{8,0},{16,24},{24,16},{1,9},{9,1},{17,25},{25,17},{2,10},{10... | collective-permute-start | bytes 3145736 | tf_op jit(solution)/shard_map/up_weight/ppermute | solution.py:568
  238.5 66.2 %collective-permute-start.35 = (bf16[512,1024]{1,0:T(8,128)(2,1)}, bf16[512,1024]{1,0:T(8,128)(2,1)}, u32[]{:S(2)}, u32[]{:S(2)}) collective-permute-start(bf16[512,1024]{1,0:T(8,128)(2,1)} %refs_14_.3), channel_id=1, source_target_pairs={{0,8},{8,0},{16,24},{24,16},{1,9},{9,1},{17,25},{25,17},{2,10},{10... | collective-permute-start | bytes 3145736 | tf_op jit(solution)/shard_map/down_weight/ppermute | solution.py:568
  240.5 69.8 %collective-permute-start.40 = (bf16[256,2048]{1,0:T(8,128)(2,1)}, bf16[256,2048]{1,0:T(8,128)(2,1)}, u32[]{:S(2)}, u32[]{:S(2)}) collective-permute-start(bf16[256,2048]{1,0:T(8,128)(2,1)} %pad_maximum_fusion.4.refs_2_.refs_14_), channel_id=1, source_target_pairs={{0,1},{1,0},{2,3},{3,2},{4,5},{5,4},{6,7},{7,6},{8,9},{9,8},{10,11... | collective-permute-start | bytes 3145736 | tf_op jit(solution)/shard_map/cotangent_ring/ppermute | solution.py:565
  255.3 55.8 %collective-permute-start.36 = (bf16[512,1024]{1,0:T(8,128)(2,1)}, bf16[512,1024]{1,0:T(8,128)(2,1)S(1)}, u32[]{:S(2)}, u32[]{:S(2)}) collective-permute-start(bf16[512,1024]{1,0:T(8,128)(2,1)} %refs_14_.3), channel_id=1, source_target_pairs={{0,16},{8,24},{16,0},{24,8},{1,17},{9,25},{17,1},{25,9},{2,18},{10... | collective-permute-start | bytes 3145736 | tf_op jit(solution)/shard_map/down_weight/ppermute | solution.py:568
  260.3 53.0 %collective-permute-start.25 = (bf16[256,2048]{1,0:T(8,128)(2,1)}, bf16[256,2048]{1,0:T(8,128)(2,1)S(1)}, u32[]{:S(2)}, u32[]{:S(2)}) collective-permute-start(bf16[256,2048]{1,0:T(8,128)(2,1)} %get-tuple-element.111.refs_0_), channel_id=1, source_target_pairs={{0,2},{1,3},{2,6},{3,7},{4,0},{5,1},{6,4},{7,5},{8,10},{9,11},{10,... | collective-permute-start | bytes 3145736 | tf_op jit(solution)/shard_map/normed_ring/ppermute | solution.py:562
  325.5 48.9 %collective-permute-start.28 = (bf16[256,2048]{1,0:T(8,128)(2,1)}, bf16[256,2048]{1,0:T(8,128)(2,1)S(1)}, u32[]{:S(2)}, u32[]{:S(2)}) collective-permute-start(bf16[256,2048]{1,0:T(8,128)(2,1)} %collective-permute-done.27.refs_2_), channel_id=1, source_target_pairs={{0,1},{1,0},{2,3},{3,2},{4,5},{5,4},{6,7},{7,6},{8,9},{9,8},{10,11... | collective-permute-start | bytes 3145736 | tf_op jit(solution)/shard_map/cotangent_ring/ppermute | solution.py:565
  336.7 71.4 %collective-permute-start.51 = (bf16[256,2048]{1,0:T(8,128)(2,1)}, bf16[256,2048]{1,0:T(8,128)(2,1)S(1)}, u32[]{:S(2)}, u32[]{:S(2)}) collective-permute-start(bf16[256,2048]{1,0:T(8,128)(2,1)} %copy-done.56), channel_id=1, source_target_pairs={{0,2},{1,3},{2,6},{3,7},{4,0},{5,1},{6,4},{7,5},{8,10},{9,11},{10,... | collective-permute-start | bytes 3145736 | tf_op jit(solution)/shard_map/cotangent_ring/ppermute | solution.py:562
  373.8 58.6 %collective-permute-start.56 = (bf16[2,256,2048]{2,1,0:T(8,128)(2,1)}, bf16[2,256,2048]{2,1,0:T(8,128)(2,1)S(1)}, u32[]{:S(2)}, u32[]{:S(2)}) collective-permute-start(bf16[2,256,2048]{2,1,0:T(8,128)(2,1)} %get-tuple-element.145), channel_id=1, source_target_pairs={{0,1},{1,0},{2,3},{3,2},{4,5},{5,4},{6,7},{7,6},{8,9},{9,8},{10,11... | collective-permute-start | bytes 6291464 | tf_op jit(solution)/shard_map/feed_forward_pair/ppermute | solution.py:565
  408.1 48.8 %collective-permute-start.41 = (bf16[2,256,2048]{2,1,0:T(8,128)(2,1)}, bf16[2,256,2048]{2,1,0:T(8,128)(2,1)S(1)}, u32[]{:S(2)}, u32[]{:S(2)}) collective-permute-start(bf16[2,256,2048]{2,1,0:T(8,128)(2,1)} %get-tuple-element.122), channel_id=1, source_target_pairs={{0,1},{1,0},{2,3},{3,2},{4,5},{5,4},{6,7},{7,6},{8,9},{9,8},{10,11... | collective-permute-start | bytes 6291464 | tf_op jit(solution)/shard_map/feed_forward_pair/ppermute | solution.py:565
  432.1 51.5 %collective-permute-start.47 = (bf16[2,256,2048]{2,1,0:T(8,128)(2,1)}, bf16[2,256,2048]{2,1,0:T(8,128)(2,1)S(1)}, u32[]{:S(2)}, u32[]{:S(2)}) collective-permute-start(bf16[2,256,2048]{2,1,0:T(8,128)(2,1)} %get-tuple-element.130), channel_id=1, source_target_pairs={{0,1},{1,0},{2,3},{3,2},{4,5},{5,4},{6,7},{7,6},{8,9},{9,8},{10,11... | collective-permute-start | bytes 6291464 | tf_op jit(solution)/shard_map/feed_forward_pair/ppermute | solution.py:565
  456.6 53.7 %collective-permute-start.53 = (bf16[2,256,2048]{2,1,0:T(8,128)(2,1)}, bf16[2,256,2048]{2,1,0:T(8,128)(2,1)S(1)}, u32[]{:S(2)}, u32[]{:S(2)}) collective-permute-start(bf16[2,256,2048]{2,1,0:T(8,128)(2,1)} %get-tuple-element.138), channel_id=1, source_target_pairs={{0,1},{1,0},{2,3},{3,2},{4,5},{5,4},{6,7},{7,6},{8,9},{9,8},{10,11... | collective-permute-start | bytes 6291464 | tf_op jit(solution)/shard_map/feed_forward_pair/ppermute | solution.py:565
  469.4 50.5 %collective-permute-start.70 = (bf16[512,1024]{1,0:T(8,128)(2,1)S(1)}, bf16[512,1024]{1,0:T(8,128)(2,1)S(1)}, u32[]{:S(2)}, u32[]{:S(2)}) collective-permute-start(bf16[512,1024]{1,0:T(8,128)(2,1)S(1)} %fusion.42), channel_id=1, source_target_pairs={{0,24},{8,16},{16,8},{24,0},{1,25},{9,17},{17,9},{25,1},{2,26},{10... | collective-permute-start | bytes 3145736 | tf_op jit(solution)/shard_map/gate_grad/ppermute | solution.py:568
  519.9 58.3 %collective-permute-start.71 = (bf16[512,1024]{1,0:T(8,128)(2,1)}, bf16[512,1024]{1,0:T(8,128)(2,1)}, u32[]{:S(2)}, u32[]{:S(2)}) collective-permute-start(bf16[512,1024]{1,0:T(8,128)(2,1)} %fusion.45), channel_id=1, source_target_pairs={{0,24},{8,16},{16,8},{24,0},{1,25},{9,17},{17,9},{25,1},{2,26},{10... | collective-permute-start | bytes 3145736 | tf_op jit(solution)/shard_map/up_grad/ppermute | solution.py:568
  577.8 133.0 %collective-permute-start.69 = (bf16[2048,1024]{1,0:T(8,128)(2,1)}, bf16[2048,1024]{1,0:T(8,128)(2,1)}, u32[]{:S(2)}, u32[]{:S(2)}) collective-permute-start(bf16[2048,1024]{1,0:T(8,128)(2,1)} %bitcast.57), channel_id=1, source_target_pairs={{0,1},{1,0},{2,3},{3,2},{4,5},{5,4},{6,7},{7,6},{8,9},{9,8},{10,11... | collective-permute-start | bytes 12582920 | tf_op jit(solution)/shard_map/out_grad/ppermute | solution.py:565
  611.3 82.2 %collective-permute-start.57 = (bf16[256,2048]{1,0:T(8,128)(2,1)}, bf16[256,2048]{1,0:T(8,128)(2,1)}, u32[]{:S(2)}, u32[]{:S(2)}) collective-permute-start(bf16[256,2048]{1,0:T(8,128)(2,1)} %fusion.10), channel_id=1, source_target_pairs={{0,2},{1,3},{2,6},{3,7},{4,0},{5,1},{6,4},{7,5},{8,10},{9,11},{10,... | collective-permute-start | bytes 3145736 | tf_op jit(solution)/shard_map/down_ring/ppermute | solution.py:562
  648.9 47.0 %collective-permute-start.59 = (bf16[256,2048]{1,0:T(8,128)(2,1)}, bf16[256,2048]{1,0:T(8,128)(2,1)}, u32[]{:S(2)}, u32[]{:S(2)}) collective-permute-start(bf16[256,2048]{1,0:T(8,128)(2,1)} %convolution_convert_fusion.9), channel_id=1, source_target_pairs={{0,1},{1,0},{2,3},{3,2},{4,5},{5,4},{6,7},{7,6},{8,9},{9,8},{10,11... | collective-permute-start | bytes 3145736 | tf_op jit(solution)/shard_map/first_ring/ppermute | solution.py:565
  682.9 57.6 %collective-permute-start.80 = (bf16[512,1024]{1,0:T(8,128)(2,1)}, bf16[512,1024]{1,0:T(8,128)(2,1)}, u32[]{:S(2)}, u32[]{:S(2)}) collective-permute-start(bf16[512,1024]{1,0:T(8,128)(2,1)} %fusion.54), channel_id=1, source_target_pairs={{0,8},{8,0},{16,24},{24,16},{1,9},{9,1},{17,25},{25,17},{2,10},{10... | collective-permute-start | bytes 3145736 | tf_op jit(solution)/shard_map/gate_grad/ppermute | solution.py:568
  685.1 56.1 %collective-permute-start.81 = (bf16[512,1024]{1,0:T(8,128)(2,1)}, bf16[512,1024]{1,0:T(8,128)(2,1)}, u32[]{:S(2)}, u32[]{:S(2)}) collective-permute-start(bf16[512,1024]{1,0:T(8,128)(2,1)} %fusion.60), channel_id=1, source_target_pairs={{0,16},{8,24},{16,0},{24,8},{1,17},{9,25},{17,1},{25,9},{2,18},{10... | collective-permute-start | bytes 3145736 | tf_op jit(solution)/shard_map/gate_grad/ppermute | solution.py:568
  695.9 47.0 %collective-permute-start.61 = (bf16[256,2048]{1,0:T(8,128)(2,1)}, bf16[256,2048]{1,0:T(8,128)(2,1)}, u32[]{:S(2)}, u32[]{:S(2)}) collective-permute-start(bf16[256,2048]{1,0:T(8,128)(2,1)} %convolution_convert_fusion.7), channel_id=1, source_target_pairs={{0,1},{1,0},{2,3},{3,2},{4,5},{5,4},{6,7},{7,6},{8,9},{9,8},{10,11... | collective-permute-start | bytes 3145736 | tf_op jit(solution)/shard_map/first_ring/ppermute | solution.py:565
  742.9 47.4 %collective-permute-start.74 = (bf16[512,1024]{1,0:T(8,128)(2,1)S(1)}, bf16[512,1024]{1,0:T(8,128)(2,1)S(1)}, u32[]{:S(2)}, u32[]{:S(2)}) collective-permute-start(bf16[512,1024]{1,0:T(8,128)(2,1)S(1)} %get-tuple-element.168), channel_id=1, source_target_pairs={{0,16},{8,24},{16,0},{24,8},{1,17},{9,25},{17,1},{25,9},{2,18},{10... | collective-permute-start | bytes 3145736 | tf_op jit(solution)/shard_map/out_grad/ppermute | solution.py:568
  744.3 47.5 %collective-permute-start.73 = (bf16[512,1024]{1,0:T(8,128)(2,1)S(1)}, bf16[512,1024]{1,0:T(8,128)(2,1)S(1)}, u32[]{:S(2)}, u32[]{:S(2)}) collective-permute-start(bf16[512,1024]{1,0:T(8,128)(2,1)S(1)} %get-tuple-element.167), channel_id=1, source_target_pairs={{0,8},{8,0},{16,24},{24,16},{1,9},{9,1},{17,25},{25,17},{2,10},{10... | collective-permute-start | bytes 3145736 | tf_op jit(solution)/shard_map/out_grad/ppermute | solution.py:568
  762.2 50.9 %collective-permute-start.82 = (bf16[512,1024]{1,0:T(8,128)(2,1)S(1)}, bf16[512,1024]{1,0:T(8,128)(2,1)S(1)}, u32[]{:S(2)}, u32[]{:S(2)}) collective-permute-start(bf16[512,1024]{1,0:T(8,128)(2,1)S(1)} %copy-done.53), channel_id=1, source_target_pairs={{0,8},{8,0},{16,24},{24,16},{1,9},{9,1},{17,25},{25,17},{2,10},{10... | collective-permute-start | bytes 3145736 | tf_op jit(solution)/shard_map/up_grad/ppermute | solution.py:568
  813.1 47.1 %collective-permute-start.65 = (bf16[256,2048]{1,0:T(8,128)(2,1)S(1)}, bf16[256,2048]{1,0:T(8,128)(2,1)S(1)}, u32[]{:S(2)}, u32[]{:S(2)}) collective-permute-start(bf16[256,2048]{1,0:T(8,128)(2,1)S(1)} %copy-done.33), channel_id=1, source_target_pairs={{0,1},{1,0},{2,3},{3,2},{4,5},{5,4},{6,7},{7,6},{8,9},{9,8},{10,11... | collective-permute-start | bytes 3145736 | tf_op jit(solution)/shard_map/first_ring/ppermute | solution.py:565
  813.1 47.1 %collective-permute-start.64 = (bf16[256,2048]{1,0:T(8,128)(2,1)S(1)}, bf16[256,2048]{1,0:T(8,128)(2,1)S(1)}, u32[]{:S(2)}, u32[]{:S(2)}) collective-permute-start(bf16[256,2048]{1,0:T(8,128)(2,1)S(1)} %add_convert_fusion.2), channel_id=1, source_target_pairs={{0,2},{1,3},{2,6},{3,7},{4,0},{5,1},{6,4},{7,5},{8,10},{9,11},{10,... | collective-permute-start | bytes 3145736 | tf_op jit(solution)/shard_map/first_ring/ppermute | solution.py:562
  (130 other events, 2555.7 us)

commit v3 on v2

--- a/solution.py
+++ b/solution.py
@@ -67,7 +67,7 @@
     inverse = lax.rsqrt(jnp.mean(x * x, axis=-1, keepdims=True) + epsilon)
     low = (x * inverse * gain[...]).astype(bf16)
     normed[...] = low
-    y = mm(low, w[...], NN)
+    y = mm(low, w[:, : width + 2 * HD], NN)
     for first in range(0, width, LANES):
         part = y[:, first : first + LANES]
         queries[:, first : first + LANES] = turn(part, cos[...], sin[...]).astype(bf16)
@@ -350,7 +350,7 @@
 def ffn_kernel(pieces, *refs):
     x_mine, x_other, c_mine, c_other = refs[:4]
     weights = [refs[4 + i * pieces : 4 + (i + 1) * pieces] for i in range(3)]
-    xs, cs, hidden, d_gate, d_up, back_mine, down_mine, others, back, down = refs[-10:]
+    xs, cs, hidden, d_gate, d_up, back_mine, down_mine, back_other, down_other, back, down = refs[-11:]
     u = pl.program_id(0)
     w_gate, w_up, w_down = (jnp.concatenate([r[...] for r in w], axis=0) for w in weights)
     x = jnp.concatenate([x_mine[...], x_other[...]], axis=0)
@@ -384,8 +384,8 @@
         rows = back_mine.shape[0]
         back_mine[...] = back[:rows].astype(bf16)
         down_mine[...] = down[:rows].astype(bf16)
-        others[0] = back[rows:].astype(bf16)
-        others[1] = down[rows:].astype(bf16)
+        back_other[...] = back[rows:].astype(bf16)
+        down_other[...] = down[rows:].astype(bf16)
 
 
 def ffn_call(s, count, x_mine, x_other, c_mine, c_other, w_gate, w_up, w_down, held, tile=256):
@@ -403,11 +403,8 @@
         functools.partial(ffn_kernel, len(w_gate)),
         grid=(units // tile,),
         in_specs=[block] * 4 + weights * 3 + [pl.BlockSpec(memory_space=pl.ANY)] * len(held),
-        out_specs=[full] * 2 + [act] * 3 + [block] * 2 + [pl.BlockSpec((2, rows, depth), lambda u: (0, 0, 0))],
-        out_shape=[full_shape] * 2
-        + [act_shape] * 3
-        + [row_shape] * 2
-        + [jax.ShapeDtypeStruct((2, rows, depth), bf16)],
+        out_specs=[full] * 2 + [act] * 3 + [block] * 4,
+        out_shape=[full_shape] * 2 + [act_shape] * 3 + [row_shape] * 4,
         scratch_shapes=[pltpu.VMEM((2 * rows, depth), f32)] * 2,
         input_output_aliases={first + i: i for i in range(len(held))},
         compiler_params=params(),
@@ -556,7 +553,7 @@
     pair_at = 2 * chunk[:, None] + jnp.stack([core_at, 1 - core_at])[None, :]
     dp_order = dp_at ^ jnp.arange(dp_count)
     group_order = (dp_order[:, None] * (groups // dp_count) + jnp.arange(groups // dp_count)).reshape(-1)
-    at = jnp.concatenate([core_at[None], dp_order, group_order]).astype(jnp.int32)
+    at = jnp.concatenate([core_at[None], jnp.arange(dp_count), group_order]).astype(jnp.int32)
 
     def step_ring(x):
         return lax.ppermute(x, "seq", ring)
@@ -573,12 +570,12 @@
     def cols_at(x, start, count):
         return lax.dynamic_slice_in_dim(x, start, count, 1)
 
-    def reorder(x):
-        return jnp.concatenate([cols_at(x, dp_order[k] * block, block) for k in range(dp_count)], axis=1)
-
     def gather_dp(x):
+        return [x] + [step_dp(x, k) for k in range(1, dp_count)]
+
+    def gather_hops(x):
         if dp_count != 4:
-            return [x] + [step_dp(x, k) for k in range(1, dp_count)]
+            return gather_dp(x)
         cut = x.shape[0] // 2
         one, two = step_dp(x, 1), step_dp(x, 2)
         return [x, one, two, step_dp(one[:cut], 2), step_dp(two[cut:], 1)]
@@ -586,17 +583,17 @@
     def scatter_dp(parts):
         return [step_dp(parts[k], k) for k in range(1, dp_count)]
 
+    def full_weight(w):
+        return [lax.all_gather(w, "dp", axis=0, tiled=True)]
+
+    def owned_grad(grad):
+        return lax.psum_scatter(grad, "dp", scatter_dimension=0, tiled=True)
+
     def pair_sides(own, got):
         return jnp.where(core_at == 0, jnp.concatenate([own, got]), jnp.concatenate([got, own]))
 
-    x_own = reorder(tokens.reshape(piece, depth))
-    cot_own = reorder(cotangent.reshape(piece, depth))
-
-    with jax.named_scope("tokens_ring"):
-        x_mine, x_other = [x_own], [step_swap(x_own)]
-        for _ in range(chips - 1):
-            x_mine.append(step_ring(x_mine[-1]))
-            x_other.append(step_swap(x_mine[-1]))
+    x_own = tokens.reshape(piece, depth)
+    cot_own = cotangent.reshape(piece, depth)
 
     def per_group(w):
         return jnp.repeat(w.reshape(own_rows, KV, HD), repeat, axis=1)
@@ -613,66 +610,57 @@
         dp_rows = groups * own_rows
         cols_dp = lax.all_to_all(jnp.transpose(own_cols, (1, 0, 2)), "seq", 0, 0, tiled=True)
         cols_dp = cols_dp.reshape(dp_rows, cols)
-        cols_all = jnp.concatenate([cols_dp] + [step_dp(cols_dp, k) for k in range(1, dp_count)], axis=0)
+
+    with jax.named_scope("tokens_ring"):
+        x_mine = [x_own, step_ring(after(x_own, own_cols))]
+
+    with jax.named_scope("projection_columns"):
+        cols_all = jnp.zeros((depth, cols), bf16)
+        for k, part in enumerate(gather_dp(cols_dp)):
+            cols_all = lax.dynamic_update_slice_in_dim(cols_all, part, dp_order[k] * dp_rows, 0)
         w_qkv = cols_all[:, : width + 2 * HD]
         gains = jnp.transpose(cols_all[:, width + 2 * HD : width + 2 * HD + 2].astype(f32))
         gain_one, gain_two = gains[:1], gains[1:]
+
+    with jax.named_scope("tokens_ring"):
+        for s in range(2, chips):
+            x_mine.append(step_ring(after(x_mine[-1], cols_dp if s == 2 else cols_all)))
+        x_other = [step_swap(x) for x in x_mine]
 
     with jax.named_scope("out_weight"):
         keep = cols_at(w_out, core_at * half, half)
         give = cols_at(w_out, (1 - core_at) * half, half)
         chip_rows = [pair_sides(keep, step_swap(give))]
-        for _ in range(chips - 1):
-            chip_rows.append(step_ring(chip_rows[-1]))
+        for s in range(1, chips):
+            chip_rows.append(step_ring(after(chip_rows[0], x_mine[-1]) if s == 1 else chip_rows[-1]))
         out_rows = jnp.zeros((dp_rows, half), bf16)
         for s in range(chips):
             out_rows = lax.dynamic_update_slice_in_dim(out_rows, chip_rows[s], chunk[s] * 2 * own_rows, 0)
 
-    with jax.named_scope("gate_weight"):
-        gate_full = gather_dp(w_gate)
-    with jax.named_scope("out_weight"):
-        out_mine = gather_dp(after(out_rows, gate_full[-1]))
+        out_mine = gather_hops(out_rows)
         out_other = [step_swap(p) for p in out_mine]
-    with jax.named_scope("up_weight"):
-        up_full = gather_dp(after(w_up, out_mine[-1]))
-    with jax.named_scope("down_weight"):
-        down_full = gather_dp(after(w_down, up_full[-1]))
+
+    with jax.named_scope("feed_forward_weights"):
+        gate_full, up_full, down_full = full_weight(w_gate), full_weight(w_up), full_weight(w_down)
 
     cos, sin = rope_tables(length)
 
     held = ()
     for s in range(chips):
         held = qkv_call(
-            pair_at[s], x_mine[s], x_other[s], gain_one, w_qkv, cos, sin, width, length, held
+            pair_at[s], x_mine[s], after(x_other[s], chip_rows[s]), gain_one, cols_all, cos, sin, width, length, held
         )
     normed, queries, keys_values = held
 
     with jax.named_scope("cotangent_ring"):
-        c_mine = [cot_own, step_ring(after(cot_own, x_mine[-1]))]
+        c_mine = [cot_own, step_ring(after(cot_own, chip_rows[-1]))]
         c_other = [step_swap(c) for c in c_mine]
 
     head_out, out_t, lse = attn_fwd(queries, keys_values)
     with jax.named_scope("mixed"):
-        mixed = lax.all_to_all(head_out.reshape(groups, piece, width), "seq", 0, 0, tiled=True)
+        head_out = after(head_out, c_mine[1]).reshape(groups, piece, width)
+        mixed = lax.all_to_all(head_out, "seq", 0, 0, tiled=True)
     middle, normed_two = out_call(at, out_mine, out_other, mixed, x_own, gain_two, dp_count)
-
-    n_mine, n_other, ffn, held = [], [], [], ()
-    for s in range(chips):
-        with jax.named_scope("normed_ring"):
-            n_mine.append(step_ring(n_mine[-1]) if s else normed_two)
-            n_other.append(step_swap(n_mine[-1]))
-        if s >= 2:
-            with jax.named_scope("cotangent_ring"):
-                c_mine.append(step_ring(after(c_mine[-1], mixed if s == 2 else n_mine[s - 2])))
-                c_other.append(step_swap(c_mine[-1]))
-        out = ffn_call(
-            s, chips, n_mine[s], n_other[s], c_mine[s], c_other[s], gate_full, up_full, down_full, held
-        )
-        held, rest = out[:5], out[5:]
-        with jax.named_scope("feed_forward_pair"):
-            swapped = step_swap(rest[2])
-        ffn.append((rest[0], rest[1], swapped[0], swapped[1]))
-    n_all, c_all, hidden, d_gate, d_up = held
 
     def add(*parts):
         total = parts[0].astype(f32)
@@ -681,23 +669,46 @@
         return total
 
     def weight_grad(rows, grads):
-        return [
-            mm(rows[:, k * block : (k + 1) * block], grads, TN).astype(bf16) for k in range(dp_count)
-        ]
-
+        return mm(rows, grads, TN).astype(bf16)
+
+    n_mine = [normed_two]
+    for s in range(1, chips):
+        if s + 1 < chips:
+            with jax.named_scope("cotangent_ring"):
+                c_mine.append(step_ring(after(c_mine[-1], mixed if s == 1 else n_mine[-1])))
+                c_other.append(step_swap(c_mine[-1]))
+        with jax.named_scope("normed_ring"):
+            n_mine.append(step_ring(n_mine[-1] if s == 1 else after(n_mine[-1], c_mine[-1])))
+    with jax.named_scope("normed_ring"):
+        n_other = [step_swap(n) for n in n_mine]
+
+    ffn, held, acc = [], (), None
+    for s in range(chips):
+        n_here = n_other[s] if acc is None else after(n_other[s], acc)
+        out = ffn_call(
+            s, chips, n_mine[s], n_here, c_mine[s], c_other[s], gate_full, up_full, down_full, held
+        )
+        held, rest = out[:5], out[5:]
+        with jax.named_scope("feed_forward_pair"):
+            back_swapped = step_swap(rest[2])
+            down_swapped = step_swap(rest[3])
+        ffn.append((rest[0], rest[1], back_swapped, down_swapped))
+        if s:
+            with jax.named_scope("back_ring"):
+                so_far = add(ffn[s][0]) if acc is None else add(step_ring(acc), ffn[s][0])
+                acc = add(lax.optimization_barrier(so_far), ffn[s][2]).astype(bf16)
+    n_all, c_all, hidden, d_gate, d_up = held
+    n_all = after(n_all, acc)
     with jax.named_scope("back_ring"):
-        acc = add(ffn[1][0], ffn[1][2]).astype(bf16)
-        for s in range(2, chips):
-            acc = add(step_ring(acc), ffn[s][0], ffn[s][2]).astype(bf16)
         back_got = step_ring(acc)
 
     with jax.named_scope("gate_grad"):
-        gate_parts = weight_grad(n_all, d_gate)
-        gate_sent = scatter_dp(gate_parts)
+        gate_part = weight_grad(n_all, d_gate)
+        grad_gate = owned_grad(gate_part)
     with jax.named_scope("up_grad"):
-        up_parts = weight_grad(n_all, d_up)
-        up_sent = scatter_dp([after(p, gate_sent[-1]) for p in up_parts])
-    back_got = after(back_got, gate_parts[-1], up_parts[-1])
+        up_part = weight_grad(n_all, d_up)
+        grad_up = owned_grad(up_part)
+    back_got = after(back_got, gate_part, up_part)
 
     d_middle, branch, d_gain_two, d_mixed = mid_call(
         at, out_mine, out_other, back_got, ffn[0][0], ffn[0][2], middle, cot_own, gain_two, width, dp_count
@@ -716,14 +727,18 @@
         out_own = out_part(core_at * half)
     with jax.named_scope("down_grad"):
         down_rows, _ = lax.optimization_barrier((c_all, branch))
-        down_parts = weight_grad(down_rows, hidden)
-        down_sent = scatter_dp([after(p, up_sent[-1]) for p in down_parts])
+        down_part = weight_grad(down_rows, hidden)
+        grad_down = owned_grad(down_part)
 
     with jax.named_scope("down_ring"):
         acc = add(after(ffn[1][1], back_got), ffn[1][3]).astype(bf16)
         down_two = step_ring(acc)
 
-    d_heads = after(d_heads, down_parts[-1], out_own)
+    with jax.named_scope("out_grad"):
+        out_sum = add(out_own, out_theirs_sent).astype(bf16)
+        out_dp = owned_grad(out_sum)
+
+    d_heads = after(d_heads, down_part, out_sum)
 
     d_queries, d_kv = attn_bwd(queries, keys_values, d_heads, out_t, lse, cos, sin)
 
@@ -731,11 +746,6 @@
         for s in range(2, chips):
             acc = add(after(down_two, d_heads if s == 2 else d_kv), ffn[s][1], ffn[s][3]).astype(bf16)
             down_two = step_ring(acc)
-
-    with jax.named_scope("out_grad"):
-        out_sum = add(out_own, after(out_theirs_sent, d_kv)).astype(bf16)
-        out_parts = [rows_at(out_sum, dp_order[k] * dp_rows, dp_rows) for k in range(dp_count)]
-        out_sent = scatter_dp([after(p, down_sent[-1]) for p in out_parts])
 
     with jax.named_scope("first_ring"):
         def d_normed(s, side):
@@ -746,39 +756,32 @@
         steps = list(range(1, chips)) + [0]
         theirs = {s: step_swap(d_normed(s, 1)) for s in steps}
         own = {s: d_normed(s, 0) for s in steps}
-        acc = add(own[1], theirs[1]).astype(bf16)
+        first_acc = [add(own[1], theirs[1]).astype(bf16)]
         for s in range(2, chips):
-            acc = add(step_ring(acc), own[s], theirs[s]).astype(bf16)
-        first_last = acc
-        first_got = step_ring(acc)
+            first_acc.append(add(step_ring(first_acc[-1]), own[s], theirs[s]).astype(bf16))
+        first_got = step_ring(first_acc[-1])
 
     with jax.named_scope("projection_grads"):
         d_qkv = jnp.concatenate([d_queries, d_kv], axis=1)
-        grad_cols = mm(normed, d_qkv, TN).astype(bf16)
+        grad_cols = mm(after(normed, first_acc[0]), d_qkv, TN).astype(bf16)
         high = d_gain_two.astype(bf16)
         rest = (d_gain_two - high.astype(f32)).astype(bf16)
         extra = jnp.pad(jnp.transpose(jnp.concatenate([high, rest], axis=0)), ((0, 0), (0, LANES - 2)))
         grad_cols = jnp.concatenate([grad_cols, extra], axis=1)
-        col_parts = [grad_cols[k * block : (k + 1) * block] for k in range(dp_count)]
-        total = add(col_parts[0], *scatter_dp(col_parts)).astype(bf16)
+        col_parts = [rows_at(grad_cols, dp_order[k] * block, block) for k in range(dp_count)]
+        col_sent = [after(p, first_acc[1]) for p in scatter_dp(col_parts)]
+        total = add(col_parts[0], *col_sent).astype(bf16)
         dealt = lax.all_to_all(total.reshape(groups, own_rows, cols), "seq", 0, 0, tiled=True)
 
     with jax.named_scope("feed_forward_grads"):
-        gate_sent, up_sent, down_sent = lax.optimization_barrier((gate_sent, up_sent, down_sent, first_last))[:3]
-        grad_gate = add(gate_parts[0], *gate_sent)
-        grad_up = add(up_parts[0], *up_sent)
-        grad_down = add(down_parts[0], *down_sent)
+        grads = lax.optimization_barrier((grad_gate, grad_up, grad_down, first_acc[-1]))
+        grad_gate, grad_up, grad_down = (g.astype(f32) for g in grads[:3])
 
     with jax.named_scope("out_grad"):
-        out_dp = add(out_parts[0], *out_sent).astype(bf16)
-
-        def chip_part(s):
-            return rows_at(out_dp, chunk[s] * 2 * own_rows, 2 * own_rows)
-
-        acc = chip_part(1)
-        for s in range(2, chips):
-            acc = add(step_ring(acc), chip_part(s)).astype(bf16)
-        acc = add(step_ring(acc), chip_part(0))
+        same_core = [[2 * c + k for c in range(chips)] for k in range(2)]
+        out_dp = after(out_dp, first_acc[-1]).reshape(chips, 2 * own_rows, half)
+        out_terms = lax.all_to_all(out_dp, "seq", 0, 0, axis_index_groups=same_core, tiled=True)
+        acc = jnp.sum(out_terms.astype(f32), axis=0)
         out_keep = rows_at(acc, core_at * own_rows, own_rows)
         out_give = rows_at(acc, (1 - core_at) * own_rows, own_rows).astype(bf16)
         out_take = step_swap(out_give).astype(f32)
@@ -789,7 +792,7 @@
         )
 
     grad_tokens = first_call(at, first_got, own[0], theirs[0], x_own, d_middle, gain_one, dp_count)
-    block_out = reorder((middle + add(down_two, ffn[0][1], ffn[0][3])).astype(bf16))
+    block_out = (middle + add(down_two, ffn[0][1], ffn[0][3])).astype(bf16)
 
     def join(x):
         return jnp.transpose(x, (1, 0, 2)).reshape(own_rows, -1)
@@ -797,7 +800,7 @@
     def fold(x):
         return join(jnp.sum(x.reshape(KV, repeat, own_rows, HD), axis=1))
 
-    dealt = dealt.astype(f32)
+    dealt = after(dealt, first_acc[-1]).astype(f32)
     grad_query = join(dealt[:, :, :width])
     grad_key = fold(dealt[:, :, width : width + HD])
     grad_value = fold(dealt[:, :, width + HD : width + 2 * HD])

time: 876 us -> 730 us (0.83)
  waiting for transfers between devices: 389 us -> 303 us
  starting transfers between devices: 102 us -> 62.5 us
  matrix products: 87.2 us -> 60.1 us
  local copies, waits for them, and re-layouts: 45.4 us -> 31.7 us
  between operations: 13 us -> 26.5 us
  other arithmetic: 35.7 us -> 45.2 us
    ppermute x34 -> x10, waiting for transfers between devices: 231 us -> 76.6 us  [step_dp(): return lax.ppermute(x, 'dp', [(i, i ^ k) for i in range(dp_count)])]
    ppermute x34 -> x10, starting transfers between devices: 42.1 us -> 9.06 us  [step_dp(): return lax.ppermute(x, 'dp', [(i, i ^ k) for i in range(dp_count)])]
    all_to_all x1, waiting for transfers between devices: 0.01 us -> 25.9 us  [shards(): lax.all_to_all(jnp.transpose(own_cols, (1, 0, 2)), 'seq', 0, 0, tiled=True)]
    dot_general x21 -> x12, matrix products: 78.2 us -> 55.1 us  [mm(): return lax.dot_general(a, b, dims, preferred_element_type=f32)]
    all_to_all x1, waiting for transfers between devices: 5.49 us -> 24.5 us  [shards(): lax.all_to_all(total.reshape(groups, own_rows, cols), 'seq', 0, 0, tiled=...]
    ppermute x24 -> x21, waiting for transfers between devices: 127 us -> 144 us  [step_ring(): return lax.ppermute(x, 'seq', ring)]
    all_to_all x1, waiting for transfers between devices: 25.1 us -> 8.1 us  [shards(): lax.all_to_all(d_mixed, 'seq', 0, 0, tiled=True).reshape(length, width)]
    slice x11 -> x3, local copies, waits for them, and re-layouts: 14.9 us -> 2.74 us  [the longest x2 2.15 us: gather_hops(): return [x, one, two, step_dp(one[:cut], 2), step_dp(two[cut:], 1)]]
  transfers between devices with their start and end apart: 90 -> 75, of which waited for: 34 -> 27; matrix products, arithmetic and copies ran while one was open for 17% -> 17% of each run, Pallas kernels for 22% -> 25%
where the time goes in v3:
time: 730 us; the launch traced here: 722 us
  waiting for transfers between devices  303 us (42%)
  Pallas kernels  192 us (26%)
  starting transfers between devices  62.5 us (9%)
  matrix products  60.1 us (8%)
  other arithmetic  45.2 us (6%)
  local copies, waits for them, and re-layouts  31.7 us (4%)
  between operations  26.5 us (4%)
    ppermute x21, waiting for transfers between devices, step_ring(): return lax.ppermute(x, 'seq', ring)  144 us
    pallas_call x4, Pallas kernels, ffn_call(): pl.pallas_call(functools.partial(ffn_kernel, len(w_gate)), grid=(units //...  87 us
    ppermute x10, waiting for transfers between devices, step_dp(): return lax.ppermute(x, 'dp', [(i, i ^ k) for i in range(dp_count)])  76.6 us
    dot_general x12, matrix products, mm(): return lax.dot_general(a, b, dims, preferred_element_type=f32)  55.1 us
    pallas_call x1, Pallas kernels, attn_bwd(): pl.pallas_call(functools.partial(bwd_kernel, bq, share), grid=(length //...  33.2 us
    all_to_all x1, waiting for transfers between devices, shards(): lax.all_to_all(jnp.transpose(own_cols, (1, 0, 2)), 'seq', 0, 0, tiled=True)  25.9 us
    pallas_call x4, Pallas kernels, qkv_call(): pl.pallas_call(functools.partial(qkv_kernel, width), grid_spec=pltpu.Pref...  25.4 us
    ppermute x21, starting transfers between devices, step_ring(): return lax.ppermute(x, 'seq', ring)  25 us
  transfers between devices with their start and end apart: 75, of which 27 were waited for; matrix products, arithmetic and copies ran while one was open for 17% of the time, Pallas kernels for 25%

profile of v3, /device:TPU:0, one launch (start us, length us, event | category | flops | bytes accessed | tf_op | source)
XLA Modules:
  0.0 721.6 jit_solution(852947241403315655)
XLA Ops:
  21.4 25.9 %all-to-all-done = bf16[8,64,512]{2,1,0:T(8,128)(2,1)S(1)} async-done(((bf16[8,64,512]{2,1,0:T(8,128)(2,1)}), bf16[8,64,512]{2,1,0:T(8,128)(2,1)S(1)}, u32[]{:S(2)}, u32[]{:S(2)}) %all-to-all-start) | async-done | bytes 524320 | tf_op jit(solution)/shard_map/projection_columns/all_to_all | solution.py:611
  57.8 16.8 %collective-permute-done.3 = bf16[512,512]{0,1:T(8,128)(2,1)} collective-permute-done((bf16[512,512]{0,1:T(8,128)(2,1)S(1)}, bf16[512,512]{0,1:T(8,128)(2,1)}, u32[]{:S(2)}, u32[]{:S(2)}) %collective-permute-start.3) | collective-permute-done | bytes 524320 | tf_op jit(solution)/shard_map/projection_columns/ppermute | solution.py:565
  76.6 11.8 %collective-permute-done.5 = bf16[512,512]{0,1:T(8,128)(2,1)} collective-permute-done((bf16[512,512]{0,1:T(8,128)(2,1)S(1)}, bf16[512,512]{0,1:T(8,128)(2,1)}, u32[]{:S(2)}, u32[]{:S(2)}) %collective-permute-start.5) | collective-permute-done | bytes 524320 | tf_op jit(solution)/shard_map/projection_columns/ppermute | solution.py:565
  91.2 5.5 fusion.11
  99.1 16.2 %collective-permute-done.6.mine = bf16[256,2048]{1,0:T(8,128)(2,1)} collective-permute-done((bf16[256,2048]{1,0:T(8,128)(2,1)}, bf16[256,2048]{1,0:T(8,128)(2,1)}, u32[]{:S(2)}, u32[]{:S(2)}) %collective-permute-start.6) | collective-permute-done | bytes 1048608 | tf_op jit(solution)/shard_map/tokens_ring/ppermute | solution.py:559
  116.0 7.0 collective-permute-done.7
  129.0 5.8 qkv.4
  138.2 6.4 qkv.5
  146.0 6.9 qkv.6
  154.2 6.4 qkv.7
  160.6 19.9 %attn_fwd.1 = (bf16[2048,256]{1,0:T(8,128)(2,1)}, f32[256,2048]{1,0:T(8,128)}, f32[8,2048]{1,0:T(8,128)S(1)}) custom-call(bf16[2048,256]{1,0:T(8,128)(2,1)S(1)} %get-tuple-element.119.q_ref, bf16[2048,128]{1,0:T(8,128)(2,1)S(1)} %get-tuple-element.120.kv_ref), custom_call_target="tpu_custom_call" | custom-call | flops 8589934592 | bytes 4194304 | tf_op jit(solution)/shard_map/attn_fwd/pallas_call | solution.py:161
  195.6 20.7 %collective-permute-done.12.refs_3_ = bf16[256,1024]{1,0:T(8,128)(2,1)S(1)} collective-permute-done((bf16[256,1024]{1,0:T(8,128)(2,1)S(1)}, bf16[256,1024]{1,0:T(8,128)(2,1)S(1)}, u32[]{:S(2)}, u32[]{:S(2)}) %collective-permute-start.12) | collective-permute-done | bytes 524320 | tf_op jit(solution)/shard_map/out_weight/ppermute | solution.py:565
  220.8 9.2 %out_norm.1 = (f32[256,2048]{1,0:T(8,128)}, bf16[256,2048]{1,0:T(8,128)(2,1)}) custom-call(s32[13]{0:T(128)S(1)} %pad_add_fusion.at, bf16[512,1024]{1,0:T(8,128)(2,1)} %constant_dynamic-update-slice_fusion.refs_0_, bf16[512,1024]{1,0:T(8,128)(2,1)} %collective-permute-done.10.refs_1_, bf16[512,1024]{1,0:T(8,128)(2,1)} %collective-permute-done.11.refs_2_, ...), custom_call_target="tpu_custom_call" | custom-call | flops 2147483648 | bytes 12582912 | tf_op jit(solution)/shard_map/out_norm/pallas_call | solution.py:330
  232.4 24.8 %collective-permute-done.24.refs_0_ = bf16[256,2048]{1,0:T(8,128)(2,1)} collective-permute-done((bf16[256,2048]{1,0:T(8,128)(2,1)}, bf16[256,2048]{1,0:T(8,128)(2,1)}, u32[]{:S(2)}, u32[]{:S(2)}) %collective-permute-start.24) | collective-permute-done | bytes 1048608 | tf_op jit(solution)/shard_map/normed_ring/ppermute | solution.py:559
  257.3 21.6 %collective-permute-done.31.refs_2_ = bf16[256,2048]{1,0:T(8,128)(2,1)} collective-permute-done((bf16[256,2048]{1,0:T(8,128)(2,1)}, bf16[256,2048]{1,0:T(8,128)(2,1)}, u32[]{:S(2)}, u32[]{:S(2)}) %collective-permute-start.31) | collective-permute-done | bytes 1048608 | tf_op jit(solution)/shard_map/cotangent_ring/ppermute | solution.py:559
  279.0 22.0 %ffn.4 = (bf16[2048,2048]{1,0:T(8,128)(2,1)}, bf16[2048,2048]{1,0:T(8,128)(2,1)}, bf16[2048,1024]{1,0:T(8,128)(2,1)}, bf16[2048,1024]{1,0:T(8,128)(2,1)}, bf16[2...) custom-call(bf16[256,2048]{1,0:T(8,128)(2,1)} %get-tuple-element.125, ...), custom_call_target="tpu_custom_call" | custom-call | flops 12884901888 | bytes 26214400 | tf_op jit(solution)/shard_map/ffn/pallas_call | solution.py:402
  305.0 21.6 %ffn.5 = (bf16[2048,2048]{1,0:T(8,128)(2,1)}, bf16[2048,2048]{1,0:T(8,128)(2,1)}, bf16[2048,1024]{1,0:T(8,128)(2,1)}, bf16[2048,1024]{1,0:T(8,128)(2,1)}, bf16[2...) custom-call(bf16[256,2048]{1,0:T(8,128)(2,1)} %collective-permute-do, ...), custom_call_target="tpu_custom_call", output_to_operand_aliasing={{0}: (7, {}), {1}: (8, {}), {2}: (9, {}), {3}: (10, {}), {4... | custom-call | flops 12884901888 | bytes 26214400 | tf_op jit(solution)/shard_map/ffn/pallas_call | solution.py:402
  336.0 21.7 %ffn.6 = (bf16[2048,2048]{1,0:T(8,128)(2,1)}, bf16[2048,2048]{1,0:T(8,128)(2,1)}, bf16[2048,1024]{1,0:T(8,128)(2,1)}, bf16[2048,1024]{1,0:T(8,128)(2,1)}, bf16[2...) custom-call(bf16[256,2048]{1,0:T(8,128)(2,1)} %copy-done.31, ...), custom_call_target="tpu_custom_call", output_to_operand_aliasing={{0}: (7, {}), {1}: (8, {}), {2}: (9, {}), {3}: (10, {}), {4... | custom-call | flops 12884901888 | bytes 26214400 | tf_op jit(solution)/shard_map/ffn/pallas_call | solution.py:402
  358.3 21.3 %collective-permute-done.38.refs_0_ = bf16[256,2048]{1,0:T(8,128)(2,1)S(1)} collective-permute-done((bf16[256,2048]{1,0:T(8,128)(2,1)S(1)}, bf16[256,2048]{1,0:T(8,128)(2,1)S(1)}, u32[]{:S(2)}, u32[]{:S(2)}) %collective-permute-start.38) | collective-permute-done | bytes 1048608 | tf_op jit(solution)/shard_map/normed_ring/ppermute | solution.py:559
  383.6 21.7 %ffn.7 = (bf16[2048,2048]{1,0:T(8,128)(2,1)}, bf16[2048,2048]{1,0:T(8,128)(2,1)}, bf16[2048,1024]{1,0:T(8,128)(2,1)}, bf16[2048,1024]{1,0:T(8,128)(2,1)}, bf16[2...) custom-call(bf16[256,2048]{1,0:T(8,128)(2,1)} %copy-done.32, ...), custom_call_target="tpu_custom_call", output_to_operand_aliasing={{0}: (7, {}), {1}: (8, {}), {2}: (9, {}), {3}: (10, {}), {4... | custom-call | flops 12884901888 | bytes 26214400 | tf_op jit(solution)/shard_map/ffn/pallas_call | solution.py:402
  411.9 12.5 %convolution_convert_fusion.1 = bf16[2048,1024]{1,0:T(8,128)(2,1)} fusion(bf16[2048,2048]{1,0:T(8,128)(2,1)S(1)} %copy-done.38, bf16[2048,1024]{1,0:T(8,128)(2,1)} %get-tuple-element.157), kind=kOutput, calls=%fused_computation.6 | convolution fusion | flops 8592031744 | bytes 16777216 | tf_op jit(solution)/shard_map/up_grad/dot_general | solution.py:31
  424.5 14.0 %convolution_convert_fusion.2 = bf16[2048,1024]{1,0:T(8,128)(2,1)} fusion(bf16[2048,2048]{1,0:T(8,128)(2,1)} %get-tuple-element.155, bf16[2048,1024]{1,0:T(8,128)(2,1)} %get-tuple-element.156), kind=kOutput, calls=%fused_computation.7 | convolution fusion | flops 8592031744 | bytes 16777216 | tf_op jit(solution)/shard_map/gate_grad/dot_general | solution.py:31
  438.5 12.4 %mid.1 = (f32[256,2048]{1,0:T(8,128)}, bf16[256,2048]{1,0:T(8,128)(2,1)S(1)}, f32[1,2048]{1,0:T(1,128)S(1)}, bf16[8,256,256]{2,1,0:T(8,128)(2,1)}) custom-call(s32[13]{0:T(128)S(1)} %pad_add_fusion.at, bf16[512,1024]{1,0:T(8,128)(2,1)} %constant_dynamic-update-slice_fusion.refs_0_, bf16[512,1024]{1,0:T(8,128)(2,1)} %collective-permute-done.10.refs_1_, ...), custom_call_target="tpu_custom_call" | custom-call | flops 2147483648 | bytes 16777216 | tf_op jit(solution)/shard_map/mid/pallas_call | solution.py:468
  481.5 14.4 %convolution_convert_fusion = bf16[2048,1024]{1,0:T(8,128)(2,1)} fusion(bf16[2048,2048]{1,0:T(8,128)(2,1)} %get-tuple-element.166, bf16[2048,1024]{1,0:T(8,128)(2,1)} %get-tuple-element.167), kind=kOutput, calls=%fused_computation.5 | convolution fusion | flops 8592031744 | bytes 16777216 | tf_op jit(solution)/shard_map/down_grad/dot_general | solution.py:31
  496.0 8.1 %all-to-all-done.2 = bf16[8,256,256]{2,1,0:T(8,128)(2,1)} async-done(((bf16[8,256,256]{2,1,0:T(8,128)(2,1)}), bf16[8,256,256]{2,1,0:T(8,128)(2,1)}, u32[]{:S(2)}, u32[]{:S(2)}) %all-to-all-start.2) | async-done | bytes 1048608 | tf_op jit(solution)/shard_map/d_mixed/all_to_all | solution.py:717
  504.1 33.2 %attn_bwd.1 = (bf16[2048,256]{1,0:T(8,128)(2,1)S(1)}, bf16[2048,128]{1,0:T(8,128)(2,1)S(1)}) custom-call(bf16[2048,256]{1,0:T(8,128)(2,1)S(1)} %get-tuple-element.119.q_ref, bf16[2048,128]{1,0:T(8,128)(2,1)S(1)} %get-tuple-element.120.kv_ref, bf16[2048,256]{1,0:T(8,128)(2,1)} %bitcast.24.do_ref, f32[256,2048]{1,0:T(8,128)} %get-tuple-element.172.ot_ref, ...), custom_call_target="tpu_custom_call" | custom-call | flops 21474836480 | bytes 8388608 | tf_op jit(solution)/shard_map/attn_bwd/pallas_call | solution.py:251
  553.6 18.4 %collective-permute-done.48 = bf16[256,2048]{1,0:T(8,128)(2,1)S(1)} collective-permute-done((bf16[256,2048]{1,0:T(8,128)(2,1)S(1)}, bf16[256,2048]{1,0:T(8,128)(2,1)S(1)}, u32[]{:S(2)}, u32[]{:S(2)}) %collective-permute-start.48) | collective-permute-done | bytes 1048608 | tf_op jit(solution)/shard_map/down_ring/ppermute | solution.py:559
  573.5 20.4 %collective-permute-done.53 = bf16[256,2048]{1,0:T(8,128)(2,1)S(1)} collective-permute-done((bf16[256,2048]{1,0:T(8,128)(2,1)S(1)}, bf16[256,2048]{1,0:T(8,128)(2,1)S(1)}, u32[]{:S(2)}, u32[]{:S(2)}) %collective-permute-start.53) | collective-permute-done | bytes 1048608 | tf_op jit(solution)/shard_map/first_ring/ppermute | solution.py:559
  599.6 19.1 %collective-permute-done.61 = bf16[512,512]{0,1:T(8,128)(2,1)S(1)} collective-permute-done((bf16[512,512]{0,1:T(8,128)(2,1)S(1)}, bf16[512,512]{0,1:T(8,128)(2,1)S(1)}, u32[]{:S(2)}, u32[]{:S(2)}) %collective-permute-start.61) | collective-permute-done | bytes 524320 | tf_op jit(solution)/shard_map/projection_grads/ppermute | solution.py:565
  631.7 24.5 %all-to-all-done.3 = bf16[8,64,512]{2,1,0:T(8,128)(2,1)} async-done(((bf16[8,64,512]{2,1,0:T(8,128)(2,1)}), bf16[8,64,512]{2,1,0:T(8,128)(2,1)}, u32[]{:S(2)}, u32[]{:S(2)}) %all-to-all-start.3) | async-done | bytes 524320 | tf_op jit(solution)/shard_map/projection_grads/all_to_all | solution.py:774
  676.4 10.6 %all-to-all-done.4 = bf16[4,128,1024]{2,1,0:T(8,128)(2,1)} async-done(((bf16[4,128,1024]{2,1,0:T(8,128)(2,1)}), bf16[4,128,1024]{2,1,0:T(8,128)(2,1)}, u32[]{:S(2)}, u32[]{:S(2)}) %all-to-all-start.4) | async-done | bytes 1048608 | tf_op jit(solution)/shard_map/out_grad/all_to_all | solution.py:783
  700.0 8.4 %collective-permute-done.57.ring = bf16[256,2048]{1,0:T(8,128)(2,1)S(1)} collective-permute-done((bf16[256,2048]{1,0:T(8,128)(2,1)}, bf16[256,2048]{1,0:T(8,128)(2,1)S(1)}, u32[]{:S(2)}, u32[]{:S(2)}) %collective-permute-start.57) | collective-permute-done | bytes 1048608 | tf_op jit(solution)/shard_map/first_ring/ppermute | solution.py:559
  (325 shorter events, 185.7 us)
Async XLA Ops:
  7.2 271.7 %all-gather.4.cloned.1.call-start = ((), (), s32[]{:S(2)}) async-start(), calls=%async_computation.9 | async-start | bytes 5242880 | tf_op jit(solution)/shard_map/feed_forward_weights/all_gather | solution.py:587
  8.0 271.0 %all-gather.6.cloned.1.call-start = ((), (), s32[]{:S(2)}) async-start(), calls=%async_computation.10 | async-start | bytes 5242880 | tf_op jit(solution)/shard_map/feed_forward_weights/all_gather | solution.py:587
  8.7 38.6 %collective-permute-start.1 = (bf16[256,2048]{1,0:T(8,128)(2,1)S(1)}, bf16[256,2048]{1,0:T(8,128)(2,1)}, u32[]{:S(2)}, u32[]{:S(2)}) collective-permute-start(bf16[256,2048]{1,0:T(8,128)(2,1)S(1)} %bitcast.78), channel_id=1, source_target_pairs={{0,2},{1,3},{2,6},{3,7},{4,0},{5,1},{6,4},{7,5},{8,10},{9,11},{10,... | collective-permute-start | bytes 3145736 | tf_op jit(solution)/shard_map/tokens_ring/ppermute | solution.py:559
  17.5 261.5 %all-gather.8.cloned.1.call-start = ((), (), s32[]{:S(2)}) async-start(), calls=%async_computation.11 | async-start | bytes 5242880 | tf_op jit(solution)/shard_map/feed_forward_weights/all_gather | solution.py:587
  17.5 81.1 %collective-permute-start.22 = (bf16[256,2048]{1,0:T(8,128)(2,1)S(1)}, bf16[256,2048]{1,0:T(8,128)(2,1)S(1)}, u32[]{:S(2)}, u32[]{:S(2)}) collective-permute-start(bf16[256,2048]{1,0:T(8,128)(2,1)S(1)} %bitcast.79), channel_id=1, source_target_pairs={{0,1},{1,0},{2,3},{3,2},{4,5},{5,4},{6,7},{7,6},{8,9},{9,8},{10,11... | collective-permute-start | bytes 3145736 | tf_op jit(solution)/shard_map/tokens_ring/ppermute | solution.py:562
  47.3 42.2 %collective-permute-start.2 = (bf16[256,2048]{1,0:T(8,128)(2,1)}, bf16[256,2048]{1,0:T(8,128)(2,1)}, u32[]{:S(2)}, u32[]{:S(2)}) collective-permute-start(bf16[256,2048]{1,0:T(8,128)(2,1)} %collective-permute-done.1.mine), channel_id=1, source_target_pairs={{0,2},{1,3},{2,6},{3,7},{4,0},{5,1},{6,4},{7,5},{8,10},{9,11},{10,... | collective-permute-start | bytes 3145736 | tf_op jit(solution)/shard_map/tokens_ring/ppermute | solution.py:559
  51.6 36.8 %collective-permute-start.5 = (bf16[512,512]{0,1:T(8,128)(2,1)S(1)}, bf16[512,512]{0,1:T(8,128)(2,1)}, u32[]{:S(2)}, u32[]{:S(2)}) collective-permute-start(bf16[512,512]{0,1:T(8,128)(2,1)S(1)} %copy.90), channel_id=1, source_target_pairs={{0,24},{8,16},{16,8},{24,0},{1,25},{9,17},{17,9},{25,1},{2,26},{10... | collective-permute-start | bytes 1572872 | tf_op jit(solution)/shard_map/projection_columns/ppermute | solution.py:565
  96.7 38.0 %collective-permute-start.21 = (bf16[256,2048]{1,0:T(8,128)(2,1)}, bf16[256,2048]{1,0:T(8,128)(2,1)}, u32[]{:S(2)}, u32[]{:S(2)}) collective-permute-start(bf16[256,2048]{1,0:T(8,128)(2,1)} %collective-permute-done.1.mine), channel_id=1, source_target_pairs={{0,1},{1,0},{2,3},{3,2},{4,5},{5,4},{6,7},{7,6},{8,9},{9,8},{10,11... | collective-permute-start | bytes 3145736 | tf_op jit(solution)/shard_map/tokens_ring/ppermute | solution.py:562
  98.6 46.7 %collective-permute-start.20 = (bf16[256,2048]{1,0:T(8,128)(2,1)}, bf16[256,2048]{1,0:T(8,128)(2,1)}, u32[]{:S(2)}, u32[]{:S(2)}) collective-permute-start(bf16[256,2048]{1,0:T(8,128)(2,1)} %collective-permute-done.2.mine), channel_id=1, source_target_pairs={{0,1},{1,0},{2,3},{3,2},{4,5},{5,4},{6,7},{7,6},{8,9},{9,8},{10,11... | collective-permute-start | bytes 3145736 | tf_op jit(solution)/shard_map/tokens_ring/ppermute | solution.py:562
  116.0 38.2 %collective-permute-start.19 = (bf16[256,2048]{1,0:T(8,128)(2,1)}, bf16[256,2048]{1,0:T(8,128)(2,1)}, u32[]{:S(2)}, u32[]{:S(2)}) collective-permute-start(bf16[256,2048]{1,0:T(8,128)(2,1)} %collective-permute-done.6.mine), channel_id=1, source_target_pairs={{0,1},{1,0},{2,3},{3,2},{4,5},{5,4},{6,7},{7,6},{8,9},{9,8},{10,11... | collective-permute-start | bytes 3145736 | tf_op jit(solution)/shard_map/tokens_ring/ppermute | solution.py:562
  153.6 37.0 %collective-permute-start.10 = (bf16[512,1024]{1,0:T(8,128)(2,1)}, bf16[512,1024]{1,0:T(8,128)(2,1)}, u32[]{:S(2)}, u32[]{:S(2)}) collective-permute-start(bf16[512,1024]{1,0:T(8,128)(2,1)} %constant_dynamic-update-slice_fusion.refs_0_), channel_id=1, source_target_pairs={{0,8},{8,0},{16,24},{24,16},{1,9},{9,1},{17,25},{25,17},{2,10},{10... | collective-permute-start | bytes 3145736 | tf_op jit(solution)/shard_map/out_weight/ppermute | solution.py:565
  153.6 39.5 %collective-permute-start.11 = (bf16[512,1024]{1,0:T(8,128)(2,1)}, bf16[512,1024]{1,0:T(8,128)(2,1)}, u32[]{:S(2)}, u32[]{:S(2)}) collective-permute-start(bf16[512,1024]{1,0:T(8,128)(2,1)} %constant_dynamic-update-slice_fusion.refs_0_), channel_id=1, source_target_pairs={{0,16},{8,24},{16,0},{24,8},{1,17},{9,25},{17,1},{25,9},{2,18},{10... | collective-permute-start | bytes 3145736 | tf_op jit(solution)/shard_map/out_weight/ppermute | solution.py:565
  180.5 40.3 %all-to-all-start.1 = ((bf16[8,256,256]{2,1,0:T(8,128)(2,1)}), bf16[8,256,256]{2,1,0:T(8,128)(2,1)}, u32[]{:S(2)}, u32[]{:S(2)}) async-start(bf16[8,256,256]{2,1,0:T(8,128)(2,1)} %bitcast.23), calls=%async_computation.1 | async-start | bytes 2097152 | tf_op jit(solution)/shard_map/mixed/all_to_all | solution.py:662
  184.8 446.9 %reduce-scatter.5.cloned.1.call-start = ((), (), s32[]{:S(2)}) async-start(), calls=%async_computation.12 | async-start | bytes 5242880 | tf_op jit(solution)/shard_map/out_grad/reduce_scatter | solution.py:590
  231.0 47.9 %collective-permute-start.31 = (bf16[256,2048]{1,0:T(8,128)(2,1)}, bf16[256,2048]{1,0:T(8,128)(2,1)}, u32[]{:S(2)}, u32[]{:S(2)}) collective-permute-start(bf16[256,2048]{1,0:T(8,128)(2,1)} %collective-permute-done.23.refs_2_), channel_id=1, source_target_pairs={{0,2},{1,3},{2,6},{3,7},{4,0},{5,1},{6,4},{7,5},{8,10},{9,11},{10,... | collective-permute-start | bytes 3145736 | tf_op jit(solution)/shard_map/cotangent_ring/ppermute | solution.py:559
  231.9 47.1 %collective-permute-start.28 = (bf16[256,2048]{1,0:T(8,128)(2,1)S(1)}, bf16[256,2048]{1,0:T(8,128)(2,1)}, u32[]{:S(2)}, u32[]{:S(2)}) collective-permute-start(bf16[256,2048]{1,0:T(8,128)(2,1)S(1)} %bitcast.94), channel_id=1, source_target_pairs={{0,1},{1,0},{2,3},{3,2},{4,5},{5,4},{6,7},{7,6},{8,9},{9,8},{10,11... | collective-permute-start | bytes 3145736 | tf_op jit(solution)/shard_map/cotangent_ring/ppermute | solution.py:562
  231.9 47.1 %collective-permute-start.27 = (bf16[256,2048]{1,0:T(8,128)(2,1)}, bf16[256,2048]{1,0:T(8,128)(2,1)}, u32[]{:S(2)}, u32[]{:S(2)}) collective-permute-start(bf16[256,2048]{1,0:T(8,128)(2,1)} %get-tuple-element.125.refs_0_), channel_id=1, source_target_pairs={{0,1},{1,0},{2,3},{3,2},{4,5},{5,4},{6,7},{7,6},{8,9},{9,8},{10,11... | collective-permute-start | bytes 3145736 | tf_op jit(solution)/shard_map/normed_ring/ppermute | solution.py:562
  232.4 72.6 %collective-permute-start.26 = (bf16[256,2048]{1,0:T(8,128)(2,1)}, bf16[256,2048]{1,0:T(8,128)(2,1)}, u32[]{:S(2)}, u32[]{:S(2)}) collective-permute-start(bf16[256,2048]{1,0:T(8,128)(2,1)} %collective-permute-done.23.refs_2_), channel_id=1, source_target_pairs={{0,1},{1,0},{2,3},{3,2},{4,5},{5,4},{6,7},{7,6},{8,9},{9,8},{10,11... | collective-permute-start | bytes 3145736 | tf_op jit(solution)/shard_map/cotangent_ring/ppermute | solution.py:562
  331.1 48.5 %collective-permute-start.30 = (bf16[256,2048]{1,0:T(8,128)(2,1)S(1)}, bf16[256,2048]{1,0:T(8,128)(2,1)S(1)}, u32[]{:S(2)}, u32[]{:S(2)}) collective-permute-start(bf16[256,2048]{1,0:T(8,128)(2,1)S(1)} %add_convert_fusion.8), channel_id=1, source_target_pairs={{0,2},{1,3},{2,6},{3,7},{4,0},{5,1},{6,4},{7,5},{8,10},{9,11},{10,... | collective-permute-start | bytes 3145736 | tf_op jit(solution)/shard_map/back_ring/ppermute | solution.py:559
  331.9 47.7 %collective-permute-start.38 = (bf16[256,2048]{1,0:T(8,128)(2,1)S(1)}, bf16[256,2048]{1,0:T(8,128)(2,1)S(1)}, u32[]{:S(2)}, u32[]{:S(2)}) collective-permute-start(bf16[256,2048]{1,0:T(8,128)(2,1)S(1)} %collective-permute-done.33.refs_0_), channel_id=1, source_target_pairs={{0,2},{1,3},{2,6},{3,7},{4,0},{5,1},{6,4},{7,5},{8,10},{9,11},{10,... | collective-permute-start | bytes 3145736 | tf_op jit(solution)/shard_map/normed_ring/ppermute | solution.py:559
  465.1 225.9 %reduce-scatter.9.cloned.1.call-start = ((), (), s32[]{:S(2)}) async-start(), calls=%async_computation.14 | async-start | bytes 5242880 | tf_op jit(solution)/shard_map/up_grad/reduce_scatter | solution.py:590
  465.7 225.3 %reduce-scatter.7.cloned.1.call-start = ((), (), s32[]{:S(2)}) async-start(), calls=%async_computation.13 | async-start | bytes 5242880 | tf_op jit(solution)/shard_map/gate_grad/reduce_scatter | solution.py:590
  472.1 70.6 %collective-permute-start.47 = (bf16[256,2048]{1,0:T(8,128)(2,1)}, bf16[256,2048]{1,0:T(8,128)(2,1)}, u32[]{:S(2)}, u32[]{:S(2)}) collective-permute-start(bf16[256,2048]{1,0:T(8,128)(2,1)} %get-tuple-element.171), channel_id=1, source_target_pairs={{0,1},{1,0},{2,3},{3,2},{4,5},{5,4},{6,7},{7,6},{8,9},{9,8},{10,11... | collective-permute-start | bytes 3145736 | tf_op jit(solution)/shard_map/feed_forward_pair/ppermute | solution.py:562
  472.6 123.8 %collective-permute-start.49 = (bf16[256,2048]{1,0:T(8,128)(2,1)}, bf16[256,2048]{1,0:T(8,128)(2,1)}, u32[]{:S(2)}, u32[]{:S(2)}) collective-permute-start(bf16[256,2048]{1,0:T(8,128)(2,1)} %get-tuple-element.177), channel_id=1, source_target_pairs={{0,1},{1,0},{2,3},{3,2},{4,5},{5,4},{6,7},{7,6},{8,9},{9,8},{10,11... | collective-permute-start | bytes 3145736 | tf_op jit(solution)/shard_map/feed_forward_pair/ppermute | solution.py:562
  477.0 217.0 %reduce-scatter.11.cloned.1.call-start = ((), (), s32[]{:S(2)}) async-start(), calls=%async_computation.15 | async-start | bytes 5242880 | tf_op jit(solution)/shard_map/down_grad/reduce_scatter | solution.py:590
  479.6 63.1 %collective-permute-start.44 = (bf16[256,2048]{1,0:T(8,128)(2,1)}, bf16[256,2048]{1,0:T(8,128)(2,1)}, u32[]{:S(2)}, u32[]{:S(2)}) collective-permute-start(bf16[256,2048]{1,0:T(8,128)(2,1)} %add_convert_fusion.5), channel_id=1, source_target_pairs={{0,2},{1,3},{2,6},{3,7},{4,0},{5,1},{6,4},{7,5},{8,10},{9,11},{10,... | collective-permute-start | bytes 3145736 | tf_op jit(solution)/shard_map/down_ring/ppermute | solution.py:559
  542.7 85.8 %collective-permute-start.56 = (bf16[256,2048]{1,0:T(8,128)(2,1)}, bf16[256,2048]{1,0:T(8,128)(2,1)}, u32[]{:S(2)}, u32[]{:S(2)}) collective-permute-start(bf16[256,2048]{1,0:T(8,128)(2,1)} %convolution_convert_fusion.8), channel_id=1, source_target_pairs={{0,1},{1,0},{2,3},{3,2},{4,5},{5,4},{6,7},{7,6},{8,9},{9,8},{10,11... | collective-permute-start | bytes 3145736 | tf_op jit(solution)/shard_map/first_ring/ppermute | solution.py:562
  548.2 45.7 %collective-permute-start.53 = (bf16[256,2048]{1,0:T(8,128)(2,1)S(1)}, bf16[256,2048]{1,0:T(8,128)(2,1)S(1)}, u32[]{:S(2)}, u32[]{:S(2)}) collective-permute-start(bf16[256,2048]{1,0:T(8,128)(2,1)S(1)} %fusion.6), channel_id=1, source_target_pairs={{0,2},{1,3},{2,6},{3,7},{4,0},{5,1},{6,4},{7,5},{8,10},{9,11},{10,... | collective-permute-start | bytes 3145736 | tf_op jit(solution)/shard_map/first_ring/ppermute | solution.py:559
  599.1 61.6 %collective-permute-start.51 = (bf16[256,2048]{1,0:T(8,128)(2,1)}, bf16[256,2048]{1,0:T(8,128)(2,1)}, u32[]{:S(2)}, u32[]{:S(2)}) collective-permute-start(bf16[256,2048]{1,0:T(8,128)(2,1)} %get-tuple-element.179), channel_id=1, source_target_pairs={{0,1},{1,0},{2,3},{3,2},{4,5},{5,4},{6,7},{7,6},{8,9},{9,8},{10,11... | collective-permute-start | bytes 3145736 | tf_op jit(solution)/shard_map/feed_forward_pair/ppermute | solution.py:562
  599.1 100.8 %collective-permute-start.58 = (bf16[256,2048]{1,0:T(8,128)(2,1)}, bf16[256,2048]{1,0:T(8,128)(2,1)S(1)}, u32[]{:S(2)}, u32[]{:S(2)}) collective-permute-start(bf16[256,2048]{1,0:T(8,128)(2,1)} %convolution_convert_fusion.6), channel_id=1, source_target_pairs={{0,1},{1,0},{2,3},{3,2},{4,5},{5,4},{6,7},{7,6},{8,9},{9,8},{10,11... | collective-permute-start | bytes 3145736 | tf_op jit(solution)/shard_map/first_ring/ppermute | solution.py:562
  618.8 41.9 %collective-permute-start.50 = (bf16[256,2048]{1,0:T(8,128)(2,1)}, bf16[256,2048]{1,0:T(8,128)(2,1)}, u32[]{:S(2)}, u32[]{:S(2)}) collective-permute-start(bf16[256,2048]{1,0:T(8,128)(2,1)} %add_convert_fusion.3), channel_id=1, source_target_pairs={{0,2},{1,3},{2,6},{3,7},{4,0},{5,1},{6,4},{7,5},{8,10},{9,11},{10,... | collective-permute-start | bytes 3145736 | tf_op jit(solution)/shard_map/down_ring/ppermute | solution.py:559
  664.5 43.9 %collective-permute-start.57 = (bf16[256,2048]{1,0:T(8,128)(2,1)}, bf16[256,2048]{1,0:T(8,128)(2,1)S(1)}, u32[]{:S(2)}, u32[]{:S(2)}) collective-permute-start(bf16[256,2048]{1,0:T(8,128)(2,1)} %add_convert_fusion), channel_id=1, source_target_pairs={{0,2},{1,3},{2,6},{3,7},{4,0},{5,1},{6,4},{7,5},{8,10},{9,11},{10,... | collective-permute-start | bytes 3145736 | tf_op jit(solution)/shard_map/first_ring/ppermute | solution.py:559
  (84 other events, 1250.6 us)
Sparse Core Ops, SparseCore 0:
  9.9 69.8 all-gather.3
  81.7 57.6 all-gather.5
  141.2 78.6 all-gather.7
  465.2 50.3 reduce-scatter.4
  518.4 52.5 reduce-scatter.8
  573.8 64.4 reduce-scatter.6
  641.3 52.5 reduce-scatter.10

commit v4 on v3

--- a/solution.py
+++ b/solution.py
@@ -631,8 +631,23 @@
         keep = cols_at(w_out, core_at * half, half)
         give = cols_at(w_out, (1 - core_at) * half, half)
         chip_rows = [pair_sides(keep, step_swap(give))]
-        for s in range(1, chips):
-            chip_rows.append(step_ring(after(chip_rows[0], x_mine[-1]) if s == 1 else chip_rows[-1]))
+
+    cos, sin = rope_tables(length)
+    held = ()
+
+    def project(s, ahead):
+        other = after(x_other[s], ahead)
+        return qkv_call(
+            pair_at[s], x_mine[s], other, gain_one, cols_all, cos, sin, width, length, held
+        )
+
+    for s in range(min(2, chips)):
+        held = project(s, chip_rows[0])
+
+    with jax.named_scope("out_weight"):
+        chip_rows.append(step_ring(after(chip_rows[0], x_mine[-1], held[0])))
+        for _ in range(2, chips):
+            chip_rows.append(step_ring(chip_rows[-1]))
         out_rows = jnp.zeros((dp_rows, half), bf16)
         for s in range(chips):
             out_rows = lax.dynamic_update_slice_in_dim(out_rows, chip_rows[s], chunk[s] * 2 * own_rows, 0)
@@ -643,14 +658,10 @@
     with jax.named_scope("feed_forward_weights"):
         gate_full, up_full, down_full = full_weight(w_gate), full_weight(w_up), full_weight(w_down)
 
-    cos, sin = rope_tables(length)
-
-    held = ()
-    for s in range(chips):
-        held = qkv_call(
-            pair_at[s], x_mine[s], after(x_other[s], chip_rows[s]), gain_one, cols_all, cos, sin, width, length, held
-        )
+    for s in range(2, chips):
+        held = project(s, chip_rows[s - 1])
     normed, queries, keys_values = held
+    queries = after(queries, chip_rows[-1])
 
     with jax.named_scope("cotangent_ring"):
         c_mine = [cot_own, step_ring(after(cot_own, chip_rows[-1]))]

time: 730 us -> 730 us (level)
  waiting for transfers between devices: 303 us -> 290 us
  matrix products: 60.1 us -> 68.7 us
    ppermute x21, waiting for transfers between devices: 144 us -> 164 us  [step_ring(): return lax.ppermute(x, 'seq', ring)]
    all_to_all x1, waiting for transfers between devices: 25.9 us -> 6.05 us  [shards(): lax.all_to_all(jnp.transpose(own_cols, (1, 0, 2)), 'seq', 0, 0, tiled=True)]
    ppermute x10, waiting for transfers between devices: 76.6 us -> 61.3 us  [step_dp(): return lax.ppermute(x, 'dp', [(i, i ^ k) for i in range(dp_count)])]
    dot_general x12, matrix products: 55.1 us -> 63.7 us  [mm(): return lax.dot_general(a, b, dims, preferred_element_type=f32)]
  transfers between devices with their start and end apart: 75 -> 75, of which waited for: 27 -> 30; matrix products, arithmetic and copies ran while one was open for 17% -> 19% of each run, Pallas kernels for 25% -> 25%
where the time goes in v4:
time: 730 us; the launch traced here: 721 us
  waiting for transfers between devices  290 us (40%)
  Pallas kernels  192 us (26%)
  matrix products  68.7 us (9%)
  starting transfers between devices  61.8 us (8%)
  other arithmetic  46.2 us (6%)
  local copies, waits for them, and re-layouts  36 us (5%)
  between operations  26.7 us (4%)
    ppermute x21, waiting for transfers between devices, step_ring(): return lax.ppermute(x, 'seq', ring)  164 us
    pallas_call x4, Pallas kernels, ffn_call(): pl.pallas_call(functools.partial(ffn_kernel, len(w_gate)), grid=(units //...  87 us
    dot_general x12, matrix products, mm(): return lax.dot_general(a, b, dims, preferred_element_type=f32)  63.7 us
    ppermute x10, waiting for transfers between devices, step_dp(): return lax.ppermute(x, 'dp', [(i, i ^ k) for i in range(dp_count)])  61.3 us
    pallas_call x1, Pallas kernels, attn_bwd(): pl.pallas_call(functools.partial(bwd_kernel, bq, share), grid=(length //...  33.2 us
    pallas_call x4, Pallas kernels, qkv_call(): pl.pallas_call(functools.partial(qkv_kernel, width), grid_spec=pltpu.Pref...  25 us
    all_to_all x1, waiting for transfers between devices, shards(): lax.all_to_all(total.reshape(groups, own_rows, cols), 'seq', 0, 0, tiled=...  24 us
    pallas_call x1, Pallas kernels, attn_fwd(): pl.pallas_call(functools.partial(fwd_kernel, bq, share), grid=(length //...  19.9 us
  transfers between devices with their start and end apart: 75, of which 30 were waited for; matrix products, arithmetic and copies ran while one was open for 19% of the time, Pallas kernels for 25%

profile of v4, /device:TPU:0, one launch (start us, length us, event | category | flops | bytes accessed | tf_op | source)
XLA Modules:
  0.0 721.0 jit_solution(17908915865177305261)
XLA Ops:
  32.8 22.0 %collective-permute-done.1.mine = bf16[256,2048]{1,0:T(8,128)(2,1)} collective-permute-done((bf16[256,2048]{1,0:T(8,128)(2,1)S(1)}, bf16[256,2048]{1,0:T(8,128)(2,1)}, u32[]{:S(2)}, u32[]{:S(2)}) %collective-permute-start.1) | collective-permute-done | bytes 1048608 | tf_op jit(solution)/shard_map/tokens_ring/ppermute | solution.py:559
  65.5 11.1 %collective-permute-done.3 = bf16[512,512]{0,1:T(8,128)(2,1)S(1)} collective-permute-done((bf16[512,512]{0,1:T(8,128)(2,1)S(1)}, bf16[512,512]{0,1:T(8,128)(2,1)S(1)}, u32[]{:S(2)}, u32[]{:S(2)}) %collective-permute-start.3) | collective-permute-done | bytes 524320 | tf_op jit(solution)/shard_map/projection_columns/ppermute | solution.py:565
  79.8 9.8 %collective-permute-done.5 = bf16[512,512]{0,1:T(8,128)(2,1)} collective-permute-done((bf16[512,512]{0,1:T(8,128)(2,1)S(1)}, bf16[512,512]{0,1:T(8,128)(2,1)}, u32[]{:S(2)}, u32[]{:S(2)}) %collective-permute-start.5) | collective-permute-done | bytes 524320 | tf_op jit(solution)/shard_map/projection_columns/ppermute | solution.py:565
  106.8 9.7 %collective-permute-done.6.mine = bf16[256,2048]{1,0:T(8,128)(2,1)} collective-permute-done((bf16[256,2048]{1,0:T(8,128)(2,1)}, bf16[256,2048]{1,0:T(8,128)(2,1)}, u32[]{:S(2)}, u32[]{:S(2)}) %collective-permute-start.6) | collective-permute-done | bytes 1048608 | tf_op jit(solution)/shard_map/tokens_ring/ppermute | solution.py:559
  116.5 6.4 qkv.5
  123.8 8.8 %collective-permute-done.9 = bf16[128,1024]{1,0:T(8,128)(2,1)S(1)} collective-permute-done((bf16[128,1024]{1,0:T(8,128)(2,1)S(1)}, bf16[128,1024]{1,0:T(8,128)(2,1)S(1)}, u32[]{:S(2)}, u32[]{:S(2)}) %collective-permute-start.9) | collective-permute-done | bytes 262176 | tf_op jit(solution)/shard_map/out_weight/ppermute | solution.py:559
  133.4 7.9 %collective-permute-done.10 = bf16[128,1024]{1,0:T(8,128)(2,1)S(1)} collective-permute-done((bf16[128,1024]{1,0:T(8,128)(2,1)S(1)}, bf16[128,1024]{1,0:T(8,128)(2,1)S(1)}, u32[]{:S(2)}, u32[]{:S(2)}) %collective-permute-start.10) | collective-permute-done | bytes 262176 | tf_op jit(solution)/shard_map/out_weight/ppermute | solution.py:559
  144.1 6.3 qkv.6
  158.1 6.5 qkv.7
  164.6 19.9 %attn_fwd.1 = (bf16[2048,256]{1,0:T(8,128)(2,1)}, f32[256,2048]{1,0:T(8,128)}, f32[8,2048]{1,0:T(8,128)S(1)}) custom-call(bf16[2048,256]{1,0:T(8,128)(2,1)S(1)} %get-tuple-element.121.q_ref, bf16[2048,128]{1,0:T(8,128)(2,1)S(1)} %get-tuple-element.122.kv_ref), custom_call_target="tpu_custom_call" | custom-call | flops 8589934592 | bytes 4194304 | tf_op jit(solution)/shard_map/attn_fwd/pallas_call | solution.py:161
  189.6 14.2 %collective-permute-done.12.refs_1_ = bf16[512,1024]{1,0:T(8,128)(2,1)} collective-permute-done((bf16[512,1024]{1,0:T(8,128)(2,1)}, bf16[512,1024]{1,0:T(8,128)(2,1)}, u32[]{:S(2)}, u32[]{:S(2)}) %collective-permute-start.12) | collective-permute-done | bytes 1048608 | tf_op jit(solution)/shard_map/out_weight/ppermute | solution.py:565
  208.3 6.1 collective-permute-done.14.refs_3_
  217.4 9.2 %out_norm.1 = (f32[256,2048]{1,0:T(8,128)}, bf16[256,2048]{1,0:T(8,128)(2,1)}) custom-call(s32[13]{0:T(128)S(1)} %pad_add_fusion.at, bf16[512,1024]{1,0:T(8,128)(2,1)} %constant_dynamic-update-slice_fusion.refs_0_, bf16[512,1024]{1,0:T(8,128)(2,1)} %collective-permute-done.12.refs_1_, bf16[512,1024]{1,0:T(8,128)(2,1)} %collective-permute-done.13.refs_2_, ...), custom_call_target="tpu_custom_call" | custom-call | flops 2147483648 | bytes 12582912 | tf_op jit(solution)/shard_map/out_norm/pallas_call | solution.py:330
  228.3 25.5 %collective-permute-done.24.refs_0_ = bf16[256,2048]{1,0:T(8,128)(2,1)} collective-permute-done((bf16[256,2048]{1,0:T(8,128)(2,1)}, bf16[256,2048]{1,0:T(8,128)(2,1)}, u32[]{:S(2)}, u32[]{:S(2)}) %collective-permute-start.24) | collective-permute-done | bytes 1048608 | tf_op jit(solution)/shard_map/normed_ring/ppermute | solution.py:559
  253.9 21.6 %collective-permute-done.31.refs_2_ = bf16[256,2048]{1,0:T(8,128)(2,1)} collective-permute-done((bf16[256,2048]{1,0:T(8,128)(2,1)}, bf16[256,2048]{1,0:T(8,128)(2,1)}, u32[]{:S(2)}, u32[]{:S(2)}) %collective-permute-start.31) | collective-permute-done | bytes 1048608 | tf_op jit(solution)/shard_map/cotangent_ring/ppermute | solution.py:559
  275.6 22.0 %ffn.4 = (bf16[2048,2048]{1,0:T(8,128)(2,1)}, bf16[2048,2048]{1,0:T(8,128)(2,1)}, bf16[2048,1024]{1,0:T(8,128)(2,1)}, bf16[2048,1024]{1,0:T(8,128)(2,1)}, bf16[2...) custom-call(bf16[256,2048]{1,0:T(8,128)(2,1)} %get-tuple-element.127, ...), custom_call_target="tpu_custom_call" | custom-call | flops 12884901888 | bytes 26214400 | tf_op jit(solution)/shard_map/ffn/pallas_call | solution.py:402
  301.3 21.7 %ffn.5 = (bf16[2048,2048]{1,0:T(8,128)(2,1)}, bf16[2048,2048]{1,0:T(8,128)(2,1)}, bf16[2048,1024]{1,0:T(8,128)(2,1)}, bf16[2048,1024]{1,0:T(8,128)(2,1)}, bf16[2...) custom-call(bf16[256,2048]{1,0:T(8,128)(2,1)} %collective-permute-do, ...), custom_call_target="tpu_custom_call", output_to_operand_aliasing={{0}: (7, {}), {1}: (8, {}), {2}: (9, {}), {3}: (10, {}), {4... | custom-call | flops 12884901888 | bytes 26214400 | tf_op jit(solution)/shard_map/ffn/pallas_call | solution.py:402
  331.8 21.6 %ffn.6 = (bf16[2048,2048]{1,0:T(8,128)(2,1)}, bf16[2048,2048]{1,0:T(8,128)(2,1)}, bf16[2048,1024]{1,0:T(8,128)(2,1)}, bf16[2048,1024]{1,0:T(8,128)(2,1)}, bf16[2...) custom-call(bf16[256,2048]{1,0:T(8,128)(2,1)} %copy-done.29, ...), custom_call_target="tpu_custom_call", output_to_operand_aliasing={{0}: (7, {}), {1}: (8, {}), {2}: (9, {}), {3}: (10, {}), {4... | custom-call | flops 12884901888 | bytes 26214400 | tf_op jit(solution)/shard_map/ffn/pallas_call | solution.py:402
  354.0 22.2 %collective-permute-done.38.refs_0_ = bf16[256,2048]{1,0:T(8,128)(2,1)S(1)} collective-permute-done((bf16[256,2048]{1,0:T(8,128)(2,1)S(1)}, bf16[256,2048]{1,0:T(8,128)(2,1)S(1)}, u32[]{:S(2)}, u32[]{:S(2)}) %collective-permute-start.38) | collective-permute-done | bytes 1048608 | tf_op jit(solution)/shard_map/normed_ring/ppermute | solution.py:559
  380.2 21.7 %ffn.7 = (bf16[2048,2048]{1,0:T(8,128)(2,1)}, bf16[2048,2048]{1,0:T(8,128)(2,1)}, bf16[2048,1024]{1,0:T(8,128)(2,1)}, bf16[2048,1024]{1,0:T(8,128)(2,1)}, bf16[2...) custom-call(bf16[256,2048]{1,0:T(8,128)(2,1)} %copy-done.30, ...), custom_call_target="tpu_custom_call", output_to_operand_aliasing={{0}: (7, {}), {1}: (8, {}), {2}: (9, {}), {3}: (10, {}), {4... | custom-call | flops 12884901888 | bytes 26214400 | tf_op jit(solution)/shard_map/ffn/pallas_call | solution.py:402
  407.5 12.5 %convolution_convert_fusion.1 = bf16[2048,1024]{1,0:T(8,128)(2,1)} fusion(bf16[2048,2048]{1,0:T(8,128)(2,1)S(1)} %copy-done.36, bf16[2048,1024]{1,0:T(8,128)(2,1)} %get-tuple-element.159), kind=kOutput, calls=%fused_computation.6 | convolution fusion | flops 8592031744 | bytes 16777216 | tf_op jit(solution)/shard_map/up_grad/dot_general | solution.py:31
  420.0 14.0 %convolution_convert_fusion.2 = bf16[2048,1024]{1,0:T(8,128)(2,1)} fusion(bf16[2048,2048]{1,0:T(8,128)(2,1)} %get-tuple-element.157, bf16[2048,1024]{1,0:T(8,128)(2,1)} %get-tuple-element.158), kind=kOutput, calls=%fused_computation.7 | convolution fusion | flops 8592031744 | bytes 16777216 | tf_op jit(solution)/shard_map/gate_grad/dot_general | solution.py:31
  434.0 12.3 %mid.1 = (f32[256,2048]{1,0:T(8,128)}, bf16[256,2048]{1,0:T(8,128)(2,1)S(1)}, f32[1,2048]{1,0:T(1,128)S(1)}, bf16[8,256,256]{2,1,0:T(8,128)(2,1)}) custom-call(s32[13]{0:T(128)S(1)} %pad_add_fusion.at, bf16[512,1024]{1,0:T(8,128)(2,1)} %constant_dynamic-update-slice_fusion.refs_0_, bf16[512,1024]{1,0:T(8,128)(2,1)} %collective-permute-done.12.refs_1_, ...), custom_call_target="tpu_custom_call" | custom-call | flops 2147483648 | bytes 16777216 | tf_op jit(solution)/shard_map/mid/pallas_call | solution.py:468
  477.2 14.5 %convolution_convert_fusion = bf16[2048,1024]{1,0:T(8,128)(2,1)} fusion(bf16[2048,2048]{1,0:T(8,128)(2,1)} %get-tuple-element.168, bf16[2048,1024]{1,0:T(8,128)(2,1)} %get-tuple-element.169), kind=kOutput, calls=%fused_computation.5 | convolution fusion | flops 8592031744 | bytes 16777216 | tf_op jit(solution)/shard_map/down_grad/dot_general | solution.py:31
  491.7 7.9 %all-to-all-done.2 = bf16[8,256,256]{2,1,0:T(8,128)(2,1)} async-done(((bf16[8,256,256]{2,1,0:T(8,128)(2,1)}), bf16[8,256,256]{2,1,0:T(8,128)(2,1)}, u32[]{:S(2)}, u32[]{:S(2)}) %all-to-all-start.2) | async-done | bytes 1048608 | tf_op jit(solution)/shard_map/d_mixed/all_to_all | solution.py:728
  499.7 33.2 %attn_bwd.1 = (bf16[2048,256]{1,0:T(8,128)(2,1)S(1)}, bf16[2048,128]{1,0:T(8,128)(2,1)S(1)}) custom-call(bf16[2048,256]{1,0:T(8,128)(2,1)S(1)} %get-tuple-element.121.q_ref, bf16[2048,128]{1,0:T(8,128)(2,1)S(1)} %get-tuple-element.122.kv_ref, bf16[2048,256]{1,0:T(8,128)(2,1)} %bitcast.24.do_ref, f32[256,2048]{1,0:T(8,128)} %get-tuple-element.174.ot_ref, ...), custom_call_target="tpu_custom_call" | custom-call | flops 21474836480 | bytes 8388608 | tf_op jit(solution)/shard_map/attn_bwd/pallas_call | solution.py:251
  557.3 13.3 %collective-permute-done.48 = bf16[256,2048]{1,0:T(8,128)(2,1)S(1)} collective-permute-done((bf16[256,2048]{1,0:T(8,128)(2,1)S(1)}, bf16[256,2048]{1,0:T(8,128)(2,1)S(1)}, u32[]{:S(2)}, u32[]{:S(2)}) %collective-permute-start.48) | collective-permute-done | bytes 1048608 | tf_op jit(solution)/shard_map/down_ring/ppermute | solution.py:559
  573.5 19.0 %collective-permute-done.53 = bf16[256,2048]{1,0:T(8,128)(2,1)S(1)} collective-permute-done((bf16[256,2048]{1,0:T(8,128)(2,1)S(1)}, bf16[256,2048]{1,0:T(8,128)(2,1)S(1)}, u32[]{:S(2)}, u32[]{:S(2)}) %collective-permute-start.53) | collective-permute-done | bytes 1048608 | tf_op jit(solution)/shard_map/first_ring/ppermute | solution.py:559
  599.4 19.1 %collective-permute-done.61 = bf16[512,512]{0,1:T(8,128)(2,1)S(1)} collective-permute-done((bf16[512,512]{0,1:T(8,128)(2,1)S(1)}, bf16[512,512]{0,1:T(8,128)(2,1)S(1)}, u32[]{:S(2)}, u32[]{:S(2)}) %collective-permute-start.61) | collective-permute-done | bytes 524320 | tf_op jit(solution)/shard_map/projection_grads/ppermute | solution.py:565
  631.4 24.0 %all-to-all-done.3 = bf16[8,64,512]{2,1,0:T(8,128)(2,1)} async-done(((bf16[8,64,512]{2,1,0:T(8,128)(2,1)}), bf16[8,64,512]{2,1,0:T(8,128)(2,1)}, u32[]{:S(2)}, u32[]{:S(2)}) %all-to-all-start.3) | async-done | bytes 524320 | tf_op jit(solution)/shard_map/projection_grads/all_to_all | solution.py:785
  675.6 10.8 %all-to-all-done.4 = bf16[4,128,1024]{2,1,0:T(8,128)(2,1)} async-done(((bf16[4,128,1024]{2,1,0:T(8,128)(2,1)}), bf16[4,128,1024]{2,1,0:T(8,128)(2,1)}, u32[]{:S(2)}, u32[]{:S(2)}) %all-to-all-start.4) | async-done | bytes 1048608 | tf_op jit(solution)/shard_map/out_grad/all_to_all | solution.py:794
  700.1 7.6 %collective-permute-done.57.ring = bf16[256,2048]{1,0:T(8,128)(2,1)S(1)} collective-permute-done((bf16[256,2048]{1,0:T(8,128)(2,1)}, bf16[256,2048]{1,0:T(8,128)(2,1)S(1)}, u32[]{:S(2)}, u32[]{:S(2)}) %collective-permute-start.57) | collective-permute-done | bytes 1048608 | tf_op jit(solution)/shard_map/first_ring/ppermute | solution.py:559
  (321 shorter events, 211.5 us)
Async XLA Ops:
  7.2 268.3 %all-gather.4.cloned.1.call-start = ((), (), s32[]{:S(2)}) async-start(), calls=%async_computation.9 | async-start | bytes 5242880 | tf_op jit(solution)/shard_map/feed_forward_weights/all_gather | solution.py:587
  8.0 267.6 %all-gather.6.cloned.1.call-start = ((), (), s32[]{:S(2)}) async-start(), calls=%async_computation.10 | async-start | bytes 5242880 | tf_op jit(solution)/shard_map/feed_forward_weights/all_gather | solution.py:587
  8.7 86.0 %collective-permute-start.8 = (bf16[256,2048]{1,0:T(8,128)(2,1)S(1)}, bf16[256,2048]{1,0:T(8,128)(2,1)S(1)}, u32[]{:S(2)}, u32[]{:S(2)}) collective-permute-start(bf16[256,2048]{1,0:T(8,128)(2,1)S(1)} %bitcast.78), channel_id=1, source_target_pairs={{0,1},{1,0},{2,3},{3,2},{4,5},{5,4},{6,7},{7,6},{8,9},{9,8},{10,11... | collective-permute-start | bytes 3145736 | tf_op jit(solution)/shard_map/tokens_ring/ppermute | solution.py:562
  16.9 258.7 %all-gather.8.cloned.1.call-start = ((), (), s32[]{:S(2)}) async-start(), calls=%async_computation.11 | async-start | bytes 5242880 | tf_op jit(solution)/shard_map/feed_forward_weights/all_gather | solution.py:587
  17.0 37.9 %collective-permute-start.1 = (bf16[256,2048]{1,0:T(8,128)(2,1)S(1)}, bf16[256,2048]{1,0:T(8,128)(2,1)}, u32[]{:S(2)}, u32[]{:S(2)}) collective-permute-start(bf16[256,2048]{1,0:T(8,128)(2,1)S(1)} %bitcast.79), channel_id=1, source_target_pairs={{0,2},{1,3},{2,6},{3,7},{4,0},{5,1},{6,4},{7,5},{8,10},{9,11},{10,... | collective-permute-start | bytes 3145736 | tf_op jit(solution)/shard_map/tokens_ring/ppermute | solution.py:559
  54.8 36.6 %collective-permute-start.2 = (bf16[256,2048]{1,0:T(8,128)(2,1)}, bf16[256,2048]{1,0:T(8,128)(2,1)}, u32[]{:S(2)}, u32[]{:S(2)}) collective-permute-start(bf16[256,2048]{1,0:T(8,128)(2,1)} %collective-permute-done.1.mine), channel_id=1, source_target_pairs={{0,2},{1,3},{2,6},{3,7},{4,0},{5,1},{6,4},{7,5},{8,10},{9,11},{10,... | collective-permute-start | bytes 3145736 | tf_op jit(solution)/shard_map/tokens_ring/ppermute | solution.py:559
  99.8 44.3 %collective-permute-start.22 = (bf16[256,2048]{1,0:T(8,128)(2,1)}, bf16[256,2048]{1,0:T(8,128)(2,1)}, u32[]{:S(2)}, u32[]{:S(2)}) collective-permute-start(bf16[256,2048]{1,0:T(8,128)(2,1)} %collective-permute-done.2.mine), channel_id=1, source_target_pairs={{0,1},{1,0},{2,3},{3,2},{4,5},{5,4},{6,7},{7,6},{8,9},{9,8},{10,11... | collective-permute-start | bytes 3145736 | tf_op jit(solution)/shard_map/tokens_ring/ppermute | solution.py:562
  116.5 41.5 %collective-permute-start.21 = (bf16[256,2048]{1,0:T(8,128)(2,1)}, bf16[256,2048]{1,0:T(8,128)(2,1)S(1)}, u32[]{:S(2)}, u32[]{:S(2)}) collective-permute-start(bf16[256,2048]{1,0:T(8,128)(2,1)} %collective-permute-done.6.mine), channel_id=1, source_target_pairs={{0,1},{1,0},{2,3},{3,2},{4,5},{5,4},{6,7},{7,6},{8,9},{9,8},{10,11... | collective-permute-start | bytes 3145736 | tf_op jit(solution)/shard_map/tokens_ring/ppermute | solution.py:562
  151.2 33.3 %collective-permute-start.23 = (bf16[256,2048]{1,0:T(8,128)(2,1)S(1)}, bf16[256,2048]{1,0:T(8,128)(2,1)}, u32[]{:S(2)}, u32[]{:S(2)}) collective-permute-start(bf16[256,2048]{1,0:T(8,128)(2,1)S(1)} %bitcast.93), channel_id=1, source_target_pairs={{0,2},{1,3},{2,6},{3,7},{4,0},{5,1},{6,4},{7,5},{8,10},{9,11},{10,... | collective-permute-start | bytes 3145736 | tf_op jit(solution)/shard_map/cotangent_ring/ppermute | solution.py:559
  157.0 46.9 %collective-permute-start.12 = (bf16[512,1024]{1,0:T(8,128)(2,1)}, bf16[512,1024]{1,0:T(8,128)(2,1)}, u32[]{:S(2)}, u32[]{:S(2)}) collective-permute-start(bf16[512,1024]{1,0:T(8,128)(2,1)} %constant_dynamic-update-slice_fusion.refs_0_), channel_id=1, source_target_pairs={{0,8},{8,0},{16,24},{24,16},{1,9},{9,1},{17,25},{25,17},{2,10},{10... | collective-permute-start | bytes 3145736 | tf_op jit(solution)/shard_map/out_weight/ppermute | solution.py:565
  157.5 47.5 %collective-permute-start.13 = (bf16[512,1024]{1,0:T(8,128)(2,1)}, bf16[512,1024]{1,0:T(8,128)(2,1)}, u32[]{:S(2)}, u32[]{:S(2)}) collective-permute-start(bf16[512,1024]{1,0:T(8,128)(2,1)} %constant_dynamic-update-slice_fusion.refs_0_), channel_id=1, source_target_pairs={{0,16},{8,24},{16,0},{24,8},{1,17},{9,25},{17,1},{25,9},{2,18},{10... | collective-permute-start | bytes 3145736 | tf_op jit(solution)/shard_map/out_weight/ppermute | solution.py:565
  188.8 442.6 %reduce-scatter.5.cloned.1.call-start = ((), (), s32[]{:S(2)}) async-start(), calls=%async_computation.12 | async-start | bytes 5242880 | tf_op jit(solution)/shard_map/out_grad/reduce_scatter | solution.py:590
  226.8 48.8 %collective-permute-start.31 = (bf16[256,2048]{1,0:T(8,128)(2,1)}, bf16[256,2048]{1,0:T(8,128)(2,1)}, u32[]{:S(2)}, u32[]{:S(2)}) collective-permute-start(bf16[256,2048]{1,0:T(8,128)(2,1)} %collective-permute-done.23.refs_2_), channel_id=1, source_target_pairs={{0,2},{1,3},{2,6},{3,7},{4,0},{5,1},{6,4},{7,5},{8,10},{9,11},{10,... | collective-permute-start | bytes 3145736 | tf_op jit(solution)/shard_map/cotangent_ring/ppermute | solution.py:559
  227.8 47.7 %collective-permute-start.28 = (bf16[256,2048]{1,0:T(8,128)(2,1)S(1)}, bf16[256,2048]{1,0:T(8,128)(2,1)}, u32[]{:S(2)}, u32[]{:S(2)}) collective-permute-start(bf16[256,2048]{1,0:T(8,128)(2,1)S(1)} %bitcast.94), channel_id=1, source_target_pairs={{0,1},{1,0},{2,3},{3,2},{4,5},{5,4},{6,7},{7,6},{8,9},{9,8},{10,11... | collective-permute-start | bytes 3145736 | tf_op jit(solution)/shard_map/cotangent_ring/ppermute | solution.py:562
  227.8 47.8 %collective-permute-start.27 = (bf16[256,2048]{1,0:T(8,128)(2,1)}, bf16[256,2048]{1,0:T(8,128)(2,1)}, u32[]{:S(2)}, u32[]{:S(2)}) collective-permute-start(bf16[256,2048]{1,0:T(8,128)(2,1)} %get-tuple-element.127.refs_0_), channel_id=1, source_target_pairs={{0,1},{1,0},{2,3},{3,2},{4,5},{5,4},{6,7},{7,6},{8,9},{9,8},{10,11... | collective-permute-start | bytes 3145736 | tf_op jit(solution)/shard_map/normed_ring/ppermute | solution.py:562
  228.3 72.9 %collective-permute-start.26 = (bf16[256,2048]{1,0:T(8,128)(2,1)}, bf16[256,2048]{1,0:T(8,128)(2,1)}, u32[]{:S(2)}, u32[]{:S(2)}) collective-permute-start(bf16[256,2048]{1,0:T(8,128)(2,1)} %collective-permute-done.23.refs_2_), channel_id=1, source_target_pairs={{0,1},{1,0},{2,3},{3,2},{4,5},{5,4},{6,7},{7,6},{8,9},{9,8},{10,11... | collective-permute-start | bytes 3145736 | tf_op jit(solution)/shard_map/cotangent_ring/ppermute | solution.py:562
  327.7 48.5 %collective-permute-start.30 = (bf16[256,2048]{1,0:T(8,128)(2,1)S(1)}, bf16[256,2048]{1,0:T(8,128)(2,1)S(1)}, u32[]{:S(2)}, u32[]{:S(2)}) collective-permute-start(bf16[256,2048]{1,0:T(8,128)(2,1)S(1)} %add_convert_fusion.8), channel_id=1, source_target_pairs={{0,2},{1,3},{2,6},{3,7},{4,0},{5,1},{6,4},{7,5},{8,10},{9,11},{10,... | collective-permute-start | bytes 3145736 | tf_op jit(solution)/shard_map/back_ring/ppermute | solution.py:559
  327.8 48.4 %collective-permute-start.38 = (bf16[256,2048]{1,0:T(8,128)(2,1)S(1)}, bf16[256,2048]{1,0:T(8,128)(2,1)S(1)}, u32[]{:S(2)}, u32[]{:S(2)}) collective-permute-start(bf16[256,2048]{1,0:T(8,128)(2,1)S(1)} %collective-permute-done.33.refs_0_), channel_id=1, source_target_pairs={{0,2},{1,3},{2,6},{3,7},{4,0},{5,1},{6,4},{7,5},{8,10},{9,11},{10,... | collective-permute-start | bytes 3145736 | tf_op jit(solution)/shard_map/normed_ring/ppermute | solution.py:559
  460.6 229.8 %reduce-scatter.9.cloned.1.call-start = ((), (), s32[]{:S(2)}) async-start(), calls=%async_computation.14 | async-start | bytes 5242880 | tf_op jit(solution)/shard_map/up_grad/reduce_scatter | solution.py:590
  461.1 229.2 %reduce-scatter.7.cloned.1.call-start = ((), (), s32[]{:S(2)}) async-start(), calls=%async_computation.13 | async-start | bytes 5242880 | tf_op jit(solution)/shard_map/gate_grad/reduce_scatter | solution.py:590
  467.7 73.7 %collective-permute-start.47 = (bf16[256,2048]{1,0:T(8,128)(2,1)}, bf16[256,2048]{1,0:T(8,128)(2,1)}, u32[]{:S(2)}, u32[]{:S(2)}) collective-permute-start(bf16[256,2048]{1,0:T(8,128)(2,1)} %get-tuple-element.173), channel_id=1, source_target_pairs={{0,1},{1,0},{2,3},{3,2},{4,5},{5,4},{6,7},{7,6},{8,9},{9,8},{10,11... | collective-permute-start | bytes 3145736 | tf_op jit(solution)/shard_map/feed_forward_pair/ppermute | solution.py:562
  468.1 128.0 %collective-permute-start.49 = (bf16[256,2048]{1,0:T(8,128)(2,1)}, bf16[256,2048]{1,0:T(8,128)(2,1)}, u32[]{:S(2)}, u32[]{:S(2)}) collective-permute-start(bf16[256,2048]{1,0:T(8,128)(2,1)} %get-tuple-element.179), channel_id=1, source_target_pairs={{0,1},{1,0},{2,3},{3,2},{4,5},{5,4},{6,7},{7,6},{8,9},{9,8},{10,11... | collective-permute-start | bytes 3145736 | tf_op jit(solution)/shard_map/feed_forward_pair/ppermute | solution.py:562
  472.5 221.6 %reduce-scatter.11.cloned.1.call-start = ((), (), s32[]{:S(2)}) async-start(), calls=%async_computation.15 | async-start | bytes 5242880 | tf_op jit(solution)/shard_map/down_grad/reduce_scatter | solution.py:590
  475.3 65.9 %collective-permute-start.44 = (bf16[256,2048]{1,0:T(8,128)(2,1)}, bf16[256,2048]{1,0:T(8,128)(2,1)}, u32[]{:S(2)}, u32[]{:S(2)}) collective-permute-start(bf16[256,2048]{1,0:T(8,128)(2,1)} %add_convert_fusion.5), channel_id=1, source_target_pairs={{0,2},{1,3},{2,6},{3,7},{4,0},{5,1},{6,4},{7,5},{8,10},{9,11},{10,... | collective-permute-start | bytes 3145736 | tf_op jit(solution)/shard_map/down_ring/ppermute | solution.py:559
  537.4 34.9 %collective-permute-start.54 = (bf16[256,2048]{1,0:T(8,128)(2,1)S(1)}, bf16[256,2048]{1,0:T(8,128)(2,1)S(1)}, u32[]{:S(2)}, u32[]{:S(2)}) collective-permute-start(bf16[256,2048]{1,0:T(8,128)(2,1)S(1)} %convolution_convert_fusion.10), channel_id=1, source_target_pairs={{0,1},{1,0},{2,3},{3,2},{4,5},{5,4},{6,7},{7,6},{8,9},{9,8},{10,11... | collective-permute-start | bytes 3145736 | tf_op jit(solution)/shard_map/first_ring/ppermute | solution.py:562
  541.2 87.1 %collective-permute-start.56 = (bf16[256,2048]{1,0:T(8,128)(2,1)}, bf16[256,2048]{1,0:T(8,128)(2,1)}, u32[]{:S(2)}, u32[]{:S(2)}) collective-permute-start(bf16[256,2048]{1,0:T(8,128)(2,1)} %convolution_convert_fusion.8), channel_id=1, source_target_pairs={{0,1},{1,0},{2,3},{3,2},{4,5},{5,4},{6,7},{7,6},{8,9},{9,8},{10,11... | collective-permute-start | bytes 3145736 | tf_op jit(solution)/shard_map/first_ring/ppermute | solution.py:562
  551.2 41.2 %collective-permute-start.53 = (bf16[256,2048]{1,0:T(8,128)(2,1)S(1)}, bf16[256,2048]{1,0:T(8,128)(2,1)S(1)}, u32[]{:S(2)}, u32[]{:S(2)}) collective-permute-start(bf16[256,2048]{1,0:T(8,128)(2,1)S(1)} %fusion.6), channel_id=1, source_target_pairs={{0,2},{1,3},{2,6},{3,7},{4,0},{5,1},{6,4},{7,5},{8,10},{9,11},{10,... | collective-permute-start | bytes 3145736 | tf_op jit(solution)/shard_map/first_ring/ppermute | solution.py:559
  598.8 61.2 %collective-permute-start.51 = (bf16[256,2048]{1,0:T(8,128)(2,1)}, bf16[256,2048]{1,0:T(8,128)(2,1)}, u32[]{:S(2)}, u32[]{:S(2)}) collective-permute-start(bf16[256,2048]{1,0:T(8,128)(2,1)} %get-tuple-element.181), channel_id=1, source_target_pairs={{0,1},{1,0},{2,3},{3,2},{4,5},{5,4},{6,7},{7,6},{8,9},{9,8},{10,11... | collective-permute-start | bytes 3145736 | tf_op jit(solution)/shard_map/feed_forward_pair/ppermute | solution.py:562
  598.9 101.3 %collective-permute-start.58 = (bf16[256,2048]{1,0:T(8,128)(2,1)}, bf16[256,2048]{1,0:T(8,128)(2,1)S(1)}, u32[]{:S(2)}, u32[]{:S(2)}) collective-permute-start(bf16[256,2048]{1,0:T(8,128)(2,1)} %convolution_convert_fusion.6), channel_id=1, source_target_pairs={{0,1},{1,0},{2,3},{3,2},{4,5},{5,4},{6,7},{7,6},{8,9},{9,8},{10,11... | collective-permute-start | bytes 3145736 | tf_op jit(solution)/shard_map/first_ring/ppermute | solution.py:562
  618.5 41.6 %collective-permute-start.50 = (bf16[256,2048]{1,0:T(8,128)(2,1)}, bf16[256,2048]{1,0:T(8,128)(2,1)}, u32[]{:S(2)}, u32[]{:S(2)}) collective-permute-start(bf16[256,2048]{1,0:T(8,128)(2,1)} %add_convert_fusion.3), channel_id=1, source_target_pairs={{0,2},{1,3},{2,6},{3,7},{4,0},{5,1},{6,4},{7,5},{8,10},{9,11},{10,... | collective-permute-start | bytes 3145736 | tf_op jit(solution)/shard_map/down_ring/ppermute | solution.py:559
  619.8 35.6 %all-to-all-start.3 = ((bf16[8,64,512]{2,1,0:T(8,128)(2,1)}), bf16[8,64,512]{2,1,0:T(8,128)(2,1)}, u32[]{:S(2)}, u32[]{:S(2)}) async-start(bf16[8,64,512]{2,1,0:T(8,128)(2,1)} %bitcast.40), calls=%async_computation.3 | async-start | bytes 1048576 | tf_op jit(solution)/shard_map/projection_grads/all_to_all | solution.py:785
  663.9 43.9 %collective-permute-start.57 = (bf16[256,2048]{1,0:T(8,128)(2,1)}, bf16[256,2048]{1,0:T(8,128)(2,1)S(1)}, u32[]{:S(2)}, u32[]{:S(2)}) collective-permute-start(bf16[256,2048]{1,0:T(8,128)(2,1)} %add_convert_fusion), channel_id=1, source_target_pairs={{0,2},{1,3},{2,6},{3,7},{4,0},{5,1},{6,4},{7,5},{8,10},{9,11},{10,... | collective-permute-start | bytes 3145736 | tf_op jit(solution)/shard_map/first_ring/ppermute | solution.py:559
  (82 other events, 1112.8 us)
Sparse Core Ops, SparseCore 0:
  9.9 62.7 all-gather.3
  74.5 54.7 all-gather.5
  131.1 74.0 all-gather.7
  460.7 52.1 reduce-scatter.4
  515.7 52.5 reduce-scatter.8
  571.1 67.3 reduce-scatter.6
  641.5 52.5 reduce-scatter.10
